TPU v7x, 32 devices: a whole 2x2x4 slice. The times are simulated.
32 devices in a mesh: section: 4 (over z), rows: 8 (over y, x, core).
Axes of the slice: x: 2, y: 2, z: 4, core: 2. Of those that a mesh axis runs over, the one named last changes fastest.
Arguments:
- rows_data: float32 [16, 8192, 128], P('section', 'rows'), may hold values from -6 to 6
- row_keys: int32 [16, 8192], P('section', 'rows'), may hold values from 0 to 8191
- valid_counts: int32 [16, 8], P('section', 'rows'), may hold values from 256 to 1024
- predicates: int32 [4, 16, 256], P('section', None, 'rows'), may hold values from -2147483648 to 2147483647, as said below
- section_weight: float32 [4, 128, 128], P('section'), may hold values from -0.5 to 0.5
- section_bias: float32 [4, 128], P('section'), may hold values from -3 to 3
Outputs:
- key_means: float32 [8192, 128], P(('section', 'rows'))
- key_counts: float32 [8192], P(('section', 'rows'))
Inputs may be any that keep to these rules, and one draw needn't show every extreme that they name: Bit j of predicates[s, m, w] is the flag of row 32 w + j of micro-batch m for section s; about three flags in four are 1. `row_keys`: keys are drawn from a skewed distribution: a few keys are very frequent and most are rare.
All inputs are finite; a program needn't handle non-finite values.
Results may differ from a plain program's by a relative error of at most 0.0001.
Values sent between devices are 32-bit elements; how exact they have to be, the bound alone decides.
No kernel may reach another device: no remote copies, remote signals or barrier semaphores. Data moves between devices by JAX's collectives and lax.ppermute only.
A program may use at most 64 MiB of HBM per device.

v0:
```python
import jax
import jax.numpy as jnp
from jax import lax
from jax.sharding import PartitionSpec as P

KEYS = 8192
SECTIONS = 4


def advance(hidden, weight, bias):
    return hidden + jnp.tanh(
        jnp.dot(hidden, weight, precision=lax.Precision.HIGHEST, preferred_element_type=jnp.float32)
        + bias
    )


def unpack_flags(words):
    shifts = lax.broadcasted_iota(jnp.int32, (32,), 0)
    flags = jnp.right_shift(words[..., None], shifts) & 1
    return flags.reshape(words.shape[:-1] + (words.shape[-1] * 32,))


def tally_rows(row_sums, row_counts, keys):
    sums = jax.ops.segment_sum(row_sums, keys, num_segments=KEYS)
    counts = jax.ops.segment_sum(row_counts, keys, num_segments=KEYS)
    return (sums, counts)


def shards(rows_data, row_keys, valid_counts, predicates, section_weight, section_bias):
    held_batches = rows_data.shape[0]
    block = rows_data.shape[1]
    width = rows_data.shape[2]
    section = lax.axis_index("section")
    position = lax.broadcasted_iota(jnp.int32, (block,), 0)
    every_words = lax.all_gather(predicates, "section", axis=0, tiled=True)
    weights, biases = (
        lax.all_gather(section_weight, "section", axis=0, tiled=True),
        lax.all_gather(section_bias, "section", axis=0, tiled=True),
    )
    first = section * held_batches
    hidden = rows_data.reshape(held_batches * block, width)
    alive = (position[None, :] < valid_counts).reshape(-1)
    held_words = lax.dynamic_slice_in_dim(every_words, first, held_batches, 1)
    marks = unpack_flags(held_words)
    row_sums = jnp.zeros((held_batches * block, width), jnp.float32)
    row_counts = jnp.zeros((held_batches * block,), jnp.float32)
    for level in range(SECTIONS):
        alive = alive & (marks[level].reshape(-1) == 1)
        hidden = advance(hidden, weights[level], biases[level])
        row_sums = row_sums + jnp.where(alive[:, None], hidden, 0.0)
        row_counts = row_counts + alive.astype(jnp.float32)
    sums, counts = tally_rows(row_sums, row_counts, row_keys.reshape(-1))
    owned_sums, owned_counts = (
        lax.psum_scatter(sums, ("section", "rows"), scatter_dimension=0, tiled=True),
        lax.psum_scatter(counts, ("section", "rows"), scatter_dimension=0, tiled=True),
    )
    key_means = owned_sums / jnp.maximum(owned_counts, 1.0)[:, None]
    return (key_means, owned_counts)


def solution(mesh):
    return jax.shard_map(
        shards,
        mesh=mesh,
        in_specs=(
            P("section", "rows", None),
            P("section", "rows"),
            P("section", "rows"),
            P("section", None, "rows"),
            P("section", None, None),
            P("section", None),
        ),
        out_specs=(P(("section", "rows"), None), P(("section", "rows"))),
        check_vma=False,
    )
```

profile of v0, /device:TPU:0, one launch (start us, length us, event | category | flops | bytes accessed | tf_op | source)
XLA Modules:
  0.0 235.0 jit_solution(805266901076463028)
XLA Ops:
  7.2 0.0 reduce-scatter.2.cloned.1.call-start
  7.2 15.1 %all_gather.9 = s32[4,16,32]{2,1,0:T(8,128)S(1)} all-gather(s32[1,16,32]{2,1,0:T(8,128)} %param.9), channel_id=1, replica_groups=mesh['section'=4,'rows'=8] {'section'}, dimensions={0}, use_global_device_ids=true | all-gather | bytes 10240 | tf_op jit(solution)/shard_map/all_gather | solution.py:35
  22.3 0.1 shift-right-arithmetic_and_fusion
  22.5 0.1 eq.59
  22.6 0.1 eq.61
  22.7 0.1 eq.63
  22.8 0.1 eq.65
  22.9 0.7 fusion.14
  23.6 14.5 %all_gather.10 = f32[4,128,128]{2,1,0:T(8,128)S(1)} all-gather(f32[1,128,128]{2,1,0:T(8,128)} %param.10), channel_id=1, replica_groups=mesh['section'=4,'rows'=8] {'section'}, dimensions={0}, use_global_device_ids=true | all-gather | bytes 327680 | tf_op jit(solution)/shard_map/all_gather | solution.py:37
  38.1 10.6 %all-gather = f32[4,1,128]{2,1,0:T(1,128)S(1)} all-gather(f32[1,1,128]{2,1,0:T(1,128)} %bitcast.49), channel_id=1, replica_groups=mesh['section'=4,'rows'=8] {'section'}, dimensions={0}, use_global_device_ids=true | all-gather | bytes 2560 | tf_op jit(solution)/shard_map/all_gather | solution.py:38
  48.8 0.7 copy.13
  49.5 4.1 %fusion.9 = f32[4096,128]{1,0:T(8,128)S(1)} fusion(f32[4096,128]{1,0:T(8,128)} %bitcast.44, f32[128]{0:T(128)S(1)} %get-tuple-element.16, f32[4,128,128]{2,1,0:T(8,128)S(1)} %all_gather.10), kind=kOutput, calls=%fused_computation.15 | convolution fusion | flops 806354944 | bytes 6357504 | tf_op jit(solution)/shard_map/dot_general | solution.py:12
  53.6 1.9 fusion.7
  55.5 1.9 fusion.5
  57.4 3.2 %fusion.3 = f32[4096,128]{1,0:T(8,128)S(1)} fusion(f32[4096,128]{1,0:T(8,128)S(1)} %fusion.5, f32[4096,128]{1,0:T(8,128)S(1)} %fusion.7, f32[4096,128]{1,0:T(8,128)S(1)} %fusion.9, f32[128]{0:T(128)S(1)} %get-tuple-element.13, pred[4096]{0:T(1024)(128)(4,1)S(1)} %get-tuple-element.5, pred[4096]{0:T(1024)(128)(4,1)S(1)} %get-tuple-element.6, ...), kind=kOutput, calls=%fused_computation.6 | convolution fusion | flops 810024960 | bytes 10568192 | tf_op jit(solution)/shard_map/dot_general | solution.py:12
  60.6 24.5 %scatter_custom_fusion = f32[8192,128]{1,0:T(8,128)} fusion(s32[4096]{0:T(1024)S(1)} %bitcast.46, f32[4096,128]{1,0:T(8,128)S(1)} %fusion.3, f32[]{:T(128)} %constant.7.clone.1), kind=kCustom, calls=%fused_computation.16 | custom fusion | flops 524288 | bytes 4194308 | tf_op jit(solution)/shard_map/scatter-add | solution.py:24
  85.1 0.0 reduce-scatter.2.cloned.1.call-update
  85.1 21.9 %scatter_custom_fusion.1 = f32[8192]{0:T(1024)S(1)} fusion(s32[4096]{0:T(1024)S(1)} %bitcast.47, f32[4096]{0:T(1024)S(1)} %get-tuple-element.4, f32[]{:T(128)} %constant.7.clone.1), kind=kCustom, calls=%fused_computation.30 | custom fusion | flops 4096 | bytes 32772 | tf_op jit(solution)/shard_map/scatter-add | solution.py:25
  107.0 38.4 %all-reduce = f32[8192]{0:T(1024)S(1)} all-reduce(f32[8192]{0:T(1024)S(1)} %scatter_custom_fusion.1), channel_id=3, replica_groups=mesh['section'=4,'rows'=8] {'section','rows'}, use_global_device_ids=true, to_apply=%region_3.4.clone | all-reduce | flops 8192 | bytes 65536
  145.4 0.6 broadcast_maximum_fusion
  146.1 80.4 %reduce-scatter.2.cloned.1.call-done = f32[256,128]{1,0:T(8,128)} async-done(((f32[8192,128]{1,0:T(8,128)}), f32[256,128]{1,0:T(8,128)}) %reduce-scatter.2.cloned.1.call-update) | async-done | bytes 131088 | tf_op jit(solution)/shard_map/reduce_scatter | solution.py:54
  226.5 1.7 broadcast_divide_fusion
  (4 shorter events, 0.1 us)
Async XLA Ops:
  7.2 219.4 %reduce-scatter.2.cloned.1.call-start = ((), (), s32[]{:S(2)}) async-start(), calls=%async_computation.1 | async-start | bytes 4325376 | tf_op jit(solution)/shard_map/reduce_scatter | solution.py:54
Sparse Core Ops, SparseCore 0:
  85.2 141.2 reduce-scatter.1
where the time goes:
time: 235 us
  waiting for transfers between devices  80.4 us (34%)
  blocking collectives  78.6 us (33%)
  other arithmetic  49.6 us (21%)
  between operations  14.1 us (6%)
  matrix products  11.1 us (5%)
    reduce_scatter x1, waiting for transfers between devices, shards(): lax.psum_scatter(sums, ('section', 'rows'), scatter_dimension=0, tiled=True)  80.4 us
    unnamed x1, blocking collectives  38.4 us
    scatter-add x1, other arithmetic, tally_rows(): sums = jax.ops.segment_sum(row_sums, keys, num_segments=KEYS)  24.5 us
    scatter-add x1, other arithmetic, tally_rows(): counts = jax.ops.segment_sum(row_counts, keys, num_segments=KEYS)  21.9 us
    all_gather x1, blocking collectives, shards(): every_words = lax.all_gather(predicates, 'section', axis=0, tiled=True)  15.1 us
    all_gather x1, blocking collectives, shards(): lax.all_gather(section_weight, 'section', axis=0, tiled=True)  14.5 us
    dot_general x4, matrix products, advance(): jnp.dot(hidden, weight, precision=lax.Precision.HIGHEST, preferred_elemen...  11.1 us
    all_gather x1, blocking collectives, shards(): lax.all_gather(section_bias, 'section', axis=0, tiled=True)  10.6 us
  transfers between devices with their start and end apart: 1, of which 1 were waited for; matrix products, arithmetic and copies ran while one was open for 10% of the time, Pallas kernels for 0%

commit v1 on v0

v1 whole, which is shorter than its diff:
```python
import functools
import jax
import jax.numpy as jnp
from jax import lax
from jax.experimental import pallas as pl
from jax.experimental.pallas import tpu as pltpu
from jax.sharding import PartitionSpec as P

KEYS = 8192
SECTIONS = 4
LANES = 128
BF16 = jnp.bfloat16
F32 = jnp.float32
VMEM = pl.BlockSpec(memory_space=pltpu.VMEM)
SMEM = pl.BlockSpec(memory_space=pltpu.SMEM)


def split(value):
    high = value.astype(BF16)
    return high, (value - high.astype(F32)).astype(BF16)


def iota(shape, axis):
    return lax.broadcasted_iota(jnp.int32, shape, axis)


class Plan:
    def __init__(self, mesh):
        self.sections = mesh.shape["section"]
        self.rows = mesh.shape["rows"]
        self.planes = self.rows.bit_length() - 2
        self.owned = KEYS // (self.sections * self.rows)
        self.color = self.owned // 2
        self.half = KEYS // 2
        self.send = self.half // 4
        bits = list(range(self.planes))
        turn = self.planes // 2
        self.orders = (bits, bits[turn:] + bits[:turn])

    def perm(self, row_xor, section_xor):
        return [
            (s * self.rows + r, (s ^ section_xor) * self.rows + (r ^ row_xor))
            for s in range(self.sections)
            for r in range(self.rows)
        ]


def slot_codes(plan, keys, z, p):
    log_color = plan.color.bit_length() - 1
    low = keys & (plan.color - 1)
    rest = keys >> log_color
    color = rest & 1
    core = (rest >> 1) & 1
    place = ((rest >> 2) & ((1 << plan.planes) - 1)) ^ p
    zrel = (rest >> (2 + plan.planes)) ^ z
    inner = []
    for order in plan.orders:
        index = 0
        for bit in order:
            index = index * 2 + (1 - ((place >> bit) & 1))
        inner.append(index)
    index = jnp.where(color == 0, inner[0], inner[1])
    count = 1 << (plan.planes - 1)
    kept = index >> (plan.planes - 1)
    index = index & (count - 1)
    slot = ((kept * 2 + color) * count + index) * plan.sections + zrel
    return slot * plan.color + low + core * plan.half


def advance_kernel(plan, x_ref, keys_ref, valid_ref, b0, b1, b2, b3, out_ref, count_ref, weight, bias, bytes_):
    batches, block, width = x_ref.shape
    z = lax.axis_index("section")
    row = lax.axis_index("rows")
    core = row & 1
    place = row >> 1
    bytes_[...] = jnp.zeros_like(bytes_)
    for k, buffer in enumerate((b0, b1, b2, b3)):
        level = z ^ k
        high, low = split(buffer[:width, :])
        weight[level, :width, :width] = high
        weight[level, width:, :width] = high
        weight[level, :width, width:] = low
        weight[level, width:, width:] = jnp.zeros_like(low)
        bytes_[level, :4, :] = buffer[width : width + 4, :]
        bias[level, :1, :] = buffer[width + 4 : width + 5, :]
    words = bytes_[...].reshape(SECTIONS * 8, LANES).astype(BF16)
    lane = iota((1, block), 1)
    table = jnp.zeros((2 * plan.half // LANES, LANES), F32)
    per_batch = block // LANES
    for m in range(batches):
        spread = (iota((LANES, block), 0) == (iota((LANES, block), 1) >> 5) + m * 32).astype(F32).astype(BF16)
        found = jnp.dot(words, spread, preferred_element_type=F32).astype(jnp.int32)
        which = (lane >> 3) & 3
        flags = []
        for s in range(SECTIONS):
            byte = found[8 * s : 8 * s + 1]
            for b in range(1, 4):
                byte = jnp.where(which == b, found[8 * s + b : 8 * s + b + 1], byte)
            flags.append((byte >> (lane & 7)) & 1)
        depth = flags[-1]
        for flag in flags[-2::-1]:
            depth = flag * (1 + depth)
        depth = jnp.where(lane < valid_ref[m, 0], depth, 0)
        code = slot_codes(plan, keys_ref[m : m + 1, :], z, place)
        code_f = code.astype(F32)
        for i in range(per_batch):
            at = batches * block + m * per_batch + i
            out_ref[at : at + 1, :] = code_f[:, i * LANES : (i + 1) * LANES]
        depth_f = depth.astype(F32)
        outer = (iota((2 * plan.half // LANES, block), 0) == (code >> 7)).astype(F32).astype(BF16)
        inner = jnp.where(iota((LANES, block), 0) == (code & (LANES - 1)), depth_f, 0.0).astype(BF16)
        table = table + lax.dot_general(outer, inner, (((1,), (1,)), ((), ())), preferred_element_type=F32)
        column = jnp.transpose(jnp.broadcast_to(depth_f, (8, block)))[:, :1]
        depth_b = jnp.broadcast_to(column, (block, width))
        hidden = x_ref[m]
        total = jnp.zeros((block, width), F32)
        for s in range(SECTIONS):
            both = jnp.concatenate(split(hidden), axis=1)
            product = jnp.dot(both, weight[s], preferred_element_type=F32)
            hidden = hidden + jnp.tanh(product[:, :width] + product[:, width:] + bias[s, :1, :])
            total = total + jnp.where(depth_b > s, hidden, 0.0)
        out_ref[m * block : (m + 1) * block, :] = total
    lines = plan.half // LANES
    first = core == 0
    at = batches * block + batches * per_batch
    count_ref[...] = jnp.where(first, table[:lines], table[lines:])
    out_ref[at : at + lines, :] = jnp.where(first, table[lines:], table[:lines])


def add_products(plan, source, first, slots, tile, piece, sums, core):
    values, codes = source
    rows = values.shape[0]
    base = (core * plan.half + first).astype(F32)
    for t in range(slots // tile):
        total = sums(t)
        for k in range(rows // piece):
            marks = []
            for i in range(piece // LANES):
                code = codes[k * piece // LANES + i : k * piece // LANES + i + 1, :] - base - float(t * tile)
                marks.append(jnp.where(code == iota((tile, LANES), 0).astype(F32), 1.0, 0.0).astype(BF16))
            mark = jnp.concatenate(marks, axis=1)
            total = total + jnp.dot(mark, values[k * piece : (k + 1) * piece, :], preferred_element_type=F32)
        yield t, total


def spread_rows(rows_ref, rows, scratch):
    high, low = split(rows_ref[:rows, :])
    width = high.shape[1]
    scratch[:, :width] = high
    scratch[:, width:] = low


def first_kernel(plan, rows, tile, piece, own_ref, out_ref, scratch):
    core = lax.axis_index("rows") & 1
    spread_rows(own_ref, rows, scratch)
    codes = own_ref.at[rows : rows + rows // LANES]
    width = out_ref.shape[1]
    for t, total in add_products(plan, (scratch, codes), 0, 2 * plan.send, tile, piece, lambda t: 0.0, core):
        out_ref[t * tile : (t + 1) * tile, :] = total[:, :width] + total[:, width:]


def second_kernel(plan, rows, tile, piece, other_ref, part_ref, count_ref, a_ref, b_ref, kept_ref, scratch):
    core = lax.axis_index("rows") & 1
    spread_rows(other_ref, rows, scratch)
    lines = rows // LANES
    codes = other_ref.at[rows : rows + lines]
    width = a_ref.shape[1]
    per = plan.send // tile
    for t, total in add_products(plan, (scratch, codes), 0, 2 * plan.send, tile, piece, lambda t: 0.0, core):
        target = (a_ref, b_ref)[t // per]
        at = (t % per) * tile
        target[at : at + tile, :] = total[:, :width] + total[:, width:] + part_ref[t * tile : (t + 1) * tile, :]
    counts = count_ref[...] + other_ref[rows + lines : rows + lines + plan.half // LANES, :]
    share = plan.send // LANES
    a_ref[plan.send :, :] = counts[:share]
    b_ref[plan.send :, :] = counts[share : 2 * share]
    kept_ref[...] = counts[2 * share :]


def third_kernel(plan, rows, tile, piece, own_ref, other_ref, count_ref, a_ref, b_ref, own_s, other_s):
    core = lax.axis_index("rows") & 1
    spread_rows(own_ref, rows, own_s)
    spread_rows(other_ref, rows, other_s)
    lines = rows // LANES
    width = a_ref.shape[1]
    per = plan.send // tile
    first = 2 * plan.send
    own = add_products(plan, (own_s, own_ref.at[rows : rows + lines]), first, first, tile, piece, lambda t: 0.0, core)
    held = {}

    def begin(t):
        held[t] = next(own)[1]
        return held[t]

    other = add_products(plan, (other_s, other_ref.at[rows : rows + lines]), first, first, tile, piece, begin, core)
    for t, total in other:
        target = (a_ref, b_ref)[t // per]
        at = (t % per) * tile
        target[at : at + tile, :] = total[:, :width] + total[:, width:]
    share = plan.send // LANES
    a_ref[plan.send :, :] = count_ref[:share]
    b_ref[plan.send :, :] = count_ref[share:]


def call(kernel, out_shape, operands, scratch=(), name=None, smem=()):
    return pl.pallas_call(
        kernel,
        out_shape=out_shape,
        in_specs=[SMEM if i in smem else VMEM for i in range(len(operands))],
        out_specs=jax.tree.map(lambda _: VMEM, out_shape),
        scratch_shapes=list(scratch),
        name=name,
    )(*operands)


def shape(*dims):
    return jax.ShapeDtypeStruct(dims, F32)


def shards(plan, rows_data, row_keys, valid_counts, predicates, section_weight, section_bias):
    batches, block, width = rows_data.shape
    axes = ("section", "rows")
    z = lax.axis_index("section")
    words = predicates.reshape(plan.sections, batches * predicates.shape[2])
    pieces = jnp.stack([(words >> (8 * b)) & 255 for b in range(4)], axis=1).astype(F32)
    buffers = []
    for k in range(plan.sections):
        part = lax.dynamic_index_in_dim(pieces, z ^ k, 0, keepdims=False)
        packed = jnp.concatenate([section_weight[0], part, section_bias, jnp.zeros((3, width), F32)], axis=0)
        if k:
            packed = lax.ppermute(packed, axes, plan.perm(0, k))
        buffers.append(packed)
    rows = batches * block
    lines = rows // LANES
    tables = plan.half // LANES
    own, count = call(
        functools.partial(advance_kernel, plan),
        (shape(rows + lines + tables, width), shape(tables, LANES)),
        (rows_data, row_keys, valid_counts, *buffers),
        scratch=[
            pltpu.VMEM((SECTIONS, 2 * width, 2 * width), BF16),
            pltpu.VMEM((SECTIONS, 8, width), F32),
            pltpu.VMEM((SECTIONS, 8, LANES), F32),
        ],
        name="advance",
        smem=(2,),
    )
    other = lax.ppermute(own, axes, plan.perm(1, 0))
    tile, piece = min(256, plan.send), min(1024, rows)
    wide = pltpu.VMEM((rows, 2 * width), BF16)
    part = call(
        functools.partial(first_kernel, plan, rows, tile, piece),
        shape(2 * plan.send, width),
        (own,),
        scratch=[wide],
        name="table_own",
    )
    share = plan.send // LANES
    message = shape(plan.send + share, width)
    send_a, send_b, kept_count = call(
        functools.partial(second_kernel, plan, rows, tile, piece),
        (message, message, shape(2 * share, LANES)),
        (other, part, count),
        scratch=[wide],
        name="table_send",
    )
    got = [lax.ppermute(m, axes, plan.perm(2 << order[0], 0)) for m, order in zip((send_a, send_b), plan.orders)]
    kept = call(
        functools.partial(third_kernel, plan, rows, tile, piece),
        (message, message),
        (own, other, kept_count),
        scratch=[wide, wide],
        name="table_keep",
    )
    states = []
    for color in range(2):
        total = kept[color] + got[color]
        states.append((total[: plan.send], total[plan.send :].reshape(-1)))
    for step in range(1, plan.planes):
        after = []
        for color in range(2):
            sums, counts = states[color]
            cut = sums.shape[0] // 2
            packed = jnp.concatenate([sums[:cut], counts[:cut].reshape(-1, LANES)], axis=0)
            moved = lax.ppermute(packed, axes, plan.perm(2 << plan.orders[color][step], 0))
            after.append((sums[cut:] + moved[:cut], counts[cut:] + moved[cut:].reshape(-1)))
        states = after
    sums = jnp.stack([s.reshape(plan.sections, plan.color, width) for s, _ in states], axis=1)
    counts = jnp.stack([c.reshape(plan.sections, plan.color) for _, c in states], axis=1)
    sums = sums.reshape(plan.sections, plan.owned, width)
    counts = counts.reshape(plan.sections, plan.owned)
    total, number = sums[0], counts[0]
    if plan.owned % LANES == 0:
        tail = counts.reshape(plan.sections, plan.owned // LANES, LANES)
    else:
        tail = jnp.pad(counts, ((0, 0), (0, LANES - plan.owned)))[:, None, :]
    for k in range(1, plan.sections):
        packed = jnp.concatenate([sums[k], tail[k]], axis=0)
        moved = lax.ppermute(packed, axes, plan.perm(0, k))
        total = total + moved[: plan.owned]
        number = number + moved[plan.owned :].reshape(-1)[: plan.owned]
    return total / jnp.maximum(number, 1.0)[:, None], number


def solution(mesh):
    return jax.shard_map(
        functools.partial(shards, Plan(mesh)),
        mesh=mesh,
        in_specs=(
            P("section", "rows", None),
            P("section", "rows"),
            P("section", "rows"),
            P("section", None, "rows"),
            P("section", None, None),
            P("section", None),
        ),
        out_specs=(P(("section", "rows"), None), P(("section", "rows"))),
        check_vma=False,
    )
```

time: 235 us -> 78.6 us (0.33)
  blocking collectives: 78.6 us -> 0 us
  waiting for transfers between devices: 80.4 us -> 19.1 us
  other arithmetic: 49.6 us -> 5.09 us
  Pallas kernels: 0 us -> 33.6 us
  starting transfers between devices: 0.04 us -> 16 us
  between operations: 14.1 us -> 0.79 us
  matrix products: 11.1 us -> 0 us
  local copies, waits for them, and re-layouts: 1.1 us -> 3.8 us
    reduce_scatter x1 -> x0, waiting for transfers between devices: 80.4 us -> none  [shards(): lax.psum_scatter(sums, ('section', 'rows'), scatter_dimension=0, tiled=True)]
    scatter-add x2 -> x0, other arithmetic: 46.4 us -> none  [the longest x1 24.5 us: tally_rows(): sums = jax.ops.segment_sum(row_sums, keys, num_segments=KEYS)]
    all_gather x3 -> x0, blocking collectives: 40.2 us -> none  [the longest x1 15.1 us: shards(): every_words = lax.all_gather(predicates, 'section', axis=0, tiled=True)]
    unnamed x1 -> x0, blocking collectives: 38.4 us -> none
    pallas_call x0 -> x4, Pallas kernels: none -> 33.6 us  [call(): pl.pallas_call(kernel, out_shape=out_shape, in_specs=[SMEM if i in smem e...]
    ppermute x0 -> x11, waiting for transfers between devices: none -> 19.1 us  [the longest x3 9.08 us: shards(): moved = lax.ppermute(packed, axes, plan.perm(0, k))]
    ppermute x0 -> x11, starting transfers between devices: none -> 16 us  [the longest x3 5.64 us: shards(): packed = lax.ppermute(packed, axes, plan.perm(0, k))]
    dot_general x4 -> x0, matrix products: 11.1 us -> none  [advance(): jnp.dot(hidden, weight, precision=lax.Precision.HIGHEST, preferred_elemen...]
  transfers between devices with their start and end apart: 1 -> 11, of which waited for: 1 -> 7; matrix products, arithmetic and copies ran while one was open for 10% -> 3% of each run, Pallas kernels for 0% -> 24%
where the time goes in v1:
time: 78.6 us; the launch traced here: 78.3 us
  Pallas kernels  33.6 us (43%)
  waiting for transfers between devices  19.1 us (24%)
  starting transfers between devices  16 us (20%)
  other arithmetic  5.09 us (6%)
  local copies, waits for them, and re-layouts  3.8 us (5%)
  between operations  0.79 us (1%)
    pallas_call x4, Pallas kernels, call(): pl.pallas_call(kernel, out_shape=out_shape, in_specs=[SMEM if i in smem e...  33.6 us
    ppermute x3, waiting for transfers between devices, shards(): moved = lax.ppermute(packed, axes, plan.perm(0, k))  9.08 us
    ppermute x2, waiting for transfers between devices, shards(): lax.ppermute(packed, axes, plan.perm(2 << plan.orders[color][step], 0))  6.14 us
    ppermute x3, starting transfers between devices, shards(): packed = lax.ppermute(packed, axes, plan.perm(0, k))  5.64 us
    ppermute x3, starting transfers between devices, shards(): moved = lax.ppermute(packed, axes, plan.perm(0, k))  4.57 us
    ppermute x3, waiting for transfers between devices, shards(): packed = lax.ppermute(packed, axes, plan.perm(0, k))  3.83 us
    unnamed x11, local copies, waits for them, and re-layouts  3.35 us
    ppermute x2, starting transfers between devices, shards(): lax.ppermute(m, axes, plan.perm(2 << order[0], 0))  3.01 us
  transfers between devices with their start and end apart: 11, of which 7 were waited for; matrix products, arithmetic and copies ran while one was open for 3% of the time, Pallas kernels for 24%

profile of v1, /device:TPU:0, one launch (start us, length us, event | category | flops | bytes accessed | tf_op | source)
XLA Modules:
  0.0 78.3 jit_solution(9481393605210894944)
XLA Ops:
  0.6 0.7 shift-right-arithmetic_and_fusion.3
  1.3 0.1 and.54
  1.4 0.1 and.56
  1.5 0.1 and.60
  1.6 0.1 and.58
  1.7 0.1 pad.29.clone
  1.8 1.6 %fusion.7 = (f32[136,128]{1,0:T(8,128)S(1)}, f32[136,128]{1,0:T(8,128)S(1)}, f32[136,128]{1,0:T(8,128)S(1)}, f32[136,128]{1,0:T(8,128)}) fusion(f32[1,128]{1,0:T(1,128)} %param.11, f32[4,128]{1,0:T(4,128)S(1)} %get-tuple-element.26, f32[128,128]{1,0:T(8,128)} %bitcast.52, f32[136]{0:T(256)S(1)} %pad.29.clone, f32[4,128]{1,0:T(4,128)S(1)} %get-tuple-element.28, ...), kind=kLoop, calls=%fused_computation.28 | loop fusion | flops 208896 | bytes 353312 | tf_op jit(solution)/shard_map/concatenate | solution.py:229
  3.4 5.1 %collective-permute-start.2 = (f32[136,128]{1,0:T(8,128)S(1)}, f32[136,128]{1,0:T(8,128)S(1)}, u32[]{:S(2)}, u32[]{:S(2)}) collective-permute-start(f32[136,128]{1,0:T(8,128)S(1)} %get-tuple-element.22), channel_id=1, source_target_pairs={{0,24},{1,25},{2,26},{3,27},{4,28},{5,29},{6,30},{7,31},{8,16},{9,... | collective-permute-start | bytes 208904 | tf_op jit(solution)/shard_map/ppermute | solution.py:231
  8.4 0.0 collective-permute-start
  8.4 0.6 collective-permute-start.1
  9.0 1.3 %copy.12.valid_ref = s32[4,1]{1,0:T(4,128)} copy(s32[4,1]{0,1:T(1,128)} %param.8) | data formatting | bytes 32 | tf_op args[2]
  10.3 1.1 %collective-permute-done.2.b3 = f32[136,128]{1,0:T(8,128)S(1)} collective-permute-done((f32[136,128]{1,0:T(8,128)S(1)}, f32[136,128]{1,0:T(8,128)S(1)}, u32[]{:S(2)}, u32[]{:S(2)}) %collective-permute-start.2) | collective-permute-done | bytes 69664 | tf_op jit(solution)/shard_map/ppermute | solution.py:231
  11.5 0.0 copy-start.2
  11.5 1.8 %collective-permute-done.b1 = f32[136,128]{1,0:T(8,128)S(1)} collective-permute-done((f32[136,128]{1,0:T(8,128)S(1)}, f32[136,128]{1,0:T(8,128)S(1)}, u32[]{:S(2)}, u32[]{:S(2)}) %collective-permute-start) | collective-permute-done | bytes 69664 | tf_op jit(solution)/shard_map/ppermute | solution.py:231
  13.3 0.0 copy-start.3
  13.3 0.9 %collective-permute-done.1.b2 = f32[136,128]{1,0:T(8,128)S(1)} collective-permute-done((f32[136,128]{1,0:T(8,128)S(1)}, f32[136,128]{1,0:T(8,128)S(1)}, u32[]{:S(2)}, u32[]{:S(2)}) %collective-permute-start.1) | collective-permute-done | bytes 69664 | tf_op jit(solution)/shard_map/ppermute | solution.py:231
  14.2 0.0 copy-start.4
  14.2 0.0 copy-done.2
  14.2 0.0 copy-done.3
  14.2 0.6 copy-done.4
  14.8 7.3 %advance.1 = (f32[4160,128]{1,0:T(8,128)}, f32[32,128]{1,0:T(8,128)}) custom-call(f32[4,1024,128]{2,1,0:T(8,128)} %x_ref.1, s32[4,1024]{1,0:T(4,128)} %keys_ref.1, s32[4,1]{1,0:T(4,128)} %copy.12.valid_ref, f32[136,128]{1,0:T(8,128)} %get-tuple-element.25.b0, f32[136,128]{1,0:T(8,128)} %copy-done.3, f32[136,128]{1,0:T(8,128)} %copy-done.4, f32[136,128]{1,0:T(8,128)} %copy-done.2), custom_call_target="tpu_custom_call" | custom-call | tf_op jit(solution)/shard_map/advance/pallas_call | solution.py:206
  22.1 0.0 collective-permute-start.3
  22.1 7.1 %table_own.1.part_ref = f32[2048,128]{1,0:T(8,128)} custom-call(f32[4160,128]{1,0:T(8,128)} %get-tuple-element.9.own_ref), custom_call_target="tpu_custom_call" | custom-call | tf_op jit(solution)/shard_map/table_own/pallas_call | solution.py:206
  29.2 0.0 collective-permute-done.3.other_ref
  29.2 0.0 copy-start
  29.2 1.4 %copy-done = f32[4160,128]{1,0:T(8,128)} copy-done((f32[4160,128]{1,0:T(8,128)}, f32[4160,128]{1,0:T(8,128)S(1)}, u32[]{:S(2)}) %copy-start) | copy-done | bytes 2129944
  30.6 7.3 %table_send.1 = (f32[1032,128]{1,0:T(8,128)}, f32[1032,128]{1,0:T(8,128)}, f32[16,128]{1,0:T(8,128)}) custom-call(f32[4160,128]{1,0:T(8,128)} %copy-done, f32[2048,128]{1,0:T(8,128)} %table_own.1.part_ref, f32[32,128]{1,0:T(8,128)} %get-tuple-element.10.count_ref), custom_call_target="tpu_custom_call" | custom-call | tf_op jit(solution)/shard_map/table_send/pallas_call | solution.py:206
  37.9 1.5 %collective-permute-start.4 = (f32[1032,128]{1,0:T(8,128)}, f32[1032,128]{1,0:T(8,128)S(1)}, u32[]{:S(2)}, u32[]{:S(2)}) collective-permute-start(f32[1032,128]{1,0:T(8,128)} %get-tuple-element.13), channel_id=1, source_target_pairs={{0,2},{1,3},{2,0},{3,1},{4,6},{5,7},{6,4},{7,5},{8,10},{9,11},{10,... | collective-permute-start | bytes 1585160 | tf_op jit(solution)/shard_map/ppermute | solution.py:267
  39.4 1.5 %collective-permute-start.6 = (f32[1032,128]{1,0:T(8,128)}, f32[1032,128]{1,0:T(8,128)S(1)}, u32[]{:S(2)}, u32[]{:S(2)}) collective-permute-start(f32[1032,128]{1,0:T(8,128)} %get-tuple-element.15), channel_id=1, source_target_pairs={{0,4},{1,5},{2,6},{3,7},{4,0},{5,1},{6,2},{7,3},{8,12},{9,13},{10,... | collective-permute-start | bytes 1585160 | tf_op jit(solution)/shard_map/ppermute | solution.py:267
  40.9 11.9 %table_keep.1 = (f32[1032,128]{1,0:T(8,128)}, f32[1032,128]{1,0:T(8,128)}) custom-call(f32[4160,128]{1,0:T(8,128)} %get-tuple-element.9.own_ref, f32[4160,128]{1,0:T(8,128)} %copy-done, f32[16,128]{1,0:T(8,128)} %get-tuple-element.11.count_ref), custom_call_target="tpu_custom_call" | custom-call | tf_op jit(solution)/shard_map/table_keep/pallas_call | solution.py:206
  52.8 0.0 copy-start.1
  52.8 0.0 collective-permute-done.4
  52.8 1.2 %add.73 = f32[1032,128]{1,0:T(8,128)S(1)} add(f32[1032,128]{1,0:T(8,128)} %get-tuple-element.12, f32[1032,128]{1,0:T(8,128)S(1)} %collective-permute-done.4) | non-fusion elementwise | flops 132096 | bytes 1585152 | tf_op jit(solution)/shard_map/add | solution.py:277
  54.0 1.2 %collective-permute-start.5 = (f32[516,128]{1,0:T(8,128)S(1)}, f32[516,128]{1,0:T(8,128)S(1)}, u32[]{:S(2)}, u32[]{:S(2)}) collective-permute-start(f32[516,128]{1,0:T(8,128)S(1)} %pad_maximum_fusion), channel_id=1, source_target_pairs={{0,4},{1,5},{2,6},{3,7},{4,0},{5,1},{6,2},{7,3},{8,12},{9,13},{10,... | collective-permute-start | bytes 792584 | tf_op jit(solution)/shard_map/ppermute | solution.py:285
  55.3 0.0 collective-permute-done.6
  55.3 0.0 copy-done.1
  55.3 0.1 add.75
  55.4 1.6 %collective-permute-start.7 = (f32[516,128]{1,0:T(8,128)S(1)}, f32[516,128]{1,0:T(8,128)S(1)}, u32[]{:S(2)}, u32[]{:S(2)}) collective-permute-start(f32[516,128]{1,0:T(8,128)S(1)} %pad_maximum_fusion.1), channel_id=1, source_target_pairs={{0,2},{1,3},{2,0},{3,1},{4,6},{5,7},{6,4},{7,5},{8,10},{9,11},{10,... | collective-permute-start | bytes 792584 | tf_op jit(solution)/shard_map/ppermute | solution.py:285
  57.0 5.3 %collective-permute-done.5 = f32[516,128]{1,0:T(8,128)S(1)} collective-permute-done((f32[516,128]{1,0:T(8,128)S(1)}, f32[516,128]{1,0:T(8,128)S(1)}, u32[]{:S(2)}, u32[]{:S(2)}) %collective-permute-start.5) | collective-permute-done | bytes 264224 | tf_op jit(solution)/shard_map/ppermute | solution.py:285
  62.4 0.8 %collective-permute-done.7 = f32[516,128]{1,0:T(8,128)S(1)} collective-permute-done((f32[516,128]{1,0:T(8,128)S(1)}, f32[516,128]{1,0:T(8,128)S(1)}, u32[]{:S(2)}, u32[]{:S(2)}) %collective-permute-start.7) | collective-permute-done | bytes 264224 | tf_op jit(solution)/shard_map/ppermute | solution.py:285
  63.3 3.1 %collective-permute-start.10 = (f32[258,128]{1,0:T(8,128)S(1)}, f32[258,128]{1,0:T(8,128)S(1)}, u32[]{:S(2)}, u32[]{:S(2)}) collective-permute-start(f32[258,128]{1,0:T(8,128)S(1)} %pad_maximum_fusion.8), channel_id=1, source_target_pairs={{0,24},{1,25},{2,26},{3,27},{4,28},{5,29},{6,30},{7,31},{8,16},{9,... | collective-permute-start | bytes 396296 | tf_op jit(solution)/shard_map/ppermute | solution.py:299
  66.4 0.1 collective-permute-start.9
  66.5 1.4 %collective-permute-start.8 = (f32[258,128]{1,0:T(8,128)S(1)}, f32[258,128]{1,0:T(8,128)S(1)}, u32[]{:S(2)}, u32[]{:S(2)}) collective-permute-start(f32[258,128]{1,0:T(8,128)S(1)} %pad_maximum_fusion.6), channel_id=1, source_target_pairs={{0,8},{1,9},{2,10},{3,11},{4,12},{5,13},{6,14},{7,15},{8,0},{9,1},... | collective-permute-start | bytes 396296 | tf_op jit(solution)/shard_map/ppermute | solution.py:299
  67.9 3.7 %collective-permute-done.10 = f32[258,128]{1,0:T(8,128)S(1)} collective-permute-done((f32[258,128]{1,0:T(8,128)S(1)}, f32[258,128]{1,0:T(8,128)S(1)}, u32[]{:S(2)}, u32[]{:S(2)}) %collective-permute-start.10) | collective-permute-done | bytes 132128 | tf_op jit(solution)/shard_map/ppermute | solution.py:299
  71.6 5.4 %collective-permute-done.9 = f32[258,128]{1,0:T(8,128)S(1)} collective-permute-done((f32[258,128]{1,0:T(8,128)S(1)}, f32[258,128]{1,0:T(8,128)S(1)}, u32[]{:S(2)}, u32[]{:S(2)}) %collective-permute-start.9) | collective-permute-done | bytes 132128 | tf_op jit(solution)/shard_map/ppermute | solution.py:299
  77.0 0.0 collective-permute-done.8
  77.0 0.6 broadcast_maximum_fusion
  77.6 0.8 fusion.3
  (18 shorter events, 0.3 us)
Async XLA Ops:
  3.4 8.1 %collective-permute-start.2 = (f32[136,128]{1,0:T(8,128)S(1)}, f32[136,128]{1,0:T(8,128)S(1)}, u32[]{:S(2)}, u32[]{:S(2)}) collective-permute-start(f32[136,128]{1,0:T(8,128)S(1)} %get-tuple-element.22), channel_id=1, source_target_pairs={{0,24},{1,25},{2,26},{3,27},{4,28},{5,29},{6,30},{7,31},{8,16},{9,... | collective-permute-start | bytes 208904 | tf_op jit(solution)/shard_map/ppermute | solution.py:231
  8.4 4.9 %collective-permute-start = (f32[136,128]{1,0:T(8,128)S(1)}, f32[136,128]{1,0:T(8,128)S(1)}, u32[]{:S(2)}, u32[]{:S(2)}) collective-permute-start(f32[136,128]{1,0:T(8,128)S(1)} %get-tuple-element.23), channel_id=1, source_target_pairs={{0,8},{1,9},{2,10},{3,11},{4,12},{5,13},{6,14},{7,15},{8,0},{9,1},... | collective-permute-start | bytes 208904 | tf_op jit(solution)/shard_map/ppermute | solution.py:231
  8.4 5.7 %collective-permute-start.1 = (f32[136,128]{1,0:T(8,128)S(1)}, f32[136,128]{1,0:T(8,128)S(1)}, u32[]{:S(2)}, u32[]{:S(2)}) collective-permute-start(f32[136,128]{1,0:T(8,128)S(1)} %get-tuple-element.24), channel_id=1, source_target_pairs={{0,16},{1,17},{2,18},{3,19},{4,20},{5,21},{6,22},{7,23},{8,24},{9,... | collective-permute-start | bytes 208904 | tf_op jit(solution)/shard_map/ppermute | solution.py:231
  11.5 2.7 %copy-start.2 = (f32[136,128]{1,0:T(8,128)}, f32[136,128]{1,0:T(8,128)S(1)}, u32[]{:S(2)}) copy-start(f32[136,128]{1,0:T(8,128)S(1)} %collective-permute-done.2.b3) | copy-start | bytes 208900
  13.3 0.9 %copy-start.3 = (f32[136,128]{1,0:T(8,128)}, f32[136,128]{1,0:T(8,128)S(1)}, u32[]{:S(2)}) copy-start(f32[136,128]{1,0:T(8,128)S(1)} %collective-permute-done.b1) | copy-start | bytes 208900
  14.2 0.6 copy-start.4
  22.1 7.1 %collective-permute-start.3 = (f32[4160,128]{1,0:T(8,128)}, f32[4160,128]{1,0:T(8,128)S(1)}, u32[]{:S(2)}, u32[]{:S(2)}) collective-permute-start(f32[4160,128]{1,0:T(8,128)} %get-tuple-element.9.own_ref), channel_id=1, source_target_pairs={{0,1},{1,0},{2,3},{3,2},{4,5},{5,4},{6,7},{7,6},{8,9},{9,8},{10,11... | collective-permute-start | bytes 6389768 | tf_op jit(solution)/shard_map/ppermute | solution.py:248
  29.2 1.4 %copy-start = (f32[4160,128]{1,0:T(8,128)}, f32[4160,128]{1,0:T(8,128)S(1)}, u32[]{:S(2)}) copy-start(f32[4160,128]{1,0:T(8,128)S(1)} %collective-permute-done.3.other_ref) | copy-start | bytes 6389764
  37.9 14.9 %collective-permute-start.4 = (f32[1032,128]{1,0:T(8,128)}, f32[1032,128]{1,0:T(8,128)S(1)}, u32[]{:S(2)}, u32[]{:S(2)}) collective-permute-start(f32[1032,128]{1,0:T(8,128)} %get-tuple-element.13), channel_id=1, source_target_pairs={{0,2},{1,3},{2,0},{3,1},{4,6},{5,7},{6,4},{7,5},{8,10},{9,11},{10,... | collective-permute-start | bytes 1585160 | tf_op jit(solution)/shard_map/ppermute | solution.py:267
  39.4 15.9 %collective-permute-start.6 = (f32[1032,128]{1,0:T(8,128)}, f32[1032,128]{1,0:T(8,128)S(1)}, u32[]{:S(2)}, u32[]{:S(2)}) collective-permute-start(f32[1032,128]{1,0:T(8,128)} %get-tuple-element.15), channel_id=1, source_target_pairs={{0,4},{1,5},{2,6},{3,7},{4,0},{5,1},{6,2},{7,3},{8,12},{9,13},{10,... | collective-permute-start | bytes 1585160 | tf_op jit(solution)/shard_map/ppermute | solution.py:267
  52.8 2.5 %copy-start.1 = (f32[1032,128]{1,0:T(8,128)S(1)}, f32[1032,128]{1,0:T(8,128)}, u32[]{:S(2)}) copy-start(f32[1032,128]{1,0:T(8,128)} %get-tuple-element.14) | copy-start | bytes 1585156
  54.0 8.3 %collective-permute-start.5 = (f32[516,128]{1,0:T(8,128)S(1)}, f32[516,128]{1,0:T(8,128)S(1)}, u32[]{:S(2)}, u32[]{:S(2)}) collective-permute-start(f32[516,128]{1,0:T(8,128)S(1)} %pad_maximum_fusion), channel_id=1, source_target_pairs={{0,4},{1,5},{2,6},{3,7},{4,0},{5,1},{6,2},{7,3},{8,12},{9,13},{10,... | collective-permute-start | bytes 792584 | tf_op jit(solution)/shard_map/ppermute | solution.py:285
  55.4 7.7 %collective-permute-start.7 = (f32[516,128]{1,0:T(8,128)S(1)}, f32[516,128]{1,0:T(8,128)S(1)}, u32[]{:S(2)}, u32[]{:S(2)}) collective-permute-start(f32[516,128]{1,0:T(8,128)S(1)} %pad_maximum_fusion.1), channel_id=1, source_target_pairs={{0,2},{1,3},{2,0},{3,1},{4,6},{5,7},{6,4},{7,5},{8,10},{9,11},{10,... | collective-permute-start | bytes 792584 | tf_op jit(solution)/shard_map/ppermute | solution.py:285
  63.3 8.3 %collective-permute-start.10 = (f32[258,128]{1,0:T(8,128)S(1)}, f32[258,128]{1,0:T(8,128)S(1)}, u32[]{:S(2)}, u32[]{:S(2)}) collective-permute-start(f32[258,128]{1,0:T(8,128)S(1)} %pad_maximum_fusion.8), channel_id=1, source_target_pairs={{0,24},{1,25},{2,26},{3,27},{4,28},{5,29},{6,30},{7,31},{8,16},{9,... | collective-permute-start | bytes 396296 | tf_op jit(solution)/shard_map/ppermute | solution.py:299
  66.4 10.6 %collective-permute-start.9 = (f32[258,128]{1,0:T(8,128)S(1)}, f32[258,128]{1,0:T(8,128)S(1)}, u32[]{:S(2)}, u32[]{:S(2)}) collective-permute-start(f32[258,128]{1,0:T(8,128)S(1)} %pad_maximum_fusion.7), channel_id=1, source_target_pairs={{0,16},{1,17},{2,18},{3,19},{4,20},{5,21},{6,22},{7,23},{8,24},{9,... | collective-permute-start | bytes 396296 | tf_op jit(solution)/shard_map/ppermute | solution.py:299
  66.5 10.5 %collective-permute-start.8 = (f32[258,128]{1,0:T(8,128)S(1)}, f32[258,128]{1,0:T(8,128)S(1)}, u32[]{:S(2)}, u32[]{:S(2)}) collective-permute-start(f32[258,128]{1,0:T(8,128)S(1)} %pad_maximum_fusion.6), channel_id=1, source_target_pairs={{0,8},{1,9},{2,10},{3,11},{4,12},{5,13},{6,14},{7,15},{8,0},{9,1},... | collective-permute-start | bytes 396296 | tf_op jit(solution)/shard_map/ppermute | solution.py:299

commit v2 on v1

--- a/solution.py
+++ b/solution.py
@@ -12,7 +12,7 @@
 BF16 = jnp.bfloat16
 F32 = jnp.float32
 VMEM = pl.BlockSpec(memory_space=pltpu.VMEM)
-SMEM = pl.BlockSpec(memory_space=pltpu.SMEM)
+HBM = pl.BlockSpec(memory_space=pltpu.HBM)
 
 
 def split(value):
@@ -67,13 +67,64 @@
     return slot * plan.color + low + core * plan.half
 
 
-def advance_kernel(plan, x_ref, keys_ref, valid_ref, b0, b1, b2, b3, out_ref, count_ref, weight, bias, bytes_):
-    batches, block, width = x_ref.shape
+def fetch(pairs, sems):
+    copies = [pltpu.make_async_copy(src, dst, sems.at[i]) for i, (src, dst) in enumerate(pairs)]
+    for copy in copies:
+        copy.start()
+    return copies
+
+
+def pack_kernel(plan, batches, predicates_hbm, weight_hbm, bias_hbm, *refs):
+    buffers = refs[: plan.sections]
+    predicates_ref, weight_ref, bias_ref, sems = refs[plan.sections :]
+    copies = fetch(
+        ((weight_hbm, weight_ref), (predicates_hbm, predicates_ref), (bias_hbm, bias_ref)),
+        sems,
+    )
+    z = lax.axis_index("section")
+    for copy in copies:
+        copy.wait()
+    width = weight_ref.shape[1]
+    words_in_batch = predicates_ref.shape[2]
+    for k, buffer in enumerate(buffers):
+        buffer[:width, :] = weight_ref[0]
+        buffer[width:, :] = jnp.zeros((buffer.shape[0] - width, width), F32)
+        words = predicates_ref[0, pl.ds((z ^ k) * batches, batches), :]
+        for b in range(4):
+            at = width + b * batches
+            buffer[at : at + batches, :words_in_batch] = ((words >> (8 * b)) & 255).astype(F32)
+        at = width + 4 * batches
+        buffer[at : at + 1, :] = bias_ref[...]
+
+
+def advance_kernel(
+    plan,
+    x_hbm,
+    keys_hbm,
+    valid_hbm,
+    b0,
+    b1,
+    b2,
+    b3,
+    out_ref,
+    count_ref,
+    x_ref,
+    keys_ref,
+    valid_ref,
+    weight,
+    bias,
+    bytes_,
+    sems,
+):
+    batches, block, width = x_hbm.shape
+    keys_copy, valid_copy, *x_copies = fetch(
+        ((keys_hbm, keys_ref), (valid_hbm, valid_ref), *((x_hbm.at[m], x_ref.at[m]) for m in range(batches))),
+        sems,
+    )
     z = lax.axis_index("section")
     row = lax.axis_index("rows")
     core = row & 1
     place = row >> 1
-    bytes_[...] = jnp.zeros_like(bytes_)
     for k, buffer in enumerate((b0, b1, b2, b3)):
         level = z ^ k
         high, low = split(buffer[:width, :])
@@ -81,26 +132,29 @@
         weight[level, width:, :width] = high
         weight[level, :width, width:] = low
         weight[level, width:, width:] = jnp.zeros_like(low)
-        bytes_[level, :4, :] = buffer[width : width + 4, :]
-        bias[level, :1, :] = buffer[width + 4 : width + 5, :]
-    words = bytes_[...].reshape(SECTIONS * 8, LANES).astype(BF16)
+        bytes_[level] = buffer[width : width + 4 * batches, :]
+        bias[level, :1, :] = buffer[width + 4 * batches : width + 4 * batches + 1, :]
+    words = bytes_[...].reshape(SECTIONS * 4 * batches, LANES).astype(BF16)
     lane = iota((1, block), 1)
+    spread = (iota((LANES, block), 0) == (iota((LANES, block), 1) >> 5)).astype(F32).astype(BF16)
+    found = jnp.dot(words, spread, preferred_element_type=F32).astype(jnp.int32)
+    which = (lane >> 3) & 3
+    keys_copy.wait()
+    valid_copy.wait()
     table = jnp.zeros((2 * plan.half // LANES, LANES), F32)
     per_batch = block // LANES
     for m in range(batches):
-        spread = (iota((LANES, block), 0) == (iota((LANES, block), 1) >> 5) + m * 32).astype(F32).astype(BF16)
-        found = jnp.dot(words, spread, preferred_element_type=F32).astype(jnp.int32)
-        which = (lane >> 3) & 3
         flags = []
         for s in range(SECTIONS):
-            byte = found[8 * s : 8 * s + 1]
+            at = s * 4 * batches + m
+            byte = found[at : at + 1]
             for b in range(1, 4):
-                byte = jnp.where(which == b, found[8 * s + b : 8 * s + b + 1], byte)
+                byte = jnp.where(which == b, found[at + b * batches : at + b * batches + 1], byte)
             flags.append((byte >> (lane & 7)) & 1)
         depth = flags[-1]
         for flag in flags[-2::-1]:
             depth = flag * (1 + depth)
-        depth = jnp.where(lane < valid_ref[m, 0], depth, 0)
+        depth = jnp.where(lane < valid_ref[:, m : m + 1], depth, 0)
         code = slot_codes(plan, keys_ref[m : m + 1, :], z, place)
         code_f = code.astype(F32)
         for i in range(per_batch):
@@ -112,6 +166,7 @@
         table = table + lax.dot_general(outer, inner, (((1,), (1,)), ((), ())), preferred_element_type=F32)
         column = jnp.transpose(jnp.broadcast_to(depth_f, (8, block)))[:, :1]
         depth_b = jnp.broadcast_to(column, (block, width))
+        x_copies[m].wait()
         hidden = x_ref[m]
         total = jnp.zeros((block, width), F32)
         for s in range(SECTIONS):
@@ -202,15 +257,16 @@
     b_ref[plan.send :, :] = count_ref[share:]
 
 
-def call(kernel, out_shape, operands, scratch=(), name=None, smem=()):
+def call(kernel, out_shape, operands, scratch=(), name=None, hbm=(), limit=24):
     return pl.pallas_call(
         kernel,
         out_shape=out_shape,
-        in_specs=[SMEM if i in smem else VMEM for i in range(len(operands))],
+        in_specs=[HBM if i in hbm else VMEM for i in range(len(operands))],
         out_specs=jax.tree.map(lambda _: VMEM, out_shape),
         scratch_shapes=list(scratch),
         name=name,
-    )(*operands)
+        compiler_params=pltpu.CompilerParams(vmem_limit_bytes=limit << 20),
+    )(*(pltpu.with_memory_space_constraint(o, pltpu.HBM) if i in hbm else o for i, o in enumerate(operands)))
 
 
 def shape(*dims):
@@ -220,30 +276,41 @@
 def shards(plan, rows_data, row_keys, valid_counts, predicates, section_weight, section_bias):
     batches, block, width = rows_data.shape
     axes = ("section", "rows")
-    z = lax.axis_index("section")
-    words = predicates.reshape(plan.sections, batches * predicates.shape[2])
-    pieces = jnp.stack([(words >> (8 * b)) & 255 for b in range(4)], axis=1).astype(F32)
-    buffers = []
-    for k in range(plan.sections):
-        part = lax.dynamic_index_in_dim(pieces, z ^ k, 0, keepdims=False)
-        packed = jnp.concatenate([section_weight[0], part, section_bias, jnp.zeros((3, width), F32)], axis=0)
-        if k:
-            packed = lax.ppermute(packed, axes, plan.perm(0, k))
-        buffers.append(packed)
+    packed = call(
+        functools.partial(pack_kernel, plan, batches),
+        (shape((width + 4 * batches + 8) // 8 * 8, width),) * plan.sections,
+        (predicates, section_weight, section_bias),
+        scratch=[
+            pltpu.VMEM(predicates.shape, jnp.int32),
+            pltpu.VMEM(section_weight.shape, F32),
+            pltpu.VMEM(section_bias.shape, F32),
+            pltpu.SemaphoreType.DMA((3,)),
+        ],
+        name="pack",
+        hbm=(0, 1, 2),
+        limit=4,
+    )
+    buffers = [packed[0]]
+    for k in range(1, plan.sections):
+        buffers.append(lax.ppermute(packed[k], axes, plan.perm(0, k)))
     rows = batches * block
     lines = rows // LANES
     tables = plan.half // LANES
     own, count = call(
         functools.partial(advance_kernel, plan),
         (shape(rows + lines + tables, width), shape(tables, LANES)),
-        (rows_data, row_keys, valid_counts, *buffers),
+        (rows_data, row_keys, valid_counts.reshape(1, batches), *buffers),
         scratch=[
+            pltpu.VMEM((batches, block, width), F32),
+            pltpu.VMEM((batches, block), jnp.int32),
+            pltpu.VMEM((1, batches), jnp.int32),
             pltpu.VMEM((SECTIONS, 2 * width, 2 * width), BF16),
             pltpu.VMEM((SECTIONS, 8, width), F32),
-            pltpu.VMEM((SECTIONS, 8, LANES), F32),
+            pltpu.VMEM((SECTIONS, 4 * batches, LANES), F32),
+            pltpu.SemaphoreType.DMA((batches + 2,)),
         ],
         name="advance",
-        smem=(2,),
+        hbm=(0, 1, 2),
     )
     other = lax.ppermute(own, axes, plan.perm(1, 0))
     tile, piece = min(256, plan.send), min(1024, rows)

time: 78.6 us -> 67.4 us (0.86)
  Pallas kernels: 33.6 us -> 24.3 us
  waiting for transfers between devices: 19.1 us -> 23.8 us
  local copies, waits for them, and re-layouts: 3.8 us -> 0.04 us
  other arithmetic: 5.09 us -> 1.67 us
    pallas_call x4 -> x5, Pallas kernels: 33.6 us -> 24.3 us  [call(): pl.pallas_call(kernel, out_shape=out_shape, in_specs=[HBM if i in hbm els...]
    unnamed x11 -> x0, local copies, waits for them, and re-layouts: 3.35 us -> none
    ppermute x3, waiting for transfers between devices: 3.83 us -> 6.29 us  [shards(): buffers.append(lax.ppermute(packed[k], axes, plan.perm(0, k)))]
    ppermute x2, waiting for transfers between devices: 0.01 us -> 2.39 us  [shards(): lax.ppermute(m, axes, plan.perm(2 << order[0], 0))]
    concatenate x1 -> x0, other arithmetic: 1.58 us -> none  [shards(): jnp.concatenate([section_weight[0], part, section_bias, jnp.zeros((3, wid...]
    add x2, other arithmetic: 1.26 us -> 0.12 us  [shards(): total = kept[color] + got[color]]
  transfers between devices with their start and end apart: 11 -> 11, of which waited for: 7 -> 7; matrix products, arithmetic and copies ran while one was open for 3% -> 0% of each run, Pallas kernels for 24% -> 20%
where the time goes in v2:
time: 67.4 us; the launch traced here: 67.2 us
  Pallas kernels  24.3 us (36%)
  waiting for transfers between devices  23.8 us (35%)
  starting transfers between devices  16.6 us (25%)
  other arithmetic  1.67 us (2%)
  between operations  0.79 us (1%)
    pallas_call x5, Pallas kernels, call(): pl.pallas_call(kernel, out_shape=out_shape, in_specs=[HBM if i in hbm els...  24.3 us
    ppermute x3, waiting for transfers between devices, shards(): moved = lax.ppermute(packed, axes, plan.perm(0, k))  8.95 us
    ppermute x3, waiting for transfers between devices, shards(): buffers.append(lax.ppermute(packed[k], axes, plan.perm(0, k)))  6.29 us
    ppermute x2, waiting for transfers between devices, shards(): lax.ppermute(packed, axes, plan.perm(2 << plan.orders[color][step], 0))  6.14 us
    ppermute x3, starting transfers between devices, shards(): buffers.append(lax.ppermute(packed[k], axes, plan.perm(0, k)))  5.71 us
    ppermute x3, starting transfers between devices, shards(): moved = lax.ppermute(packed, axes, plan.perm(0, k))  4.58 us
    ppermute x2, starting transfers between devices, shards(): lax.ppermute(packed, axes, plan.perm(2 << plan.orders[color][step], 0))  3.14 us
    ppermute x2, starting transfers between devices, shards(): lax.ppermute(m, axes, plan.perm(2 << order[0], 0))  3.08 us
  transfers between devices with their start and end apart: 11, of which 7 were waited for; matrix products, arithmetic and copies ran while one was open for 0% of the time, Pallas kernels for 20%

profile of v2, /device:TPU:0, one launch (start us, length us, event | category | flops | bytes accessed | tf_op | source)
XLA Modules:
  0.0 67.2 jit_solution(6944457005169964549)
XLA Ops:
  0.6 0.9 %pack.1 = (f32[152,128]{1,0:T(8,128)S(1)}, f32[152,128]{1,0:T(8,128)S(1)}, f32[152,128]{1,0:T(8,128)S(1)}, f32[152,128]{1,0:T(8,128)S(1)}) custom-call(s32[1,16,32]{2,1,0:T(8,128)} %predicates_hbm.1, f32[1,128,128]{2,1,0:T(8,128)} %weight_hbm.1, f32[1,128]{1,0:T(1,128)} %bias_hbm.1), custom_call_target="tpu_custom_call" | custom-call | tf_op jit(solution)/shard_map/pack/pallas_call | solution.py:261
  1.5 3.1 %collective-permute-start = (f32[152,128]{1,0:T(8,128)S(1)}, f32[152,128]{1,0:T(8,128)S(1)}, u32[]{:S(2)}, u32[]{:S(2)}) collective-permute-start(f32[152,128]{1,0:T(8,128)S(1)} %get-tuple-element.14), channel_id=1, source_target_pairs={{0,8},{1,9},{2,10},{3,11},{4,12},{5,13},{6,14},{7,15},{8,0},{9,1},... | collective-permute-start | bytes 233480 | tf_op jit(solution)/shard_map/ppermute | solution.py:295
  4.7 2.6 %collective-permute-start.1 = (f32[152,128]{1,0:T(8,128)S(1)}, f32[152,128]{1,0:T(8,128)S(1)}, u32[]{:S(2)}, u32[]{:S(2)}) collective-permute-start(f32[152,128]{1,0:T(8,128)S(1)} %get-tuple-element.15), channel_id=1, source_target_pairs={{0,16},{1,17},{2,18},{3,19},{4,20},{5,21},{6,22},{7,23},{8,24},{9,... | collective-permute-start | bytes 233480 | tf_op jit(solution)/shard_map/ppermute | solution.py:295
  7.2 0.0 collective-permute-start.2
  7.2 0.0 collective-permute-done.b1
  7.2 5.5 %collective-permute-done.1.b2 = f32[152,128]{1,0:T(8,128)S(1)} collective-permute-done((f32[152,128]{1,0:T(8,128)S(1)}, f32[152,128]{1,0:T(8,128)S(1)}, u32[]{:S(2)}, u32[]{:S(2)}) %collective-permute-start.1) | collective-permute-done | bytes 77856 | tf_op jit(solution)/shard_map/ppermute | solution.py:295
  12.7 0.8 %collective-permute-done.2.b3 = f32[152,128]{1,0:T(8,128)S(1)} collective-permute-done((f32[152,128]{1,0:T(8,128)S(1)}, f32[152,128]{1,0:T(8,128)S(1)}, u32[]{:S(2)}, u32[]{:S(2)}) %collective-permute-start.2) | collective-permute-done | bytes 77856 | tf_op jit(solution)/shard_map/ppermute | solution.py:295
  13.5 5.4 %advance.1 = (f32[4160,128]{1,0:T(8,128)S(1)}, f32[32,128]{1,0:T(8,128)S(1)}) custom-call(f32[4,1024,128]{2,1,0:T(8,128)} %x_hbm.1, s32[4,1024]{1,0:T(4,128)} %keys_hbm.1, s32[1,4]{1,0:T(1,128)} %bitcast.44, f32[152,128]{1,0:T(8,128)S(1)} %get-tuple-element.13.b0, f32[152,128]{1,0:T(8,128)S(1)} %collective-permute-done.b1, ...), custom_call_target="tpu_custom_call" | custom-call | tf_op jit(solution)/shard_map/advance/pallas_call | solution.py:261
  18.9 0.1 collective-permute-start.3
  19.0 4.5 %table_own.1.part_ref = f32[2048,128]{1,0:T(8,128)S(1)} custom-call(f32[4160,128]{1,0:T(8,128)S(1)} %get-tuple-element.17.own_ref), custom_call_target="tpu_custom_call" | custom-call | tf_op jit(solution)/shard_map/table_own/pallas_call | solution.py:261
  23.5 0.0 collective-permute-done.3.other_ref
  23.5 4.5 %table_send.1 = (f32[1032,128]{1,0:T(8,128)S(1)}, f32[1032,128]{1,0:T(8,128)S(1)}, f32[16,128]{1,0:T(8,128)S(1)}) custom-call(f32[4160,128]{1,0:T(8,128)S(1)} %collective-permute-done.3.other_ref, f32[2048,128]{1,0:T(8,128)S(1)} %table_own.1.part_ref, f32[32,128]{1,0:T(8,128)S(1)} %get-tuple-element.18.count_ref), custom_call_target="tpu_custom_call" | custom-call | tf_op jit(solution)/shard_map/table_send/pallas_call | solution.py:261
  28.1 1.6 %collective-permute-start.4 = (f32[1032,128]{1,0:T(8,128)S(1)}, f32[1032,128]{1,0:T(8,128)S(1)}, u32[]{:S(2)}, u32[]{:S(2)}) collective-permute-start(f32[1032,128]{1,0:T(8,128)S(1)} %get-tuple-element.21), channel_id=1, source_target_pairs={{0,2},{1,3},{2,0},{3,1},{4,6},{5,7},{6,4},{7,5},{8,10},{9,11},{10,... | collective-permute-start | bytes 1585160 | tf_op jit(solution)/shard_map/ppermute | solution.py:334
  29.6 1.5 %collective-permute-start.6 = (f32[1032,128]{1,0:T(8,128)S(1)}, f32[1032,128]{1,0:T(8,128)S(1)}, u32[]{:S(2)}, u32[]{:S(2)}) collective-permute-start(f32[1032,128]{1,0:T(8,128)S(1)} %get-tuple-element.23), channel_id=1, source_target_pairs={{0,4},{1,5},{2,6},{3,7},{4,0},{5,1},{6,2},{7,3},{8,12},{9,13},{10,... | collective-permute-start | bytes 1585160 | tf_op jit(solution)/shard_map/ppermute | solution.py:334
  31.2 9.0 %table_keep.1 = (f32[1032,128]{1,0:T(8,128)S(1)}, f32[1032,128]{1,0:T(8,128)S(1)}) custom-call(f32[4160,128]{1,0:T(8,128)S(1)} %get-tuple-element.17.own_ref, f32[4160,128]{1,0:T(8,128)S(1)} %collective-permute-done.3.other_ref, f32[16,128]{1,0:T(8,128)S(1)} %get-tuple-element.19.count_ref), custom_call_target="tpu_custom_call" | custom-call | tf_op jit(solution)/shard_map/table_keep/pallas_call | solution.py:261
  40.2 2.4 %collective-permute-done.4 = f32[1032,128]{1,0:T(8,128)S(1)} collective-permute-done((f32[1032,128]{1,0:T(8,128)S(1)}, f32[1032,128]{1,0:T(8,128)S(1)}, u32[]{:S(2)}, u32[]{:S(2)}) %collective-permute-start.4) | collective-permute-done | bytes 528416 | tf_op jit(solution)/shard_map/ppermute | solution.py:334
  42.6 0.1 add.56
  42.7 1.6 %collective-permute-start.5 = (f32[516,128]{1,0:T(8,128)S(1)}, f32[516,128]{1,0:T(8,128)S(1)}, u32[]{:S(2)}, u32[]{:S(2)}) collective-permute-start(f32[516,128]{1,0:T(8,128)S(1)} %pad_maximum_fusion), channel_id=1, source_target_pairs={{0,4},{1,5},{2,6},{3,7},{4,0},{5,1},{6,2},{7,3},{8,12},{9,13},{10,... | collective-permute-start | bytes 792584 | tf_op jit(solution)/shard_map/ppermute | solution.py:352
  44.3 0.0 collective-permute-done.6
  44.3 0.1 add.58
  44.4 1.6 %collective-permute-start.7 = (f32[516,128]{1,0:T(8,128)S(1)}, f32[516,128]{1,0:T(8,128)S(1)}, u32[]{:S(2)}, u32[]{:S(2)}) collective-permute-start(f32[516,128]{1,0:T(8,128)S(1)} %pad_maximum_fusion.1), channel_id=1, source_target_pairs={{0,2},{1,3},{2,0},{3,1},{4,6},{5,7},{6,4},{7,5},{8,10},{9,11},{10,... | collective-permute-start | bytes 792584 | tf_op jit(solution)/shard_map/ppermute | solution.py:352
  46.0 4.7 %collective-permute-done.5 = f32[516,128]{1,0:T(8,128)S(1)} collective-permute-done((f32[516,128]{1,0:T(8,128)S(1)}, f32[516,128]{1,0:T(8,128)S(1)}, u32[]{:S(2)}, u32[]{:S(2)}) %collective-permute-start.5) | collective-permute-done | bytes 264224 | tf_op jit(solution)/shard_map/ppermute | solution.py:352
  50.7 1.4 %collective-permute-done.7 = f32[516,128]{1,0:T(8,128)S(1)} collective-permute-done((f32[516,128]{1,0:T(8,128)S(1)}, f32[516,128]{1,0:T(8,128)S(1)}, u32[]{:S(2)}, u32[]{:S(2)}) %collective-permute-start.7) | collective-permute-done | bytes 264224 | tf_op jit(solution)/shard_map/ppermute | solution.py:352
  52.3 2.5 %collective-permute-start.10 = (f32[258,128]{1,0:T(8,128)S(1)}, f32[258,128]{1,0:T(8,128)S(1)}, u32[]{:S(2)}, u32[]{:S(2)}) collective-permute-start(f32[258,128]{1,0:T(8,128)S(1)} %pad_maximum_fusion.4), channel_id=1, source_target_pairs={{0,24},{1,25},{2,26},{3,27},{4,28},{5,29},{6,30},{7,31},{8,16},{9,... | collective-permute-start | bytes 396296 | tf_op jit(solution)/shard_map/ppermute | solution.py:366
  54.8 0.4 collective-permute-start.9
  55.3 1.6 %collective-permute-start.8 = (f32[258,128]{1,0:T(8,128)S(1)}, f32[258,128]{1,0:T(8,128)S(1)}, u32[]{:S(2)}, u32[]{:S(2)}) collective-permute-start(f32[258,128]{1,0:T(8,128)S(1)} %pad_maximum_fusion.2), channel_id=1, source_target_pairs={{0,8},{1,9},{2,10},{3,11},{4,12},{5,13},{6,14},{7,15},{8,0},{9,1},... | collective-permute-start | bytes 396296 | tf_op jit(solution)/shard_map/ppermute | solution.py:366
  56.9 3.7 %collective-permute-done.10 = f32[258,128]{1,0:T(8,128)S(1)} collective-permute-done((f32[258,128]{1,0:T(8,128)S(1)}, f32[258,128]{1,0:T(8,128)S(1)}, u32[]{:S(2)}, u32[]{:S(2)}) %collective-permute-start.10) | collective-permute-done | bytes 132128 | tf_op jit(solution)/shard_map/ppermute | solution.py:366
  60.6 5.2 %collective-permute-done.9 = f32[258,128]{1,0:T(8,128)S(1)} collective-permute-done((f32[258,128]{1,0:T(8,128)S(1)}, f32[258,128]{1,0:T(8,128)S(1)}, u32[]{:S(2)}, u32[]{:S(2)}) %collective-permute-start.9) | collective-permute-done | bytes 132128 | tf_op jit(solution)/shard_map/ppermute | solution.py:366
  65.8 0.0 collective-permute-done.8
  65.9 0.6 broadcast_maximum_fusion
  66.4 0.8 %fusion.3 = f32[256,128]{1,0:T(8,128)} fusion(f32[258,128]{1,0:T(8,128)S(1)} %collective-permute-done.10, f32[258,128]{1,0:T(8,128)S(1)} %collective-permute-done.9, f32[258,128]{1,0:T(8,128)S(1)} %collective-permute-done.8, f32[1,2,128,128]{3,2,0,1:T(8,128)S(1)} %get-tuple-element.26, f32[256]{0:T(256)S(1)} %get-tuple-element.24), kind=kLoop, calls=%fused_computation.17 | loop fusion | flops 131072 | bytes 656384 | tf_op jit(solution)/shard_map/div | solution.py:369
  (15 shorter events, 0.3 us)
Async XLA Ops:
  1.5 5.7 %collective-permute-start = (f32[152,128]{1,0:T(8,128)S(1)}, f32[152,128]{1,0:T(8,128)S(1)}, u32[]{:S(2)}, u32[]{:S(2)}) collective-permute-start(f32[152,128]{1,0:T(8,128)S(1)} %get-tuple-element.14), channel_id=1, source_target_pairs={{0,8},{1,9},{2,10},{3,11},{4,12},{5,13},{6,14},{7,15},{8,0},{9,1},... | collective-permute-start | bytes 233480 | tf_op jit(solution)/shard_map/ppermute | solution.py:295
  4.7 8.1 %collective-permute-start.1 = (f32[152,128]{1,0:T(8,128)S(1)}, f32[152,128]{1,0:T(8,128)S(1)}, u32[]{:S(2)}, u32[]{:S(2)}) collective-permute-start(f32[152,128]{1,0:T(8,128)S(1)} %get-tuple-element.15), channel_id=1, source_target_pairs={{0,16},{1,17},{2,18},{3,19},{4,20},{5,21},{6,22},{7,23},{8,24},{9,... | collective-permute-start | bytes 233480 | tf_op jit(solution)/shard_map/ppermute | solution.py:295
  7.2 6.3 %collective-permute-start.2 = (f32[152,128]{1,0:T(8,128)S(1)}, f32[152,128]{1,0:T(8,128)S(1)}, u32[]{:S(2)}, u32[]{:S(2)}) collective-permute-start(f32[152,128]{1,0:T(8,128)S(1)} %get-tuple-element.16), channel_id=1, source_target_pairs={{0,24},{1,25},{2,26},{3,27},{4,28},{5,29},{6,30},{7,31},{8,16},{9,... | collective-permute-start | bytes 233480 | tf_op jit(solution)/shard_map/ppermute | solution.py:295
  18.9 4.6 %collective-permute-start.3 = (f32[4160,128]{1,0:T(8,128)S(1)}, f32[4160,128]{1,0:T(8,128)S(1)}, u32[]{:S(2)}, u32[]{:S(2)}) collective-permute-start(f32[4160,128]{1,0:T(8,128)S(1)} %get-tuple-element.17.own_ref), channel_id=1, source_target_pairs={{0,1},{1,0},{2,3},{3,2},{4,5},{5,4},{6,7},{7,6},{8,9},{9,8},{10,11... | collective-permute-start | bytes 6389768 | tf_op jit(solution)/shard_map/ppermute | solution.py:315
  28.1 14.5 %collective-permute-start.4 = (f32[1032,128]{1,0:T(8,128)S(1)}, f32[1032,128]{1,0:T(8,128)S(1)}, u32[]{:S(2)}, u32[]{:S(2)}) collective-permute-start(f32[1032,128]{1,0:T(8,128)S(1)} %get-tuple-element.21), channel_id=1, source_target_pairs={{0,2},{1,3},{2,0},{3,1},{4,6},{5,7},{6,4},{7,5},{8,10},{9,11},{10,... | collective-permute-start | bytes 1585160 | tf_op jit(solution)/shard_map/ppermute | solution.py:334
  29.6 14.6 %collective-permute-start.6 = (f32[1032,128]{1,0:T(8,128)S(1)}, f32[1032,128]{1,0:T(8,128)S(1)}, u32[]{:S(2)}, u32[]{:S(2)}) collective-permute-start(f32[1032,128]{1,0:T(8,128)S(1)} %get-tuple-element.23), channel_id=1, source_target_pairs={{0,4},{1,5},{2,6},{3,7},{4,0},{5,1},{6,2},{7,3},{8,12},{9,13},{10,... | collective-permute-start | bytes 1585160 | tf_op jit(solution)/shard_map/ppermute | solution.py:334
  42.7 8.0 %collective-permute-start.5 = (f32[516,128]{1,0:T(8,128)S(1)}, f32[516,128]{1,0:T(8,128)S(1)}, u32[]{:S(2)}, u32[]{:S(2)}) collective-permute-start(f32[516,128]{1,0:T(8,128)S(1)} %pad_maximum_fusion), channel_id=1, source_target_pairs={{0,4},{1,5},{2,6},{3,7},{4,0},{5,1},{6,2},{7,3},{8,12},{9,13},{10,... | collective-permute-start | bytes 792584 | tf_op jit(solution)/shard_map/ppermute | solution.py:352
  44.4 7.7 %collective-permute-start.7 = (f32[516,128]{1,0:T(8,128)S(1)}, f32[516,128]{1,0:T(8,128)S(1)}, u32[]{:S(2)}, u32[]{:S(2)}) collective-permute-start(f32[516,128]{1,0:T(8,128)S(1)} %pad_maximum_fusion.1), channel_id=1, source_target_pairs={{0,2},{1,3},{2,0},{3,1},{4,6},{5,7},{6,4},{7,5},{8,10},{9,11},{10,... | collective-permute-start | bytes 792584 | tf_op jit(solution)/shard_map/ppermute | solution.py:352
  52.3 8.3 %collective-permute-start.10 = (f32[258,128]{1,0:T(8,128)S(1)}, f32[258,128]{1,0:T(8,128)S(1)}, u32[]{:S(2)}, u32[]{:S(2)}) collective-permute-start(f32[258,128]{1,0:T(8,128)S(1)} %pad_maximum_fusion.4), channel_id=1, source_target_pairs={{0,24},{1,25},{2,26},{3,27},{4,28},{5,29},{6,30},{7,31},{8,16},{9,... | collective-permute-start | bytes 396296 | tf_op jit(solution)/shard_map/ppermute | solution.py:366
  54.8 11.0 %collective-permute-start.9 = (f32[258,128]{1,0:T(8,128)S(1)}, f32[258,128]{1,0:T(8,128)S(1)}, u32[]{:S(2)}, u32[]{:S(2)}) collective-permute-start(f32[258,128]{1,0:T(8,128)S(1)} %pad_maximum_fusion.3), channel_id=1, source_target_pairs={{0,16},{1,17},{2,18},{3,19},{4,20},{5,21},{6,22},{7,23},{8,24},{9,... | collective-permute-start | bytes 396296 | tf_op jit(solution)/shard_map/ppermute | solution.py:366
  55.3 10.6 %collective-permute-start.8 = (f32[258,128]{1,0:T(8,128)S(1)}, f32[258,128]{1,0:T(8,128)S(1)}, u32[]{:S(2)}, u32[]{:S(2)}) collective-permute-start(f32[258,128]{1,0:T(8,128)S(1)} %pad_maximum_fusion.2), channel_id=1, source_target_pairs={{0,8},{1,9},{2,10},{3,11},{4,12},{5,13},{6,14},{7,15},{8,0},{9,1},... | collective-permute-start | bytes 396296 | tf_op jit(solution)/shard_map/ppermute | solution.py:366

commit v3 on v2

v3 whole, which is shorter than its diff:
```python
import functools
import jax
import jax.numpy as jnp
from jax import lax
from jax.experimental import pallas as pl
from jax.experimental.pallas import tpu as pltpu
from jax.sharding import PartitionSpec as P

KEYS = 8192
STEP = 512
SECTIONS = 4
LANES = 128
BF16 = jnp.bfloat16
F32 = jnp.float32
VMEM = pl.BlockSpec(memory_space=pltpu.VMEM)
HBM = pl.BlockSpec(memory_space=pltpu.HBM)


def split(value):
    high = value.astype(BF16)
    return high, (value - high.astype(F32)).astype(BF16)


def iota(shape, axis):
    return lax.broadcasted_iota(jnp.int32, shape, axis)


class Plan:
    def __init__(self, mesh):
        self.sections = mesh.shape["section"]
        self.rows = mesh.shape["rows"]
        self.planes = self.rows.bit_length() - 2
        self.owned = KEYS // (self.sections * self.rows)
        self.color = self.owned // 2
        self.half = KEYS // 2
        self.inner = self.sections // 2
        self.chunk = self.half // 4
        bits = list(range(self.planes))
        turn = self.planes // 2
        self.orders = (bits, bits[turn:] + bits[:turn])

    def perm(self, row_xor, section_xor):
        return [
            (s * self.rows + r, (s ^ section_xor) * self.rows + (r ^ row_xor))
            for s in range(self.sections)
            for r in range(self.rows)
        ]


def slot_codes(plan, keys, z, p):
    log_color = plan.color.bit_length() - 1
    low = keys & (plan.color - 1)
    rest = keys >> log_color
    color = rest & 1
    core = (rest >> 1) & 1
    place = ((rest >> 2) & ((1 << plan.planes) - 1)) ^ p
    zrel = (rest >> (2 + plan.planes)) ^ z
    inner = []
    for order in plan.orders:
        index = 0
        for bit in order:
            index = index * 2 + (1 - ((place >> bit) & 1))
        inner.append(index)
    index = jnp.where(color == 0, inner[0], inner[1])
    count = 1 << (plan.planes - 1)
    kept = index >> (plan.planes - 1)
    near = 1 - zrel // plan.inner
    slot = ((near * 2 + kept) * 2 + color) * count + (index & (count - 1))
    return (slot * plan.inner + (zrel & (plan.inner - 1))) * plan.color + low + core * plan.half


def fetch(pairs, sems):
    copies = [pltpu.make_async_copy(src, dst, sems.at[i]) for i, (src, dst) in enumerate(pairs)]
    for copy in copies:
        copy.start()
    return copies


def pack_kernel(plan, batches, predicates_hbm, weight_hbm, bias_hbm, *refs):
    buffers = refs[: plan.sections]
    predicates_ref, weight_ref, bias_ref, sems = refs[plan.sections :]
    copies = fetch(
        ((weight_hbm, weight_ref), (predicates_hbm, predicates_ref), (bias_hbm, bias_ref)),
        sems,
    )
    z = lax.axis_index("section")
    for copy in copies:
        copy.wait()
    width = weight_ref.shape[1]
    words_in_batch = predicates_ref.shape[2]
    for k, buffer in enumerate(buffers):
        buffer[:width, :] = weight_ref[0]
        buffer[width:, :] = jnp.zeros((buffer.shape[0] - width, width), F32)
        words = predicates_ref[0, pl.ds((z ^ k) * batches, batches), :]
        for b in range(4):
            at = width + b * batches
            buffer[at : at + batches, :words_in_batch] = ((words >> (8 * b)) & 255).astype(F32)
        at = width + 4 * batches
        buffer[at : at + 1, :] = bias_ref[...]


def advance_kernel(
    plan,
    x_hbm,
    keys_hbm,
    valid_hbm,
    b0,
    b1,
    b2,
    b3,
    out_ref,
    count_ref,
    x_ref,
    keys_ref,
    valid_ref,
    weight,
    bias,
    bytes_,
    sparse,
    packed,
    lines_ref,
    table,
    sems,
):
    batches, block, width = x_hbm.shape
    keys_copy, valid_copy, *x_copies = fetch(
        ((keys_hbm, keys_ref), (valid_hbm, valid_ref), *((x_hbm.at[m], x_ref.at[m]) for m in range(batches))),
        sems,
    )
    z = lax.axis_index("section")
    row = lax.axis_index("rows")
    core = row & 1
    place = row >> 1
    for k, buffer in enumerate((b0, b1, b2, b3)):
        level = z ^ k
        high, low = split(buffer[:width, :])
        weight[level, :width, :width] = high
        weight[level, width:, :width] = high
        weight[level, :width, width:] = low
        weight[level, width:, width:] = jnp.zeros_like(low)
        bytes_[level] = buffer[width : width + 4 * batches, :]
        bias[level, :1, :] = buffer[width + 4 * batches : width + 4 * batches + 1, :]
    words = bytes_[...].reshape(SECTIONS * 4 * batches, LANES).astype(BF16)
    lane = iota((1, block), 1)
    spread = (iota((LANES, block), 0) == (iota((LANES, block), 1) >> 5)).astype(F32).astype(BF16)
    found = jnp.dot(words, spread, preferred_element_type=F32).astype(jnp.int32)
    which = (lane >> 3) & 3
    keys_copy.wait()
    valid_copy.wait()
    tile = sparse.shape[2]
    per_batch = block // tile
    for m in range(batches):
        flags = []
        for s in range(SECTIONS):
            at = s * 4 * batches + m
            byte = found[at : at + 1]
            for b in range(1, 4):
                byte = jnp.where(which == b, found[at + b * batches : at + b * batches + 1], byte)
            flags.append((byte >> (lane & 7)) & 1)
        depth = flags[-1]
        for flag in flags[-2::-1]:
            depth = flag * (1 + depth)
        depth = jnp.where(lane < valid_ref[:, m : m + 1], depth, 0).astype(F32)
        code = slot_codes(plan, keys_ref[m : m + 1, :], z, place).astype(F32)
        for q in range(per_batch):
            at = m * per_batch + q
            sparse[0, at : at + 1, :] = depth[:, q * tile : (q + 1) * tile]
            sparse[1, at : at + 1, :] = code[:, q * tile : (q + 1) * tile]

    depths = sparse[0]
    before = (iota((tile, tile), 0) < iota((tile, tile), 1)).astype(F32).astype(BF16)
    live = jnp.where(depths > 0.0, 1.0, 0.0)
    places = jnp.dot(live.astype(BF16), before, preferred_element_type=F32)
    places = jnp.where(depths > 0.0, places, -1.0)
    row8 = iota((8, tile), 0)
    lane8 = iota((8, LANES), 1)
    empty = jnp.where(iota((8, LANES), 0) == 0, -1.0, 0.0)
    for i in range(lines_ref.shape[0]):
        lines_ref[i] = empty
    offset = 0
    for m in range(batches):
        x_copies[m].wait()
        for q in range(per_batch):
            at = m * per_batch + q
            move = jnp.where(places[at : at + 1] == iota((tile, tile), 0).astype(F32), 1.0, 0.0).astype(BF16)
            both = jnp.concatenate(split(x_ref[m, q * tile : (q + 1) * tile, :]), axis=1)
            moved = jnp.dot(move, both, preferred_element_type=F32)
            packed[pl.ds(offset, tile), :] = moved[:, :width] + moved[:, width:]
            code = sparse[1, at : at + 1, :] + 1.0
            high = jnp.floor(code * (1.0 / LANES))
            info = jnp.where(row8 == 0, high, jnp.where(row8 == 1, code - high * LANES, 0.0))
            info = jnp.where(row8 == 2, sparse[0, at : at + 1, :], info).astype(BF16)
            info = lax.dot_general(info, move, (((1,), (1,)), ((), ())), preferred_element_type=F32)
            code = info[:1] * LANES + info[1:2] - 1.0
            info = jnp.where(row8 == 0, code, jnp.where(row8 == 1, info[2:3], 0.0))
            shift = offset & (LANES - 1)
            info = pltpu.roll(jnp.concatenate([info, empty], axis=1), shift, axis=1)
            line = offset // LANES
            lines_ref[line] = jnp.where(lane8 < shift, lines_ref[line], info[:, :LANES])
            for j in range(1, tile // LANES + 1):
                lines_ref[line + j] = info[:, j * LANES : (j + 1) * LANES]
            number = jnp.sum(live[at : at + 1]).astype(jnp.int32)
            offset = pl.multiple_of(offset + ((number + 7) // 8) * 8, 8)
    packed[pl.ds(offset, STEP), :] = jnp.zeros((STEP, width), F32)
    table[...] = jnp.zeros_like(table)

    def levels(step, _):
        at = pl.multiple_of(step * STEP, STEP)
        columns, codes, depths = [], [], []
        for j in range(STEP // LANES):
            line = lines_ref[step * (STEP // LANES) + j]
            columns.append(jnp.broadcast_to(jnp.transpose(line)[:, 1:2], (LANES, width)))
            codes.append(line[:1])
            depths.append(line[1:2])
        depth = jnp.concatenate(columns, axis=0)
        code = jnp.concatenate(codes, axis=1).astype(jnp.int32)
        outer = (iota((table.shape[0], STEP), 0) == (code >> 7)).astype(F32).astype(BF16)
        inner = iota((LANES, STEP), 0) == (code & (LANES - 1))
        inner = jnp.where(inner, jnp.concatenate(depths, axis=1), 0.0).astype(BF16)
        table[...] += lax.dot_general(outer, inner, (((1,), (1,)), ((), ())), preferred_element_type=F32)
        hidden = packed[pl.ds(at, STEP), :]
        total = jnp.zeros((STEP, width), F32)
        for s in range(SECTIONS):
            both = jnp.concatenate(split(hidden), axis=1)
            product = jnp.dot(both, weight[s], preferred_element_type=F32)
            hidden = hidden + jnp.tanh(product[:, :width] + product[:, width:] + bias[s, :1, :])
            total = total + jnp.where(depth > s, hidden, 0.0)
        out_ref[pl.ds(at, STEP), :] = total
        return 0

    lax.fori_loop(0, (offset + (STEP - 1)) // STEP, levels, 0)
    rows = batches * block
    for i in range(rows // LANES):
        out_ref[rows + i : rows + i + 1, :] = lines_ref[i, :1, :]
    lines = plan.half // LANES
    first = core == 0
    at = rows + rows // LANES
    count_ref[...] = jnp.where(first, table[:lines], table[lines:])
    out_ref[at : at + lines, :] = jnp.where(first, table[lines:], table[:lines])
    out_ref[at + lines :, :] = jnp.full((8, width), offset.astype(F32))


def add_products(plan, rows, source, first, slots, sums):
    core = lax.axis_index("rows") & 1
    base = (core * plan.half + first).astype(F32)
    used = jnp.max(source[source.shape[0] - 8 :, :]).astype(jnp.int32)
    tile = min(256, slots)
    sums[:slots, :] = jnp.zeros((slots, sums.shape[1]), F32)

    def body(step, _):
        at = pl.multiple_of(step * STEP, STEP)
        both = jnp.concatenate(split(source[pl.ds(at, STEP), :]), axis=1)
        codes = [source[pl.ds(rows + step * (STEP // LANES) + i, 1), :] - base for i in range(STEP // LANES)]
        for t in range(slots // tile):
            spots = (iota((tile, LANES), 0) + t * tile).astype(F32)
            marks = [jnp.where(code == spots, 1.0, 0.0).astype(BF16) for code in codes]
            mark = jnp.concatenate(marks, axis=1)
            sums[t * tile : (t + 1) * tile, :] += jnp.dot(mark, both, preferred_element_type=F32)
        return 0

    lax.fori_loop(0, (used + (STEP - 1)) // STEP, body, 0)


def own_kernel(plan, rows, own_ref, out_ref, sums):
    width = out_ref.shape[1]
    add_products(plan, rows, own_ref, 0, plan.half, sums)
    out_ref[...] = sums[:, :width] + sums[:, width:]


def other_kernel(plan, rows, first, other_ref, part_ref, count_ref, *refs):
    *outs, sums = refs
    width = part_ref.shape[1]
    size = plan.chunk // 2
    lines = size // LANES
    at = rows + rows // LANES
    for chunk, start in enumerate(first):
        add_products(plan, rows, other_ref, start, plan.chunk, sums)
        for color in range(2):
            out = outs[2 * chunk + color]
            low = color * size
            slot = start + low
            out[:size, :] = (
                sums[low : low + size, :width] + sums[low : low + size, width:] + part_ref[slot : slot + size, :]
            )
            line = slot // LANES
            out[size:, :] = count_ref[line : line + lines, :] + other_ref[at + line : at + line + lines, :]


def call(kernel, out_shape, operands, scratch=(), name=None, hbm=(), limit=24):
    return pl.pallas_call(
        kernel,
        out_shape=out_shape,
        in_specs=[HBM if i in hbm else VMEM for i in range(len(operands))],
        out_specs=jax.tree.map(lambda _: VMEM, out_shape),
        scratch_shapes=list(scratch),
        name=name,
        compiler_params=pltpu.CompilerParams(vmem_limit_bytes=limit << 20),
    )(*(pltpu.with_memory_space_constraint(o, pltpu.HBM) if i in hbm else o for i, o in enumerate(operands)))


def shape(*dims):
    return jax.ShapeDtypeStruct(dims, F32)


def lines_of(counts):
    return jnp.pad(counts, (0, -counts.shape[0] % LANES)).reshape(-1, LANES)


def shards(plan, rows_data, row_keys, valid_counts, predicates, section_weight, section_bias):
    batches, block, width = rows_data.shape
    axes = ("section", "rows")
    packed = call(
        functools.partial(pack_kernel, plan, batches),
        (shape((width + 4 * batches + 8) // 8 * 8, width),) * plan.sections,
        (predicates, section_weight, section_bias),
        scratch=[
            pltpu.VMEM(predicates.shape, jnp.int32),
            pltpu.VMEM(section_weight.shape, F32),
            pltpu.VMEM(section_bias.shape, F32),
            pltpu.SemaphoreType.DMA((3,)),
        ],
        name="pack",
        hbm=(0, 1, 2),
        limit=4,
    )
    buffers = [packed[0]]
    for k in range(1, plan.sections):
        buffers.append(lax.ppermute(packed[k], axes, plan.perm(0, k)))
    rows = batches * block
    lines = rows // LANES
    tables = plan.half // LANES
    tile = min(256, block)
    own, count = call(
        functools.partial(advance_kernel, plan),
        (shape(rows + lines + tables + 8, width), shape(tables, LANES)),
        (rows_data, row_keys, valid_counts.reshape(1, batches), *buffers),
        scratch=[
            pltpu.VMEM((batches, block, width), F32),
            pltpu.VMEM((batches, block), jnp.int32),
            pltpu.VMEM((1, batches), jnp.int32),
            pltpu.VMEM((SECTIONS, 2 * width, 2 * width), BF16),
            pltpu.VMEM((SECTIONS, 8, width), F32),
            pltpu.VMEM((SECTIONS, 4 * batches, LANES), F32),
            pltpu.VMEM((2, rows // tile, tile), F32),
            pltpu.VMEM((rows + STEP, width), F32),
            pltpu.VMEM((lines + STEP // LANES, 8, LANES), F32),
            pltpu.VMEM((2 * tables, LANES), F32),
            pltpu.SemaphoreType.DMA((batches + 2,)),
        ],
        name="advance",
        hbm=(0, 1, 2),
    )
    other = lax.ppermute(own, axes, plan.perm(1, 0))
    part = call(
        functools.partial(own_kernel, plan, rows),
        shape(plan.half, width),
        (own,),
        scratch=[pltpu.VMEM((plan.half, 2 * width), F32)],
        name="table_own",
    )
    size = plan.chunk // 2
    message = shape(size + size // LANES, width)

    def tables_of(name, *chunks, after=()):
        operand, _ = lax.optimization_barrier((part, tuple(after)))
        outs = call(
            functools.partial(other_kernel, plan, rows, [c * plan.chunk for c in chunks]),
            (message,) * (2 * len(chunks)),
            (other, operand, count),
            scratch=[pltpu.VMEM((plan.chunk, 2 * width), F32)],
            name=name,
        )
        return [outs[2 * i : 2 * i + 2] for i in range(len(chunks))]

    def halve(messages, step):
        return [
            lax.ppermute(m, axes, plan.perm(2 << order[step], 0)) for m, order in zip(messages, plan.orders)
        ]

    got = []
    for near in range(2):
        (sent,) = tables_of("table_far" if near == 0 else "table_near", 2 * near)
        got.append(halve(sent, 0))
    finals, sent = [], []
    for near in range(2):
        (kept,) = tables_of("keep_far" if near == 0 else "keep_near", 2 * near + 1, after=sent)
        states = []
        for color in range(2):
            total = kept[color] + got[near][color]
            states.append((total[:size], total[size:].reshape(-1)))
        sent = []
        for step in range(1, plan.planes):
            cut = states[0][0].shape[0] // 2
            packed = [jnp.concatenate([sums[:cut], lines_of(counts[:cut])], axis=0) for sums, counts in states]
            sent = sent or packed
            states = [
                (sums[cut:] + m[:cut], counts[cut:] + m[cut:].reshape(-1)[:cut])
                for (sums, counts), m in zip(states, halve(packed, step))
            ]
        sums = jnp.stack([s.reshape(plan.inner, plan.color, width) for s, _ in states], axis=1)
        counts = jnp.stack([c.reshape(plan.inner, plan.color) for _, c in states], axis=1)
        sums = sums.reshape(plan.inner, plan.owned, width)
        counts = counts.reshape(plan.inner, plan.owned)
        for i in range(plan.inner):
            k = (1 - near) * plan.inner + i
            packed = jnp.concatenate([sums[i], lines_of(counts[i])], axis=0)
            finals.append(lax.ppermute(packed, axes, plan.perm(0, k)) if k else packed)
    total = functools.reduce(jnp.add, finals)
    number = total[plan.owned :].reshape(-1)[: plan.owned]
    return total[: plan.owned] / jnp.maximum(number, 1.0)[:, None], number


def solution(mesh):
    return jax.shard_map(
        functools.partial(shards, Plan(mesh)),
        mesh=mesh,
        in_specs=(
            P("section", "rows", None),
            P("section", "rows"),
            P("section", "rows"),
            P("section", None, "rows"),
            P("section", None, None),
            P("section", None),
        ),
        out_specs=(P(("section", "rows"), None), P(("section", "rows"))),
        check_vma=False,
    )
```

time: 67.4 us -> 64.1 us (0.951)
  Pallas kernels: 24.3 us -> 21 us
  waiting for transfers between devices: 23.8 us -> 21.2 us
  starting transfers between devices: 16.6 us -> 19.2 us
    pallas_call x5 -> x7, Pallas kernels: 24.3 us -> 21 us  [call(): pl.pallas_call(kernel, out_shape=out_shape, in_specs=[HBM if i in hbm els...]
    ppermute x7 -> x11, starting transfers between devices: 10.8 us -> 13.4 us  [the longest x8 10.6 us: halve(): lax.ppermute(m, axes, plan.perm(2 << order[step], 0))]
    ppermute x7 -> x11, waiting for transfers between devices: 17.5 us -> 14.9 us  [the longest x3 8.94 us: shards(): finals.append(lax.ppermute(packed, axes, plan.perm(0, k)) if k else packed)]
  transfers between devices with their start and end apart: 11 -> 15, of which waited for: 7 -> 8; matrix products, arithmetic and copies ran while one was open for 0% -> 1% of each run, Pallas kernels for 20% -> 18%
where the time goes in v3:
time: 64.1 us
  waiting for transfers between devices  21.2 us (33%)
  Pallas kernels  21 us (33%)
  starting transfers between devices  19.2 us (30%)
  other arithmetic  1.73 us (3%)
  between operations  0.91 us (1%)
    pallas_call x7, Pallas kernels, call(): pl.pallas_call(kernel, out_shape=out_shape, in_specs=[HBM if i in hbm els...  21 us
    ppermute x8, starting transfers between devices, halve(): lax.ppermute(m, axes, plan.perm(2 << order[step], 0))  10.6 us
    ppermute x3, waiting for transfers between devices, shards(): finals.append(lax.ppermute(packed, axes, plan.perm(0, k)) if k else packed)  8.94 us
    ppermute x3, waiting for transfers between devices, shards(): buffers.append(lax.ppermute(packed[k], axes, plan.perm(0, k)))  6.29 us
    ppermute x8, waiting for transfers between devices, halve(): lax.ppermute(m, axes, plan.perm(2 << order[step], 0))  6 us
    ppermute x3, starting transfers between devices, shards(): buffers.append(lax.ppermute(packed[k], axes, plan.perm(0, k)))  5.71 us
    ppermute x3, starting transfers between devices, shards(): finals.append(lax.ppermute(packed, axes, plan.perm(0, k)) if k else packed)  2.84 us
  transfers between devices with their start and end apart: 15, of which 8 were waited for; matrix products, arithmetic and copies ran while one was open for 1% of the time, Pallas kernels for 18%

profile of v3, /device:TPU:0, one launch (start us, length us, event | category | flops | bytes accessed | tf_op | source)
XLA Modules:
  0.0 64.1 jit_solution(17435259331421598487)
XLA Ops:
  0.6 0.9 %pack.1 = (f32[152,128]{1,0:T(8,128)S(1)}, f32[152,128]{1,0:T(8,128)S(1)}, f32[152,128]{1,0:T(8,128)S(1)}, f32[152,128]{1,0:T(8,128)S(1)}) custom-call(s32[1,16,32]{2,1,0:T(8,128)} %predicates_hbm.1, f32[1,128,128]{2,1,0:T(8,128)} %weight_hbm.1, f32[1,128]{1,0:T(1,128)} %bias_hbm.1), custom_call_target="tpu_custom_call" | custom-call | tf_op jit(solution)/shard_map/pack/pallas_call | solution.py:290
  1.5 3.1 %collective-permute-start = (f32[152,128]{1,0:T(8,128)S(1)}, f32[152,128]{1,0:T(8,128)S(1)}, u32[]{:S(2)}, u32[]{:S(2)}) collective-permute-start(f32[152,128]{1,0:T(8,128)S(1)} %get-tuple-element.18), channel_id=1, source_target_pairs={{0,8},{1,9},{2,10},{3,11},{4,12},{5,13},{6,14},{7,15},{8,0},{9,1},... | collective-permute-start | bytes 233480 | tf_op jit(solution)/shard_map/ppermute | solution.py:328
  4.7 2.6 %collective-permute-start.1 = (f32[152,128]{1,0:T(8,128)S(1)}, f32[152,128]{1,0:T(8,128)S(1)}, u32[]{:S(2)}, u32[]{:S(2)}) collective-permute-start(f32[152,128]{1,0:T(8,128)S(1)} %get-tuple-element.19), channel_id=1, source_target_pairs={{0,16},{1,17},{2,18},{3,19},{4,20},{5,21},{6,22},{7,23},{8,24},{9,... | collective-permute-start | bytes 233480 | tf_op jit(solution)/shard_map/ppermute | solution.py:328
  7.2 0.0 collective-permute-start.2
  7.2 0.0 collective-permute-done.b1
  7.2 5.5 %collective-permute-done.1.b2 = f32[152,128]{1,0:T(8,128)S(1)} collective-permute-done((f32[152,128]{1,0:T(8,128)S(1)}, f32[152,128]{1,0:T(8,128)S(1)}, u32[]{:S(2)}, u32[]{:S(2)}) %collective-permute-start.1) | collective-permute-done | bytes 77856 | tf_op jit(solution)/shard_map/ppermute | solution.py:328
  12.7 0.8 %collective-permute-done.2.b3 = f32[152,128]{1,0:T(8,128)S(1)} collective-permute-done((f32[152,128]{1,0:T(8,128)S(1)}, f32[152,128]{1,0:T(8,128)S(1)}, u32[]{:S(2)}, u32[]{:S(2)}) %collective-permute-start.2) | collective-permute-done | bytes 77856 | tf_op jit(solution)/shard_map/ppermute | solution.py:328
  13.5 6.2 %advance.1 = (f32[4168,128]{1,0:T(8,128)S(1)}, f32[32,128]{1,0:T(8,128)S(1)}) custom-call(f32[4,1024,128]{2,1,0:T(8,128)} %x_hbm.1, s32[4,1024]{1,0:T(4,128)} %keys_hbm.1, s32[1,4]{1,0:T(1,128)} %bitcast.36, f32[152,128]{1,0:T(8,128)S(1)} %get-tuple-element.17.b0, f32[152,128]{1,0:T(8,128)S(1)} %collective-permute-done.b1, ...), custom_call_target="tpu_custom_call" | custom-call | tf_op jit(solution)/shard_map/advance/pallas_call | solution.py:290
  19.7 0.1 collective-permute-start.3
  19.8 5.6 %table_own.1.part_ref = f32[4096,128]{1,0:T(8,128)S(1)} custom-call(f32[4168,128]{1,0:T(8,128)S(1)} %get-tuple-element.21.own_ref), custom_call_target="tpu_custom_call" | custom-call | tf_op jit(solution)/shard_map/table_own/pallas_call | solution.py:290
  25.5 0.0 collective-permute-done.3.other_ref
  25.5 2.1 %table_far.1 = (f32[516,128]{1,0:T(8,128)S(1)}, f32[516,128]{1,0:T(8,128)S(1)}) custom-call(f32[4168,128]{1,0:T(8,128)S(1)} %collective-permute-done.3.other_ref, f32[4096,128]{1,0:T(8,128)S(1)} %table_own.1.part_ref, f32[32,128]{1,0:T(8,128)S(1)} %get-tuple-element.22.count_ref), custom_call_target="tpu_custom_call" | custom-call | tf_op jit(solution)/shard_map/table_far/pallas_call | solution.py:290
  27.5 1.1 %collective-permute-start.6 = (f32[516,128]{1,0:T(8,128)S(1)}, f32[516,128]{1,0:T(8,128)S(1)}, u32[]{:S(2)}, u32[]{:S(2)}) collective-permute-start(f32[516,128]{1,0:T(8,128)S(1)} %get-tuple-element.26), channel_id=1, source_target_pairs={{0,4},{1,5},{2,6},{3,7},{4,0},{5,1},{6,2},{7,3},{8,12},{9,13},{10,... | collective-permute-start | bytes 792584 | tf_op jit(solution)/shard_map/ppermute | solution.py:377
  28.6 4.5 %collective-permute-start.4 = (f32[516,128]{1,0:T(8,128)S(1)}, f32[516,128]{1,0:T(8,128)S(1)}, u32[]{:S(2)}, u32[]{:S(2)}) collective-permute-start(f32[516,128]{1,0:T(8,128)S(1)} %get-tuple-element.24), channel_id=1, source_target_pairs={{0,2},{1,3},{2,0},{3,1},{4,6},{5,7},{6,4},{7,5},{8,10},{9,11},{10,... | collective-permute-start | bytes 792584 | tf_op jit(solution)/shard_map/ppermute | solution.py:377
  33.1 2.1 %table_near.1 = (f32[516,128]{1,0:T(8,128)S(1)}, f32[516,128]{1,0:T(8,128)S(1)}) custom-call(f32[4168,128]{1,0:T(8,128)S(1)} %collective-permute-done.3.other_ref, f32[4096,128]{1,0:T(8,128)S(1)} %table_own.1.part_ref, f32[32,128]{1,0:T(8,128)S(1)} %get-tuple-element.22.count_ref), custom_call_target="tpu_custom_call" | custom-call | tf_op jit(solution)/shard_map/table_near/pallas_call | solution.py:290
  35.2 0.1 collective-permute-start.12
  35.2 0.5 collective-permute-start.10
  35.8 2.1 %keep_far.1 = (f32[516,128]{1,0:T(8,128)S(1)}, f32[516,128]{1,0:T(8,128)S(1)}) custom-call(f32[4168,128]{1,0:T(8,128)S(1)} %collective-permute-done.3.other_ref, f32[4096,128]{1,0:T(8,128)S(1)} %table_own.1.part_ref, f32[32,128]{1,0:T(8,128)S(1)} %get-tuple-element.22.count_ref), custom_call_target="tpu_custom_call" | custom-call | tf_op jit(solution)/shard_map/keep_far/pallas_call | solution.py:290
  37.9 0.0 collective-permute-done.6
  37.9 2.4 %collective-permute-done.4 = f32[516,128]{1,0:T(8,128)S(1)} collective-permute-done((f32[516,128]{1,0:T(8,128)S(1)}, f32[516,128]{1,0:T(8,128)S(1)}, u32[]{:S(2)}, u32[]{:S(2)}) %collective-permute-start.4) | collective-permute-done | bytes 264224 | tf_op jit(solution)/shard_map/ppermute | solution.py:377
  40.4 0.1 collective-permute-start.5
  40.6 2.0 %collective-permute-start.7 = (f32[258,128]{1,0:T(8,128)S(1)}, f32[258,128]{1,0:T(8,128)S(1)}, u32[]{:S(2)}, u32[]{:S(2)}) collective-permute-start(f32[258,128]{1,0:T(8,128)S(1)} %get-tuple-element.43), channel_id=1, source_target_pairs={{0,2},{1,3},{2,0},{3,1},{4,6},{5,7},{6,4},{7,5},{8,10},{9,11},{10,... | collective-permute-start | bytes 396296 | tf_op jit(solution)/shard_map/ppermute | solution.py:377
  42.6 2.1 %keep_near.1 = (f32[516,128]{1,0:T(8,128)S(1)}, f32[516,128]{1,0:T(8,128)S(1)}) custom-call(f32[4168,128]{1,0:T(8,128)S(1)} %collective-permute-done.3.other_ref, f32[4096,128]{1,0:T(8,128)S(1)} %table_own.1.part_ref, f32[32,128]{1,0:T(8,128)S(1)} %get-tuple-element.22.count_ref), custom_call_target="tpu_custom_call" | custom-call | tf_op jit(solution)/shard_map/keep_near/pallas_call | solution.py:290
  44.7 0.0 collective-permute-done.12
  44.8 1.3 %collective-permute-done.10 = f32[516,128]{1,0:T(8,128)S(1)} collective-permute-done((f32[516,128]{1,0:T(8,128)S(1)}, f32[516,128]{1,0:T(8,128)S(1)}, u32[]{:S(2)}, u32[]{:S(2)}) %collective-permute-start.10) | collective-permute-done | bytes 264224 | tf_op jit(solution)/shard_map/ppermute | solution.py:377
  46.1 2.1 %collective-permute-start.13 = (f32[258,128]{1,0:T(8,128)S(1)}, f32[258,128]{1,0:T(8,128)S(1)}, u32[]{:S(2)}, u32[]{:S(2)}) collective-permute-start(f32[258,128]{1,0:T(8,128)S(1)} %pad_maximum_fusion.5), channel_id=1, source_target_pairs={{0,2},{1,3},{2,0},{3,1},{4,6},{5,7},{6,4},{7,5},{8,10},{9,11},{10,... | collective-permute-start | bytes 396296 | tf_op jit(solution)/shard_map/ppermute | solution.py:377
  48.2 0.2 collective-permute-start.11
  48.4 0.0 collective-permute-done.5
  48.4 0.5 collective-permute-done.7
  49.1 0.3 collective-permute-start.9
  49.4 2.1 %collective-permute-start.8 = (f32[258,128]{1,0:T(8,128)S(1)}, f32[258,128]{1,0:T(8,128)S(1)}, u32[]{:S(2)}, u32[]{:S(2)}) collective-permute-start(f32[258,128]{1,0:T(8,128)S(1)} %pad_maximum_fusion.2), channel_id=1, source_target_pairs={{0,16},{1,17},{2,18},{3,19},{4,20},{5,21},{6,22},{7,23},{8,24},{9,... | collective-permute-start | bytes 396296 | tf_op jit(solution)/shard_map/ppermute | solution.py:407
  51.5 0.0 collective-permute-done.13
  51.5 1.8 %collective-permute-done.11 = f32[258,128]{1,0:T(8,128)S(1)} collective-permute-done((f32[258,128]{1,0:T(8,128)S(1)}, f32[258,128]{1,0:T(8,128)S(1)}, u32[]{:S(2)}, u32[]{:S(2)}) %collective-permute-start.11) | collective-permute-done | bytes 132128 | tf_op jit(solution)/shard_map/ppermute | solution.py:377
  53.4 0.4 collective-permute-start.14
  53.8 3.6 %collective-permute-done.9 = f32[258,128]{1,0:T(8,128)S(1)} collective-permute-done((f32[258,128]{1,0:T(8,128)S(1)}, f32[258,128]{1,0:T(8,128)S(1)}, u32[]{:S(2)}, u32[]{:S(2)}) %collective-permute-start.9) | collective-permute-done | bytes 132128 | tf_op jit(solution)/shard_map/ppermute | solution.py:407
  57.4 5.4 %collective-permute-done.8 = f32[258,128]{1,0:T(8,128)S(1)} collective-permute-done((f32[258,128]{1,0:T(8,128)S(1)}, f32[258,128]{1,0:T(8,128)S(1)}, u32[]{:S(2)}, u32[]{:S(2)}) %collective-permute-start.8) | collective-permute-done | bytes 132128 | tf_op jit(solution)/shard_map/ppermute | solution.py:407
  62.7 0.0 collective-permute-done.14
  62.8 0.6 broadcast_maximum_fusion
  63.3 0.8 %slice_divide_fusion = f32[256,128]{1,0:T(8,128)} fusion(f32[258,128]{1,0:T(8,128)S(1)} %fusion, f32[256]{0:T(256)S(1)} %get-tuple-element.32), kind=kLoop, calls=%fused_computation.15 | loop fusion | flops 32768 | bytes 263168 | tf_op jit(solution)/shard_map/div | solution.py:410
  (31 shorter events, 0.5 us)
Async XLA Ops:
  1.5 5.7 %collective-permute-start = (f32[152,128]{1,0:T(8,128)S(1)}, f32[152,128]{1,0:T(8,128)S(1)}, u32[]{:S(2)}, u32[]{:S(2)}) collective-permute-start(f32[152,128]{1,0:T(8,128)S(1)} %get-tuple-element.18), channel_id=1, source_target_pairs={{0,8},{1,9},{2,10},{3,11},{4,12},{5,13},{6,14},{7,15},{8,0},{9,1},... | collective-permute-start | bytes 233480 | tf_op jit(solution)/shard_map/ppermute | solution.py:328
  4.7 8.1 %collective-permute-start.1 = (f32[152,128]{1,0:T(8,128)S(1)}, f32[152,128]{1,0:T(8,128)S(1)}, u32[]{:S(2)}, u32[]{:S(2)}) collective-permute-start(f32[152,128]{1,0:T(8,128)S(1)} %get-tuple-element.19), channel_id=1, source_target_pairs={{0,16},{1,17},{2,18},{3,19},{4,20},{5,21},{6,22},{7,23},{8,24},{9,... | collective-permute-start | bytes 233480 | tf_op jit(solution)/shard_map/ppermute | solution.py:328
  7.2 6.3 %collective-permute-start.2 = (f32[152,128]{1,0:T(8,128)S(1)}, f32[152,128]{1,0:T(8,128)S(1)}, u32[]{:S(2)}, u32[]{:S(2)}) collective-permute-start(f32[152,128]{1,0:T(8,128)S(1)} %get-tuple-element.20), channel_id=1, source_target_pairs={{0,24},{1,25},{2,26},{3,27},{4,28},{5,29},{6,30},{7,31},{8,16},{9,... | collective-permute-start | bytes 233480 | tf_op jit(solution)/shard_map/ppermute | solution.py:328
  19.7 5.7 %collective-permute-start.3 = (f32[4168,128]{1,0:T(8,128)S(1)}, f32[4168,128]{1,0:T(8,128)S(1)}, u32[]{:S(2)}, u32[]{:S(2)}) collective-permute-start(f32[4168,128]{1,0:T(8,128)S(1)} %get-tuple-element.21.own_ref), channel_id=1, source_target_pairs={{0,1},{1,0},{2,3},{3,2},{4,5},{5,4},{6,7},{7,6},{8,9},{9,8},{10,11... | collective-permute-start | bytes 6402056 | tf_op jit(solution)/shard_map/ppermute | solution.py:353
  27.5 10.3 %collective-permute-start.6 = (f32[516,128]{1,0:T(8,128)S(1)}, f32[516,128]{1,0:T(8,128)S(1)}, u32[]{:S(2)}, u32[]{:S(2)}) collective-permute-start(f32[516,128]{1,0:T(8,128)S(1)} %get-tuple-element.26), channel_id=1, source_target_pairs={{0,4},{1,5},{2,6},{3,7},{4,0},{5,1},{6,2},{7,3},{8,12},{9,13},{10,... | collective-permute-start | bytes 792584 | tf_op jit(solution)/shard_map/ppermute | solution.py:377
  28.6 11.7 %collective-permute-start.4 = (f32[516,128]{1,0:T(8,128)S(1)}, f32[516,128]{1,0:T(8,128)S(1)}, u32[]{:S(2)}, u32[]{:S(2)}) collective-permute-start(f32[516,128]{1,0:T(8,128)S(1)} %get-tuple-element.24), channel_id=1, source_target_pairs={{0,2},{1,3},{2,0},{3,1},{4,6},{5,7},{6,4},{7,5},{8,10},{9,11},{10,... | collective-permute-start | bytes 792584 | tf_op jit(solution)/shard_map/ppermute | solution.py:377
  35.2 9.5 %collective-permute-start.12 = (f32[516,128]{1,0:T(8,128)S(1)}, f32[516,128]{1,0:T(8,128)S(1)}, u32[]{:S(2)}, u32[]{:S(2)}) collective-permute-start(f32[516,128]{1,0:T(8,128)S(1)} %get-tuple-element.31), channel_id=1, source_target_pairs={{0,4},{1,5},{2,6},{3,7},{4,0},{5,1},{6,2},{7,3},{8,12},{9,13},{10,... | collective-permute-start | bytes 792584 | tf_op jit(solution)/shard_map/ppermute | solution.py:377
  35.2 10.8 %collective-permute-start.10 = (f32[516,128]{1,0:T(8,128)S(1)}, f32[516,128]{1,0:T(8,128)S(1)}, u32[]{:S(2)}, u32[]{:S(2)}) collective-permute-start(f32[516,128]{1,0:T(8,128)S(1)} %get-tuple-element.29), channel_id=1, source_target_pairs={{0,2},{1,3},{2,0},{3,1},{4,6},{5,7},{6,4},{7,5},{8,10},{9,11},{10,... | collective-permute-start | bytes 792584 | tf_op jit(solution)/shard_map/ppermute | solution.py:377
  40.4 7.9 %collective-permute-start.5 = (f32[258,128]{1,0:T(8,128)S(1)}, f32[258,128]{1,0:T(8,128)S(1)}, u32[]{:S(2)}, u32[]{:S(2)}) collective-permute-start(f32[258,128]{1,0:T(8,128)S(1)} %get-tuple-element.42), channel_id=1, source_target_pairs={{0,4},{1,5},{2,6},{3,7},{4,0},{5,1},{6,2},{7,3},{8,12},{9,13},{10,... | collective-permute-start | bytes 396296 | tf_op jit(solution)/shard_map/ppermute | solution.py:377
  40.6 8.4 %collective-permute-start.7 = (f32[258,128]{1,0:T(8,128)S(1)}, f32[258,128]{1,0:T(8,128)S(1)}, u32[]{:S(2)}, u32[]{:S(2)}) collective-permute-start(f32[258,128]{1,0:T(8,128)S(1)} %get-tuple-element.43), channel_id=1, source_target_pairs={{0,2},{1,3},{2,0},{3,1},{4,6},{5,7},{6,4},{7,5},{8,10},{9,11},{10,... | collective-permute-start | bytes 396296 | tf_op jit(solution)/shard_map/ppermute | solution.py:377
  46.1 5.4 %collective-permute-start.13 = (f32[258,128]{1,0:T(8,128)S(1)}, f32[258,128]{1,0:T(8,128)S(1)}, u32[]{:S(2)}, u32[]{:S(2)}) collective-permute-start(f32[258,128]{1,0:T(8,128)S(1)} %pad_maximum_fusion.5), channel_id=1, source_target_pairs={{0,2},{1,3},{2,0},{3,1},{4,6},{5,7},{6,4},{7,5},{8,10},{9,11},{10,... | collective-permute-start | bytes 396296 | tf_op jit(solution)/shard_map/ppermute | solution.py:377
  48.2 5.1 %collective-permute-start.11 = (f32[258,128]{1,0:T(8,128)S(1)}, f32[258,128]{1,0:T(8,128)S(1)}, u32[]{:S(2)}, u32[]{:S(2)}) collective-permute-start(f32[258,128]{1,0:T(8,128)S(1)} %pad_maximum_fusion.4), channel_id=1, source_target_pairs={{0,4},{1,5},{2,6},{3,7},{4,0},{5,1},{6,2},{7,3},{8,12},{9,13},{10,... | collective-permute-start | bytes 396296 | tf_op jit(solution)/shard_map/ppermute | solution.py:377
  49.1 8.3 %collective-permute-start.9 = (f32[258,128]{1,0:T(8,128)S(1)}, f32[258,128]{1,0:T(8,128)S(1)}, u32[]{:S(2)}, u32[]{:S(2)}) collective-permute-start(f32[258,128]{1,0:T(8,128)S(1)} %pad_maximum_fusion.3), channel_id=1, source_target_pairs={{0,24},{1,25},{2,26},{3,27},{4,28},{5,29},{6,30},{7,31},{8,16},{9,... | collective-permute-start | bytes 396296 | tf_op jit(solution)/shard_map/ppermute | solution.py:407
  49.4 13.3 %collective-permute-start.8 = (f32[258,128]{1,0:T(8,128)S(1)}, f32[258,128]{1,0:T(8,128)S(1)}, u32[]{:S(2)}, u32[]{:S(2)}) collective-permute-start(f32[258,128]{1,0:T(8,128)S(1)} %pad_maximum_fusion.2), channel_id=1, source_target_pairs={{0,16},{1,17},{2,18},{3,19},{4,20},{5,21},{6,22},{7,23},{8,24},{9,... | collective-permute-start | bytes 396296 | tf_op jit(solution)/shard_map/ppermute | solution.py:407
  53.4 9.3 %collective-permute-start.14 = (f32[258,128]{1,0:T(8,128)S(1)}, f32[258,128]{1,0:T(8,128)S(1)}, u32[]{:S(2)}, u32[]{:S(2)}) collective-permute-start(f32[258,128]{1,0:T(8,128)S(1)} %pad_maximum_fusion.6), channel_id=1, source_target_pairs={{0,8},{1,9},{2,10},{3,11},{4,12},{5,13},{6,14},{7,15},{8,0},{9,1},... | collective-permute-start | bytes 396296 | tf_op jit(solution)/shard_map/ppermute | solution.py:407

commit v4 on v3

--- a/solution.py
+++ b/solution.py
@@ -5,6 +5,7 @@
 from jax.experimental import pallas as pl
 from jax.experimental.pallas import tpu as pltpu
 from jax.sharding import PartitionSpec as P
+
 
 KEYS = 8192
 STEP = 512
@@ -33,7 +34,6 @@
         self.owned = KEYS // (self.sections * self.rows)
         self.color = self.owned // 2
         self.half = KEYS // 2
-        self.inner = self.sections // 2
         self.chunk = self.half // 4
         bits = list(range(self.planes))
         turn = self.planes // 2
@@ -64,9 +64,10 @@
     index = jnp.where(color == 0, inner[0], inner[1])
     count = 1 << (plan.planes - 1)
     kept = index >> (plan.planes - 1)
-    near = 1 - zrel // plan.inner
-    slot = ((near * 2 + kept) * 2 + color) * count + (index & (count - 1))
-    return (slot * plan.inner + (zrel & (plan.inner - 1))) * plan.color + low + core * plan.half
+    index = index & (count - 1)
+    far = ((color * count + index) * 2 + (zrel & 1)) * plan.color + 2 * plan.chunk * kept
+    near = ((kept * 2 + color) * count + index) * plan.color + jnp.where(zrel == 1, plan.chunk, 3 * plan.chunk)
+    return jnp.where(zrel >= 2, far, near) + low + core * plan.half
 
 
 def fetch(pairs, sems):
@@ -92,11 +93,11 @@
         buffer[:width, :] = weight_ref[0]
         buffer[width:, :] = jnp.zeros((buffer.shape[0] - width, width), F32)
         words = predicates_ref[0, pl.ds((z ^ k) * batches, batches), :]
+        words = jnp.concatenate([words[m : m + 1] for m in range(batches)], axis=1)
         for b in range(4):
-            at = width + b * batches
-            buffer[at : at + batches, :words_in_batch] = ((words >> (8 * b)) & 255).astype(F32)
-        at = width + 4 * batches
-        buffer[at : at + 1, :] = bias_ref[...]
+            at = width + b
+            buffer[at : at + 1, : batches * words_in_batch] = ((words >> (8 * b)) & 255).astype(F32)
+        buffer[width + 4 : width + 5, :] = bias_ref[...]
 
 
 def advance_kernel(
@@ -138,9 +139,11 @@
         weight[level, width:, :width] = high
         weight[level, :width, width:] = low
         weight[level, width:, width:] = jnp.zeros_like(low)
-        bytes_[level] = buffer[width : width + 4 * batches, :]
-        bias[level, :1, :] = buffer[width + 4 * batches : width + 4 * batches + 1, :]
-    words = bytes_[...].reshape(SECTIONS * 4 * batches, LANES).astype(BF16)
+        bytes_[level] = buffer[width : width + 8, :]
+        bias[level, :1, :] = buffer[width + 4 : width + 5, :]
+    words = bytes_[...].reshape(SECTIONS * 8, LANES)
+    turned = [pltpu.roll(words, (LANES - m * (block // 32)) % LANES, axis=1) for m in range(batches)]
+    words = jnp.concatenate(turned, axis=0).astype(BF16)
     lane = iota((1, block), 1)
     spread = (iota((LANES, block), 0) == (iota((LANES, block), 1) >> 5)).astype(F32).astype(BF16)
     found = jnp.dot(words, spread, preferred_element_type=F32).astype(jnp.int32)
@@ -152,10 +155,10 @@
     for m in range(batches):
         flags = []
         for s in range(SECTIONS):
-            at = s * 4 * batches + m
+            at = (m * SECTIONS + s) * 8
             byte = found[at : at + 1]
             for b in range(1, 4):
-                byte = jnp.where(which == b, found[at + b * batches : at + b * batches + 1], byte)
+                byte = jnp.where(which == b, found[at + b : at + b + 1], byte)
             flags.append((byte >> (lane & 7)) & 1)
         depth = flags[-1]
         for flag in flags[-2::-1]:
@@ -245,7 +248,6 @@
     base = (core * plan.half + first).astype(F32)
     used = jnp.max(source[source.shape[0] - 8 :, :]).astype(jnp.int32)
     tile = min(256, slots)
-    sums[:slots, :] = jnp.zeros((slots, sums.shape[1]), F32)
 
     def body(step, _):
         at = pl.multiple_of(step * STEP, STEP)
@@ -263,37 +265,37 @@
 
 def own_kernel(plan, rows, own_ref, out_ref, sums):
     width = out_ref.shape[1]
-    add_products(plan, rows, own_ref, 0, plan.half, sums)
+    sums[...] = jnp.zeros_like(sums)
+    add_products(plan, rows, own_ref, 0, sums.shape[0], sums)
     out_ref[...] = sums[:, :width] + sums[:, width:]
 
 
-def other_kernel(plan, rows, first, other_ref, part_ref, count_ref, *refs):
+def table_kernel(plan, rows, start, early, other_ref, mine_ref, count_ref, *refs):
     *outs, sums = refs
-    width = part_ref.shape[1]
-    size = plan.chunk // 2
+    width = mine_ref.shape[1]
+    size = plan.chunk // len(outs)
     lines = size // LANES
     at = rows + rows // LANES
-    for chunk, start in enumerate(first):
-        add_products(plan, rows, other_ref, start, plan.chunk, sums)
-        for color in range(2):
-            out = outs[2 * chunk + color]
-            low = color * size
-            slot = start + low
-            out[:size, :] = (
-                sums[low : low + size, :width] + sums[low : low + size, width:] + part_ref[slot : slot + size, :]
-            )
-            line = slot // LANES
-            out[size:, :] = count_ref[line : line + lines, :] + other_ref[at + line : at + line + lines, :]
-
-
-def call(kernel, out_shape, operands, scratch=(), name=None, hbm=(), limit=24):
+    sums[...] = jnp.zeros_like(sums)
+    if not early:
+        add_products(plan, rows, mine_ref, start, plan.chunk, sums)
+    add_products(plan, rows, other_ref, start, plan.chunk, sums)
+    for i, out in enumerate(outs):
+        low = i * size
+        slot = start + low
+        total = sums[low : low + size, :width] + sums[low : low + size, width:]
+        out[:size, :] = total + mine_ref[slot : slot + size, :] if early else total
+        line = slot // LANES
+        out[size:, :] = count_ref[line : line + lines, :] + other_ref[at + line : at + line + lines, :]
+
+
+def call(kernel, out_shape, operands, scratch=(), hbm=(), limit=24):
     return pl.pallas_call(
         kernel,
         out_shape=out_shape,
         in_specs=[HBM if i in hbm else VMEM for i in range(len(operands))],
         out_specs=jax.tree.map(lambda _: VMEM, out_shape),
         scratch_shapes=list(scratch),
-        name=name,
         compiler_params=pltpu.CompilerParams(vmem_limit_bytes=limit << 20),
     )(*(pltpu.with_memory_space_constraint(o, pltpu.HBM) if i in hbm else o for i, o in enumerate(operands)))
 
@@ -311,7 +313,7 @@
     axes = ("section", "rows")
     packed = call(
         functools.partial(pack_kernel, plan, batches),
-        (shape((width + 4 * batches + 8) // 8 * 8, width),) * plan.sections,
+        (shape(width + 8, width),) * plan.sections,
         (predicates, section_weight, section_bias),
         scratch=[
             pltpu.VMEM(predicates.shape, jnp.int32),
@@ -319,7 +321,6 @@
             pltpu.VMEM(section_bias.shape, F32),
             pltpu.SemaphoreType.DMA((3,)),
         ],
-        name="pack",
         hbm=(0, 1, 2),
         limit=4,
     )
@@ -340,79 +341,86 @@
             pltpu.VMEM((1, batches), jnp.int32),
             pltpu.VMEM((SECTIONS, 2 * width, 2 * width), BF16),
             pltpu.VMEM((SECTIONS, 8, width), F32),
-            pltpu.VMEM((SECTIONS, 4 * batches, LANES), F32),
+            pltpu.VMEM((SECTIONS, 8, LANES), F32),
             pltpu.VMEM((2, rows // tile, tile), F32),
             pltpu.VMEM((rows + STEP, width), F32),
             pltpu.VMEM((lines + STEP // LANES, 8, LANES), F32),
             pltpu.VMEM((2 * tables, LANES), F32),
             pltpu.SemaphoreType.DMA((batches + 2,)),
         ],
-        name="advance",
         hbm=(0, 1, 2),
     )
     other = lax.ppermute(own, axes, plan.perm(1, 0))
     part = call(
         functools.partial(own_kernel, plan, rows),
-        shape(plan.half, width),
+        shape(2 * plan.chunk, width),
         (own,),
-        scratch=[pltpu.VMEM((plan.half, 2 * width), F32)],
-        name="table_own",
-    )
+        scratch=[pltpu.VMEM((2 * plan.chunk, 2 * width), F32)],
+    )
+
+    def table(chunk, messages, after=()):
+        size = plan.chunk // messages
+        early = chunk < 2
+        operand, _ = lax.optimization_barrier((count, tuple(after)))
+        return call(
+            functools.partial(table_kernel, plan, rows, chunk * plan.chunk, early),
+            (shape(size + size // LANES, width),) * messages,
+            (other, part if early else own, operand),
+            scratch=[pltpu.VMEM((plan.chunk, 2 * width), F32)],
+        )
+
+    def open_message(message, size):
+        return message[:size], message[size:].reshape(-1)[:size]
+
+    def close_message(sums, counts):
+        return jnp.concatenate([sums, lines_of(counts)], axis=0)
+
+    def send(message, row_xor, section_xor):
+        return lax.ppermute(message, axes, plan.perm(row_xor, section_xor))
+
+    def swap(messages, step):
+        return [send(m, 2 << order[step], 0) for m, order in zip(messages, plan.orders)]
+
+    def halve(states, step):
+        cut = states[0][0].shape[0] // 2
+        packed = [close_message(sums[:cut], counts[:cut]) for sums, counts in states]
+        moved = [open_message(m, cut) for m in swap(packed, step)]
+        return packed, [(s[cut:] + a, c[cut:] + b) for (s, c), (a, b) in zip(states, moved)]
+
     size = plan.chunk // 2
-    message = shape(size + size // LANES, width)
-
-    def tables_of(name, *chunks, after=()):
-        operand, _ = lax.optimization_barrier((part, tuple(after)))
-        outs = call(
-            functools.partial(other_kernel, plan, rows, [c * plan.chunk for c in chunks]),
-            (message,) * (2 * len(chunks)),
-            (other, operand, count),
-            scratch=[pltpu.VMEM((plan.chunk, 2 * width), F32)],
-            name=name,
-        )
-        return [outs[2 * i : 2 * i + 2] for i in range(len(chunks))]
-
-    def halve(messages, step):
-        return [
-            lax.ppermute(m, axes, plan.perm(2 << order[step], 0)) for m, order in zip(messages, plan.orders)
-        ]
-
-    got = []
-    for near in range(2):
-        (sent,) = tables_of("table_far" if near == 0 else "table_near", 2 * near)
-        got.append(halve(sent, 0))
-    finals, sent = [], []
-    for near in range(2):
-        (kept,) = tables_of("keep_far" if near == 0 else "keep_near", 2 * near + 1, after=sent)
-        states = []
-        for color in range(2):
-            total = kept[color] + got[near][color]
-            states.append((total[:size], total[size:].reshape(-1)))
-        sent = []
-        for step in range(1, plan.planes):
-            cut = states[0][0].shape[0] // 2
-            packed = [jnp.concatenate([sums[:cut], lines_of(counts[:cut])], axis=0) for sums, counts in states]
-            sent = sent or packed
-            states = [
-                (sums[cut:] + m[:cut], counts[cut:] + m[cut:].reshape(-1)[:cut])
-                for (sums, counts), m in zip(states, halve(packed, step))
-            ]
-        sums = jnp.stack([s.reshape(plan.inner, plan.color, width) for s, _ in states], axis=1)
-        counts = jnp.stack([c.reshape(plan.inner, plan.color) for _, c in states], axis=1)
-        sums = sums.reshape(plan.inner, plan.owned, width)
-        counts = counts.reshape(plan.inner, plan.owned)
-        for i in range(plan.inner):
-            k = (1 - near) * plan.inner + i
-            packed = jnp.concatenate([sums[i], lines_of(counts[i])], axis=0)
-            finals.append(lax.ppermute(packed, axes, plan.perm(0, k)) if k else packed)
+    got = swap(table(0, 2), 0)
+    sent = table(1, 1)
+    near = send(sent[0], 0, 1)
+    far = [open_message(k + g, size) for k, g in zip(table(2, 2, after=sent), got)]
+    gate = ()
+    for step in range(1, plan.planes):
+        packed, far = halve(far, step)
+        gate = gate or packed
+    sums = jnp.stack([s.reshape(2, plan.color, width) for s, _ in far], axis=1).reshape(2, plan.owned, width)
+    counts = jnp.stack([c.reshape(2, plan.color) for _, c in far], axis=1).reshape(2, plan.owned)
+    finals = [send(close_message(sums[i], counts[i]), 0, 2 + i) for i in range(2)]
+    (kept,) = table(3, 1, after=gate)
+    near = kept + near
+    sums, counts = open_message(near, plan.chunk)
+    sums = sums.reshape(2, 2, size // 2, width)
+    counts = counts.reshape(2, 2, size // 2)
+    states = [(sums[:, c].reshape(size, width), counts[:, c].reshape(size)) for c in range(2)]
+    for step in range(plan.planes):
+        _, states = halve(states, step)
+    finals.append(close_message(jnp.concatenate([s for s, _ in states]), jnp.concatenate([c for _, c in states])))
     total = functools.reduce(jnp.add, finals)
     number = total[plan.owned :].reshape(-1)[: plan.owned]
     return total[: plan.owned] / jnp.maximum(number, 1.0)[:, None], number
 
 
 def solution(mesh):
+    plan = Plan(mesh)
+
+    def body(*args):
+        return shards(plan, *args)
+
     return jax.shard_map(
-        functools.partial(shards, Plan(mesh)),
+        body,
         mesh=mesh,
         in_specs=(
             P("section", "rows", None),

time: 64.1 us -> 69.1 us (1.078)
  Pallas kernels: 21 us -> 24.8 us
  starting transfers between devices: 19.2 us -> 22.1 us
  waiting for transfers between devices: 21.2 us -> 19.1 us
    pallas_call x7, Pallas kernels: 21 us -> 24.8 us  [call(): pl.pallas_call(kernel, out_shape=out_shape, in_specs=[HBM if i in hbm els...]
    ppermute x11, starting transfers between devices: 13.4 us -> 16.3 us  [send(): return lax.ppermute(message, axes, plan.perm(row_xor, section_xor))]
    ppermute x11, waiting for transfers between devices: 14.9 us -> 12.7 us  [send(): return lax.ppermute(message, axes, plan.perm(row_xor, section_xor))]
  transfers between devices with their start and end apart: 15 -> 15, of which waited for: 8 -> 8; matrix products, arithmetic and copies ran while one was open for 1% -> 1% of each run, Pallas kernels for 18% -> 22%
where the time goes in v4:
time: 69.1 us; the launch traced here: 68.9 us
  Pallas kernels  24.8 us (36%)
  starting transfers between devices  22.1 us (32%)
  waiting for transfers between devices  19.1 us (28%)
  other arithmetic  1.73 us (3%)
  between operations  0.95 us (1%)
    pallas_call x7, Pallas kernels, call(): pl.pallas_call(kernel, out_shape=out_shape, in_specs=[HBM if i in hbm els...  24.8 us
    ppermute x11, starting transfers between devices, send(): return lax.ppermute(message, axes, plan.perm(row_xor, section_xor))  16.3 us
    ppermute x11, waiting for transfers between devices, send(): return lax.ppermute(message, axes, plan.perm(row_xor, section_xor))  12.7 us
    ppermute x3, waiting for transfers between devices, shards(): buffers.append(lax.ppermute(packed[k], axes, plan.perm(0, k)))  6.2 us
    ppermute x3, starting transfers between devices, shards(): buffers.append(lax.ppermute(packed[k], axes, plan.perm(0, k)))  5.71 us
  transfers between devices with their start and end apart: 15, of which 8 were waited for; matrix products, arithmetic and copies ran while one was open for 1% of the time, Pallas kernels for 22%

profile of v4, /device:TPU:0, one launch (start us, length us, event | category | flops | bytes accessed | tf_op | source)
XLA Modules:
  0.0 68.9 jit_solution(6328006365626006095)
XLA Ops:
  0.6 1.0 %shard_map.77 = (f32[136,128]{1,0:T(8,128)S(1)}, f32[136,128]{1,0:T(8,128)S(1)}, f32[136,128]{1,0:T(8,128)S(1)}, f32[136,128]{1,0:T(8,128)S(1)}) custom-call(s32[1,16,32]{2,1,0:T(8,128)} %predicates_hbm.1, f32[1,128,128]{2,1,0:T(8,128)} %weight_hbm.1, f32[1,128]{1,0:T(1,128)} %bias_hbm.1), custom_call_target="tpu_custom_call" | custom-call | tf_op jit(solution)/shard_map/pallas_call | solution.py:293
  1.6 3.1 %collective-permute-start = (f32[136,128]{1,0:T(8,128)S(1)}, f32[136,128]{1,0:T(8,128)S(1)}, u32[]{:S(2)}, u32[]{:S(2)}) collective-permute-start(f32[136,128]{1,0:T(8,128)S(1)} %get-tuple-element.15), channel_id=1, source_target_pairs={{0,8},{1,9},{2,10},{3,11},{4,12},{5,13},{6,14},{7,15},{8,0},{9,1},... | collective-permute-start | bytes 208904 | tf_op jit(solution)/shard_map/ppermute | solution.py:329
  4.7 2.6 %collective-permute-start.1 = (f32[136,128]{1,0:T(8,128)S(1)}, f32[136,128]{1,0:T(8,128)S(1)}, u32[]{:S(2)}, u32[]{:S(2)}) collective-permute-start(f32[136,128]{1,0:T(8,128)S(1)} %get-tuple-element.16), channel_id=1, source_target_pairs={{0,16},{1,17},{2,18},{3,19},{4,20},{5,21},{6,22},{7,23},{8,24},{9,... | collective-permute-start | bytes 208904 | tf_op jit(solution)/shard_map/ppermute | solution.py:329
  7.3 0.0 collective-permute-start.2
  7.3 0.0 collective-permute-done.b1
  7.3 4.9 %collective-permute-done.1.b2 = f32[136,128]{1,0:T(8,128)S(1)} collective-permute-done((f32[136,128]{1,0:T(8,128)S(1)}, f32[136,128]{1,0:T(8,128)S(1)}, u32[]{:S(2)}, u32[]{:S(2)}) %collective-permute-start.1) | collective-permute-done | bytes 69664 | tf_op jit(solution)/shard_map/ppermute | solution.py:329
  12.2 1.3 %collective-permute-done.2.b3 = f32[136,128]{1,0:T(8,128)S(1)} collective-permute-done((f32[136,128]{1,0:T(8,128)S(1)}, f32[136,128]{1,0:T(8,128)S(1)}, u32[]{:S(2)}, u32[]{:S(2)}) %collective-permute-start.2) | collective-permute-done | bytes 69664 | tf_op jit(solution)/shard_map/ppermute | solution.py:329
  13.5 6.9 %shard_map.78 = (f32[4168,128]{1,0:T(8,128)S(1)}, f32[32,128]{1,0:T(8,128)S(1)}) custom-call(f32[4,1024,128]{2,1,0:T(8,128)} %x_hbm.1, s32[4,1024]{1,0:T(4,128)} %keys_hbm.1, s32[1,4]{1,0:T(1,128)} %bitcast.65, f32[136,128]{1,0:T(8,128)S(1)} %get-tuple-element.14.b0, f32[136,128]{1,0:T(8,128)S(1)} %collective-permute-done.b1, ...), custom_call_target="tpu_custom_call" | custom-call | tf_op jit(solution)/shard_map/pallas_call | solution.py:293
  20.5 0.1 collective-permute-start.3
  20.5 3.9 %shard_map.79.mine_ref = f32[2048,128]{1,0:T(8,128)S(1)} custom-call(f32[4168,128]{1,0:T(8,128)S(1)} %get-tuple-element.18.own_ref.mine_ref), custom_call_target="tpu_custom_call" | custom-call | tf_op jit(solution)/shard_map/pallas_call | solution.py:293
  24.5 0.2 collective-permute-done.3.other_ref
  24.7 2.1 %shard_map.82 = (f32[516,128]{1,0:T(8,128)S(1)}, f32[516,128]{1,0:T(8,128)S(1)}) custom-call(f32[4168,128]{1,0:T(8,128)S(1)} %collective-permute-done.3.other_ref, f32[2048,128]{1,0:T(8,128)S(1)} %shard_map.79.mine_ref, f32[32,128]{1,0:T(8,128)S(1)} %get-tuple-element.25.count_ref), custom_call_target="tpu_custom_call" | custom-call | tf_op jit(solution)/shard_map/pallas_call | solution.py:293
  26.8 0.8 %collective-permute-start.6 = (f32[516,128]{1,0:T(8,128)S(1)}, f32[516,128]{1,0:T(8,128)S(1)}, u32[]{:S(2)}, u32[]{:S(2)}) collective-permute-start(f32[516,128]{1,0:T(8,128)S(1)} %get-tuple-element.24), channel_id=1, source_target_pairs={{0,4},{1,5},{2,6},{3,7},{4,0},{5,1},{6,2},{7,3},{8,12},{9,13},{10,... | collective-permute-start | bytes 792584 | tf_op jit(solution)/shard_map/ppermute | solution.py:379
  27.6 1.8 %collective-permute-start.4 = (f32[516,128]{1,0:T(8,128)S(1)}, f32[516,128]{1,0:T(8,128)S(1)}, u32[]{:S(2)}, u32[]{:S(2)}) collective-permute-start(f32[516,128]{1,0:T(8,128)S(1)} %get-tuple-element.22), channel_id=1, source_target_pairs={{0,2},{1,3},{2,0},{3,1},{4,6},{5,7},{6,4},{7,5},{8,10},{9,11},{10,... | collective-permute-start | bytes 792584 | tf_op jit(solution)/shard_map/ppermute | solution.py:379
  29.4 2.1 %shard_map.80 = f32[1032,128]{1,0:T(8,128)S(1)} custom-call(f32[4168,128]{1,0:T(8,128)S(1)} %collective-permute-done.3.other_ref, f32[2048,128]{1,0:T(8,128)S(1)} %shard_map.79.mine_ref, f32[32,128]{1,0:T(8,128)S(1)} %get-tuple-element.25.count_ref), custom_call_target="tpu_custom_call" | custom-call | tf_op jit(solution)/shard_map/pallas_call | solution.py:293
  31.5 4.5 %shard_map.81 = (f32[516,128]{1,0:T(8,128)S(1)}, f32[516,128]{1,0:T(8,128)S(1)}) custom-call(f32[4168,128]{1,0:T(8,128)S(1)} %collective-permute-done.3.other_ref, f32[4168,128]{1,0:T(8,128)S(1)} %get-tuple-element.18.own_ref.mine_ref, f32[32,128]{1,0:T(8,128)S(1)} %get-tuple-element.25.count_ref), custom_call_target="tpu_custom_call" | custom-call | tf_op jit(solution)/shard_map/pallas_call | solution.py:293
  35.9 0.0 collective-permute-done.6
  36.0 0.7 %collective-permute-done.4 = f32[516,128]{1,0:T(8,128)S(1)} collective-permute-done((f32[516,128]{1,0:T(8,128)S(1)}, f32[516,128]{1,0:T(8,128)S(1)}, u32[]{:S(2)}, u32[]{:S(2)}) %collective-permute-start.4) | collective-permute-done | bytes 264224 | tf_op jit(solution)/shard_map/ppermute | solution.py:379
  36.8 0.8 %collective-permute-start.5 = (f32[258,128]{1,0:T(8,128)S(1)}, f32[258,128]{1,0:T(8,128)S(1)}, u32[]{:S(2)}, u32[]{:S(2)}) collective-permute-start(f32[258,128]{1,0:T(8,128)S(1)} %get-tuple-element.40), channel_id=1, source_target_pairs={{0,4},{1,5},{2,6},{3,7},{4,0},{5,1},{6,2},{7,3},{8,12},{9,13},{10,... | collective-permute-start | bytes 396296 | tf_op jit(solution)/shard_map/ppermute | solution.py:379
  37.7 0.3 collective-permute-start.10
  38.0 1.9 %collective-permute-start.7 = (f32[258,128]{1,0:T(8,128)S(1)}, f32[258,128]{1,0:T(8,128)S(1)}, u32[]{:S(2)}, u32[]{:S(2)}) collective-permute-start(f32[258,128]{1,0:T(8,128)S(1)} %get-tuple-element.41), channel_id=1, source_target_pairs={{0,2},{1,3},{2,0},{3,1},{4,6},{5,7},{6,4},{7,5},{8,10},{9,11},{10,... | collective-permute-start | bytes 396296 | tf_op jit(solution)/shard_map/ppermute | solution.py:379
  39.9 4.4 %shard_map.83 = f32[1032,128]{1,0:T(8,128)S(1)} custom-call(f32[4168,128]{1,0:T(8,128)S(1)} %collective-permute-done.3.other_ref, f32[4168,128]{1,0:T(8,128)S(1)} %get-tuple-element.18.own_ref.mine_ref, f32[32,128]{1,0:T(8,128)S(1)} %get-tuple-element.25.count_ref), custom_call_target="tpu_custom_call" | custom-call | tf_op jit(solution)/shard_map/pallas_call | solution.py:293
  44.4 0.0 collective-permute-done.5
  44.4 0.0 collective-permute-done.7
  44.5 2.9 %collective-permute-start.9 = (f32[258,128]{1,0:T(8,128)S(1)}, f32[258,128]{1,0:T(8,128)S(1)}, u32[]{:S(2)}, u32[]{:S(2)}) collective-permute-start(f32[258,128]{1,0:T(8,128)S(1)} %pad_maximum_fusion.3), channel_id=1, source_target_pairs={{0,24},{1,25},{2,26},{3,27},{4,28},{5,29},{6,30},{7,31},{8,16},{9,... | collective-permute-start | bytes 396296 | tf_op jit(solution)/shard_map/ppermute | solution.py:379
  47.4 3.7 %collective-permute-done.10 = f32[1032,128]{1,0:T(8,128)S(1)} collective-permute-done((f32[1032,128]{1,0:T(8,128)S(1)}, f32[1032,128]{1,0:T(8,128)S(1)}, u32[]{:S(2)}, u32[]{:S(2)}) %collective-permute-start.10) | collective-permute-done | bytes 528416 | tf_op jit(solution)/shard_map/ppermute | solution.py:379
  51.1 0.1 add.68
  51.3 2.1 %collective-permute-start.13 = (f32[258,128]{1,0:T(8,128)S(1)}, f32[258,128]{1,0:T(8,128)S(1)}, u32[]{:S(2)}, u32[]{:S(2)}) collective-permute-start(f32[258,128]{1,0:T(8,128)S(1)} %pad_maximum_fusion.5), channel_id=1, source_target_pairs={{0,4},{1,5},{2,6},{3,7},{4,0},{5,1},{6,2},{7,3},{8,12},{9,13},{10,... | collective-permute-start | bytes 396296 | tf_op jit(solution)/shard_map/ppermute | solution.py:379
  53.4 3.2 %collective-permute-start.8 = (f32[258,128]{1,0:T(8,128)S(1)}, f32[258,128]{1,0:T(8,128)S(1)}, u32[]{:S(2)}, u32[]{:S(2)}) collective-permute-start(f32[258,128]{1,0:T(8,128)S(1)} %pad_maximum_fusion.2), channel_id=1, source_target_pairs={{0,16},{1,17},{2,18},{3,19},{4,20},{5,21},{6,22},{7,23},{8,24},{9,... | collective-permute-start | bytes 396296 | tf_op jit(solution)/shard_map/ppermute | solution.py:379
  56.7 0.5 collective-permute-start.11
  57.2 0.0 collective-permute-done.13
  57.2 4.9 %collective-permute-done.11 = f32[258,128]{1,0:T(8,128)S(1)} collective-permute-done((f32[258,128]{1,0:T(8,128)S(1)}, f32[258,128]{1,0:T(8,128)S(1)}, u32[]{:S(2)}, u32[]{:S(2)}) %collective-permute-start.11) | collective-permute-done | bytes 132128 | tf_op jit(solution)/shard_map/ppermute | solution.py:379
  62.2 1.0 %collective-permute-start.14 = (f32[129,128]{1,0:T(8,128)S(1)}, f32[129,128]{1,0:T(8,128)S(1)}, u32[]{:S(2)}, u32[]{:S(2)}) collective-permute-start(f32[129,128]{1,0:T(8,128)S(1)} %pad_maximum_fusion.8), channel_id=1, source_target_pairs={{0,2},{1,3},{2,0},{3,1},{4,6},{5,7},{6,4},{7,5},{8,10},{9,11},{10,... | collective-permute-start | bytes 198152 | tf_op jit(solution)/shard_map/ppermute | solution.py:379
  63.1 0.9 %collective-permute-start.12 = (f32[129,128]{1,0:T(8,128)S(1)}, f32[129,128]{1,0:T(8,128)S(1)}, u32[]{:S(2)}, u32[]{:S(2)}) collective-permute-start(f32[129,128]{1,0:T(8,128)S(1)} %pad_maximum_fusion.7), channel_id=1, source_target_pairs={{0,4},{1,5},{2,6},{3,7},{4,0},{5,1},{6,2},{7,3},{8,12},{9,13},{10,... | collective-permute-start | bytes 198152 | tf_op jit(solution)/shard_map/ppermute | solution.py:379
  64.0 2.5 %collective-permute-done.14 = f32[129,128]{1,0:T(8,128)S(1)} collective-permute-done((f32[129,128]{1,0:T(8,128)S(1)}, f32[129,128]{1,0:T(8,128)S(1)}, u32[]{:S(2)}, u32[]{:S(2)}) %collective-permute-start.14) | collective-permute-done | bytes 66080 | tf_op jit(solution)/shard_map/ppermute | solution.py:379
  66.6 0.9 %collective-permute-done.12 = f32[129,128]{1,0:T(8,128)S(1)} collective-permute-done((f32[129,128]{1,0:T(8,128)S(1)}, f32[129,128]{1,0:T(8,128)S(1)}, u32[]{:S(2)}, u32[]{:S(2)}) %collective-permute-start.12) | collective-permute-done | bytes 66080 | tf_op jit(solution)/shard_map/ppermute | solution.py:379
  67.5 0.0 collective-permute-done.9
  67.5 0.0 collective-permute-done.8
  67.5 0.6 broadcast_maximum_fusion
  68.1 0.8 %slice_divide_fusion = f32[256,128]{1,0:T(8,128)} fusion(f32[258,128]{1,0:T(8,128)S(1)} %maximum_add_fusion, f32[256]{0:T(256)S(1)} %get-tuple-element.26), kind=kLoop, calls=%fused_computation.10 | loop fusion | flops 32768 | bytes 263168 | tf_op jit(solution)/shard_map/div | solution.py:413
  (37 shorter events, 0.4 us)
Async XLA Ops:
  1.6 5.7 %collective-permute-start = (f32[136,128]{1,0:T(8,128)S(1)}, f32[136,128]{1,0:T(8,128)S(1)}, u32[]{:S(2)}, u32[]{:S(2)}) collective-permute-start(f32[136,128]{1,0:T(8,128)S(1)} %get-tuple-element.15), channel_id=1, source_target_pairs={{0,8},{1,9},{2,10},{3,11},{4,12},{5,13},{6,14},{7,15},{8,0},{9,1},... | collective-permute-start | bytes 208904 | tf_op jit(solution)/shard_map/ppermute | solution.py:329
  4.7 7.5 %collective-permute-start.1 = (f32[136,128]{1,0:T(8,128)S(1)}, f32[136,128]{1,0:T(8,128)S(1)}, u32[]{:S(2)}, u32[]{:S(2)}) collective-permute-start(f32[136,128]{1,0:T(8,128)S(1)} %get-tuple-element.16), channel_id=1, source_target_pairs={{0,16},{1,17},{2,18},{3,19},{4,20},{5,21},{6,22},{7,23},{8,24},{9,... | collective-permute-start | bytes 208904 | tf_op jit(solution)/shard_map/ppermute | solution.py:329
  7.3 6.2 %collective-permute-start.2 = (f32[136,128]{1,0:T(8,128)S(1)}, f32[136,128]{1,0:T(8,128)S(1)}, u32[]{:S(2)}, u32[]{:S(2)}) collective-permute-start(f32[136,128]{1,0:T(8,128)S(1)} %get-tuple-element.17), channel_id=1, source_target_pairs={{0,24},{1,25},{2,26},{3,27},{4,28},{5,29},{6,30},{7,31},{8,16},{9,... | collective-permute-start | bytes 208904 | tf_op jit(solution)/shard_map/ppermute | solution.py:329
  20.5 4.3 %collective-permute-start.3 = (f32[4168,128]{1,0:T(8,128)S(1)}, f32[4168,128]{1,0:T(8,128)S(1)}, u32[]{:S(2)}, u32[]{:S(2)}) collective-permute-start(f32[4168,128]{1,0:T(8,128)S(1)} %get-tuple-element.18.own_ref.mine_ref), channel_id=1, source_target_pairs={{0,1},{1,0},{2,3},{3,2},{4,5},{5,4},{6,7},{7,6},{8,9},{9,8},{10,11... | collective-permute-start | bytes 6402056 | tf_op jit(solution)/shard_map/ppermute | solution.py:353
  26.8 9.1 %collective-permute-start.6 = (f32[516,128]{1,0:T(8,128)S(1)}, f32[516,128]{1,0:T(8,128)S(1)}, u32[]{:S(2)}, u32[]{:S(2)}) collective-permute-start(f32[516,128]{1,0:T(8,128)S(1)} %get-tuple-element.24), channel_id=1, source_target_pairs={{0,4},{1,5},{2,6},{3,7},{4,0},{5,1},{6,2},{7,3},{8,12},{9,13},{10,... | collective-permute-start | bytes 792584 | tf_op jit(solution)/shard_map/ppermute | solution.py:379
  27.6 9.1 %collective-permute-start.4 = (f32[516,128]{1,0:T(8,128)S(1)}, f32[516,128]{1,0:T(8,128)S(1)}, u32[]{:S(2)}, u32[]{:S(2)}) collective-permute-start(f32[516,128]{1,0:T(8,128)S(1)} %get-tuple-element.22), channel_id=1, source_target_pairs={{0,2},{1,3},{2,0},{3,1},{4,6},{5,7},{6,4},{7,5},{8,10},{9,11},{10,... | collective-permute-start | bytes 792584 | tf_op jit(solution)/shard_map/ppermute | solution.py:379
  36.8 7.6 %collective-permute-start.5 = (f32[258,128]{1,0:T(8,128)S(1)}, f32[258,128]{1,0:T(8,128)S(1)}, u32[]{:S(2)}, u32[]{:S(2)}) collective-permute-start(f32[258,128]{1,0:T(8,128)S(1)} %get-tuple-element.40), channel_id=1, source_target_pairs={{0,4},{1,5},{2,6},{3,7},{4,0},{5,1},{6,2},{7,3},{8,12},{9,13},{10,... | collective-permute-start | bytes 396296 | tf_op jit(solution)/shard_map/ppermute | solution.py:379
  37.7 13.5 %collective-permute-start.10 = (f32[1032,128]{1,0:T(8,128)S(1)}, f32[1032,128]{1,0:T(8,128)S(1)}, u32[]{:S(2)}, u32[]{:S(2)}) collective-permute-start(f32[1032,128]{1,0:T(8,128)S(1)} %shard_map.80), channel_id=1, source_target_pairs={{0,8},{1,9},{2,10},{3,11},{4,12},{5,13},{6,14},{7,15},{8,0},{9,1},... | collective-permute-start | bytes 1585160 | tf_op jit(solution)/shard_map/ppermute | solution.py:379
  38.0 6.4 %collective-permute-start.7 = (f32[258,128]{1,0:T(8,128)S(1)}, f32[258,128]{1,0:T(8,128)S(1)}, u32[]{:S(2)}, u32[]{:S(2)}) collective-permute-start(f32[258,128]{1,0:T(8,128)S(1)} %get-tuple-element.41), channel_id=1, source_target_pairs={{0,2},{1,3},{2,0},{3,1},{4,6},{5,7},{6,4},{7,5},{8,10},{9,11},{10,... | collective-permute-start | bytes 396296 | tf_op jit(solution)/shard_map/ppermute | solution.py:379
  44.5 23.0 %collective-permute-start.9 = (f32[258,128]{1,0:T(8,128)S(1)}, f32[258,128]{1,0:T(8,128)S(1)}, u32[]{:S(2)}, u32[]{:S(2)}) collective-permute-start(f32[258,128]{1,0:T(8,128)S(1)} %pad_maximum_fusion.3), channel_id=1, source_target_pairs={{0,24},{1,25},{2,26},{3,27},{4,28},{5,29},{6,30},{7,31},{8,16},{9,... | collective-permute-start | bytes 396296 | tf_op jit(solution)/shard_map/ppermute | solution.py:379
  51.3 5.9 %collective-permute-start.13 = (f32[258,128]{1,0:T(8,128)S(1)}, f32[258,128]{1,0:T(8,128)S(1)}, u32[]{:S(2)}, u32[]{:S(2)}) collective-permute-start(f32[258,128]{1,0:T(8,128)S(1)} %pad_maximum_fusion.5), channel_id=1, source_target_pairs={{0,4},{1,5},{2,6},{3,7},{4,0},{5,1},{6,2},{7,3},{8,12},{9,13},{10,... | collective-permute-start | bytes 396296 | tf_op jit(solution)/shard_map/ppermute | solution.py:379
  53.4 14.1 %collective-permute-start.8 = (f32[258,128]{1,0:T(8,128)S(1)}, f32[258,128]{1,0:T(8,128)S(1)}, u32[]{:S(2)}, u32[]{:S(2)}) collective-permute-start(f32[258,128]{1,0:T(8,128)S(1)} %pad_maximum_fusion.2), channel_id=1, source_target_pairs={{0,16},{1,17},{2,18},{3,19},{4,20},{5,21},{6,22},{7,23},{8,24},{9,... | collective-permute-start | bytes 396296 | tf_op jit(solution)/shard_map/ppermute | solution.py:379
  56.7 5.4 %collective-permute-start.11 = (f32[258,128]{1,0:T(8,128)S(1)}, f32[258,128]{1,0:T(8,128)S(1)}, u32[]{:S(2)}, u32[]{:S(2)}) collective-permute-start(f32[258,128]{1,0:T(8,128)S(1)} %pad_maximum_fusion.4), channel_id=1, source_target_pairs={{0,2},{1,3},{2,0},{3,1},{4,6},{5,7},{6,4},{7,5},{8,10},{9,11},{10,... | collective-permute-start | bytes 396296 | tf_op jit(solution)/shard_map/ppermute | solution.py:379
  62.2 4.4 %collective-permute-start.14 = (f32[129,128]{1,0:T(8,128)S(1)}, f32[129,128]{1,0:T(8,128)S(1)}, u32[]{:S(2)}, u32[]{:S(2)}) collective-permute-start(f32[129,128]{1,0:T(8,128)S(1)} %pad_maximum_fusion.8), channel_id=1, source_target_pairs={{0,2},{1,3},{2,0},{3,1},{4,6},{5,7},{6,4},{7,5},{8,10},{9,11},{10,... | collective-permute-start | bytes 198152 | tf_op jit(solution)/shard_map/ppermute | solution.py:379
  63.1 4.3 %collective-permute-start.12 = (f32[129,128]{1,0:T(8,128)S(1)}, f32[129,128]{1,0:T(8,128)S(1)}, u32[]{:S(2)}, u32[]{:S(2)}) collective-permute-start(f32[129,128]{1,0:T(8,128)S(1)} %pad_maximum_fusion.7), channel_id=1, source_target_pairs={{0,4},{1,5},{2,6},{3,7},{4,0},{5,1},{6,2},{7,3},{8,12},{9,13},{10,... | collective-permute-start | bytes 198152 | tf_op jit(solution)/shard_map/ppermute | solution.py:379

commit v5 on v4

--- a/solution.py
+++ b/solution.py
@@ -9,6 +9,7 @@
 
 KEYS = 8192
 STEP = 512
+LEVEL = 1024
 SECTIONS = 4
 LANES = 128
 BF16 = jnp.bfloat16
@@ -110,17 +111,17 @@
     b2,
     b3,
     out_ref,
-    count_ref,
+    own_packed,
+    own_lines,
+    weight,
+    bias,
     x_ref,
     keys_ref,
     valid_ref,
-    weight,
-    bias,
     bytes_,
     sparse,
-    packed,
-    lines_ref,
-    table,
+    out_packed,
+    out_lines,
     sems,
 ):
     batches, block, width = x_hbm.shape
@@ -171,76 +172,102 @@
             sparse[1, at : at + 1, :] = code[:, q * tile : (q + 1) * tile]
 
     depths = sparse[0]
+    here = jnp.where(sparse[1] >= plan.half, 1.0, 0.0) == core.astype(F32)
     before = (iota((tile, tile), 0) < iota((tile, tile), 1)).astype(F32).astype(BF16)
-    live = jnp.where(depths > 0.0, 1.0, 0.0)
-    places = jnp.dot(live.astype(BF16), before, preferred_element_type=F32)
-    places = jnp.where(depths > 0.0, places, -1.0)
+    lists = []
+    for same in (here, jnp.logical_not(here)):
+        live = jnp.where(jnp.logical_and(depths > 0.0, same), 1.0, 0.0)
+        places = jnp.dot(live.astype(BF16), before, preferred_element_type=F32)
+        lists.append((live, jnp.where(live > 0.0, places, -1.0)))
     row8 = iota((8, tile), 0)
     lane8 = iota((8, LANES), 1)
     empty = jnp.where(iota((8, LANES), 0) == 0, -1.0, 0.0)
-    for i in range(lines_ref.shape[0]):
-        lines_ref[i] = empty
-    offset = 0
+    packed, lines_refs = (own_packed, out_packed), (own_lines, out_lines)
+    for lines_ref in lines_refs:
+        for i in range(lines_ref.shape[0]):
+            lines_ref[i] = empty
+    offsets = [0, 0]
     for m in range(batches):
         x_copies[m].wait()
         for q in range(per_batch):
             at = m * per_batch + q
-            move = jnp.where(places[at : at + 1] == iota((tile, tile), 0).astype(F32), 1.0, 0.0).astype(BF16)
+            spots = iota((tile, tile), 0).astype(F32)
+            moves = [jnp.where(places[at : at + 1] == spots, 1.0, 0.0).astype(BF16) for _, places in lists]
+            move = jnp.concatenate(moves, axis=0)
             both = jnp.concatenate(split(x_ref[m, q * tile : (q + 1) * tile, :]), axis=1)
             moved = jnp.dot(move, both, preferred_element_type=F32)
-            packed[pl.ds(offset, tile), :] = moved[:, :width] + moved[:, width:]
+            moved = moved[:, :width] + moved[:, width:]
             code = sparse[1, at : at + 1, :] + 1.0
             high = jnp.floor(code * (1.0 / LANES))
             info = jnp.where(row8 == 0, high, jnp.where(row8 == 1, code - high * LANES, 0.0))
             info = jnp.where(row8 == 2, sparse[0, at : at + 1, :], info).astype(BF16)
-            info = lax.dot_general(info, move, (((1,), (1,)), ((), ())), preferred_element_type=F32)
-            code = info[:1] * LANES + info[1:2] - 1.0
-            info = jnp.where(row8 == 0, code, jnp.where(row8 == 1, info[2:3], 0.0))
-            shift = offset & (LANES - 1)
-            info = pltpu.roll(jnp.concatenate([info, empty], axis=1), shift, axis=1)
-            line = offset // LANES
-            lines_ref[line] = jnp.where(lane8 < shift, lines_ref[line], info[:, :LANES])
-            for j in range(1, tile // LANES + 1):
-                lines_ref[line + j] = info[:, j * LANES : (j + 1) * LANES]
-            number = jnp.sum(live[at : at + 1]).astype(jnp.int32)
-            offset = pl.multiple_of(offset + ((number + 7) // 8) * 8, 8)
-    packed[pl.ds(offset, STEP), :] = jnp.zeros((STEP, width), F32)
-    table[...] = jnp.zeros_like(table)
-
-    def levels(step, _):
-        at = pl.multiple_of(step * STEP, STEP)
+            infos = lax.dot_general(info, move, (((1,), (1,)), ((), ())), preferred_element_type=F32)
+            for l, (live, _) in enumerate(lists):
+                offset = offsets[l]
+                packed[l][pl.ds(offset, tile), :] = moved[l * tile : (l + 1) * tile]
+                info = infos[:, l * tile : (l + 1) * tile]
+                code = info[:1] * LANES + info[1:2] - 1.0
+                info = jnp.where(row8 == 0, code, jnp.where(row8 == 1, info[2:3], 0.0))
+                shift = offset & (LANES - 1)
+                info = pltpu.roll(jnp.concatenate([info, empty], axis=1), shift, axis=1)
+                line = offset // LANES
+                lines_ref = lines_refs[l]
+                lines_ref[line] = jnp.where(lane8 < shift, lines_ref[line], info[:, :LANES])
+                for j in range(1, tile // LANES + 1):
+                    lines_ref[line + j] = info[:, j * LANES : (j + 1) * LANES]
+                number = jnp.sum(live[at : at + 1]).astype(jnp.int32)
+                offsets[l] = pl.multiple_of(offset + ((number + 7) // 8) * 8, 8)
+    for l in range(2):
+        packed[l][pl.ds(offsets[l], LEVEL), :] = jnp.zeros((LEVEL, width), F32)
+    used = jnp.full((8, width), offsets[0].astype(F32))
+    own_lines[own_lines.shape[0] - 1] = used
+    used = offsets[1]
+    out_ref[out_ref.shape[0] - 8 :, :] = jnp.full((8, width), used.astype(F32))
+    rows = batches * block
+    lines = rows // LANES
+    counts = out_ref.at[rows + lines : rows + lines + plan.half // LANES]
+    run_levels(plan, rows, 1 - core, used, out_packed, out_lines, weight, bias, out_ref, counts)
+
+
+def run_levels(plan, rows, core, used, packed, lines_ref, weight, bias, target, counts):
+    width = target.shape[1]
+    counts[...] = jnp.zeros(counts.shape, F32)
+
+    def body(step, _):
+        at = pl.multiple_of(step * LEVEL, LEVEL)
         columns, codes, depths = [], [], []
-        for j in range(STEP // LANES):
-            line = lines_ref[step * (STEP // LANES) + j]
+        for j in range(LEVEL // LANES):
+            line = lines_ref[step * (LEVEL // LANES) + j]
             columns.append(jnp.broadcast_to(jnp.transpose(line)[:, 1:2], (LANES, width)))
             codes.append(line[:1])
             depths.append(line[1:2])
         depth = jnp.concatenate(columns, axis=0)
-        code = jnp.concatenate(codes, axis=1).astype(jnp.int32)
-        outer = (iota((table.shape[0], STEP), 0) == (code >> 7)).astype(F32).astype(BF16)
-        inner = iota((LANES, STEP), 0) == (code & (LANES - 1))
+        code = jnp.concatenate(codes, axis=1).astype(jnp.int32) - core * plan.half
+        outer = (iota((counts.shape[0], LEVEL), 0) == (code >> 7)).astype(F32).astype(BF16)
+        inner = iota((LANES, LEVEL), 0) == (code & (LANES - 1))
         inner = jnp.where(inner, jnp.concatenate(depths, axis=1), 0.0).astype(BF16)
-        table[...] += lax.dot_general(outer, inner, (((1,), (1,)), ((), ())), preferred_element_type=F32)
-        hidden = packed[pl.ds(at, STEP), :]
-        total = jnp.zeros((STEP, width), F32)
+        counts[...] += lax.dot_general(outer, inner, (((1,), (1,)), ((), ())), preferred_element_type=F32)
+        hidden = packed[pl.ds(at, LEVEL), :]
+        total = jnp.zeros((LEVEL, width), F32)
         for s in range(SECTIONS):
             both = jnp.concatenate(split(hidden), axis=1)
             product = jnp.dot(both, weight[s], preferred_element_type=F32)
             hidden = hidden + jnp.tanh(product[:, :width] + product[:, width:] + bias[s, :1, :])
             total = total + jnp.where(depth > s, hidden, 0.0)
-        out_ref[pl.ds(at, STEP), :] = total
+        target[pl.ds(at, LEVEL), :] = total
         return 0
 
-    lax.fori_loop(0, (offset + (STEP - 1)) // STEP, levels, 0)
-    rows = batches * block
+    lax.fori_loop(0, (used + (LEVEL - 1)) // LEVEL, body, 0)
     for i in range(rows // LANES):
-        out_ref[rows + i : rows + i + 1, :] = lines_ref[i, :1, :]
-    lines = plan.half // LANES
-    first = core == 0
-    at = rows + rows // LANES
-    count_ref[...] = jnp.where(first, table[:lines], table[lines:])
-    out_ref[at : at + lines, :] = jnp.where(first, table[lines:], table[:lines])
-    out_ref[at + lines :, :] = jnp.full((8, width), offset.astype(F32))
+        target[rows + i : rows + i + 1, :] = lines_ref[i, :1, :]
+
+
+def own_levels_kernel(plan, rows, packed, lines_ref, weight, bias, own_ref, counts):
+    core = lax.axis_index("rows") & 1
+    used = lines_ref[lines_ref.shape[0] - 1]
+    own_ref[own_ref.shape[0] - 8 :, :] = used
+    used = jnp.max(used).astype(jnp.int32)
+    run_levels(plan, rows, core, used, packed, lines_ref, weight, bias, own_ref, counts)
 
 
 def add_products(plan, rows, source, first, slots, sums):
@@ -331,26 +358,31 @@
     lines = rows // LANES
     tables = plan.half // LANES
     tile = min(256, block)
-    own, count = call(
+    listed = (shape(rows + LEVEL, width), shape(lines + LEVEL // LANES + 1, 8, LANES))
+    given, *mine = call(
         functools.partial(advance_kernel, plan),
-        (shape(rows + lines + tables + 8, width), shape(tables, LANES)),
+        (
+            shape(rows + lines + tables + 8, width),
+            *listed,
+            jax.ShapeDtypeStruct((SECTIONS, 2 * width, 2 * width), BF16),
+            shape(SECTIONS, 8, width),
+        ),
         (rows_data, row_keys, valid_counts.reshape(1, batches), *buffers),
         scratch=[
             pltpu.VMEM((batches, block, width), F32),
             pltpu.VMEM((batches, block), jnp.int32),
             pltpu.VMEM((1, batches), jnp.int32),
-            pltpu.VMEM((SECTIONS, 2 * width, 2 * width), BF16),
-            pltpu.VMEM((SECTIONS, 8, width), F32),
             pltpu.VMEM((SECTIONS, 8, LANES), F32),
             pltpu.VMEM((2, rows // tile, tile), F32),
-            pltpu.VMEM((rows + STEP, width), F32),
-            pltpu.VMEM((lines + STEP // LANES, 8, LANES), F32),
-            pltpu.VMEM((2 * tables, LANES), F32),
+            *(pltpu.VMEM(one.shape, F32) for one in listed),
             pltpu.SemaphoreType.DMA((batches + 2,)),
         ],
         hbm=(0, 1, 2),
     )
-    other = lax.ppermute(own, axes, plan.perm(1, 0))
+    other = lax.ppermute(given, axes, plan.perm(1, 0))
+    own, count = call(
+        functools.partial(own_levels_kernel, plan, rows), (shape(rows + lines + 8, width), shape(tables, LANES)), mine
+    )
     part = call(
         functools.partial(own_kernel, plan, rows),
         shape(2 * plan.chunk, width),

time: 69.1 us -> 68.5 us (level)
  Pallas kernels: 24.8 us -> 16.7 us
  waiting for transfers between devices: 19.1 us -> 26.4 us
    pallas_call x7 -> x8, Pallas kernels: 24.8 us -> 16.7 us  [call(): pl.pallas_call(kernel, out_shape=out_shape, in_specs=[HBM if i in hbm els...]
    ppermute x11, waiting for transfers between devices: 12.7 us -> 18.9 us  [send(): return lax.ppermute(message, axes, plan.perm(row_xor, section_xor))]
    ppermute x1, waiting for transfers between devices: 0.25 us -> 1.27 us  [shards(): other = lax.ppermute(given, axes, plan.perm(1, 0))]
  transfers between devices with their start and end apart: 15 -> 15, of which waited for: 8 -> 11; matrix products, arithmetic and copies ran while one was open for 1% -> 1% of each run, Pallas kernels for 22% -> 12%
where the time goes in v5:
time: 68.5 us; the launch traced here: 68.3 us
  waiting for transfers between devices  26.4 us (39%)
  starting transfers between devices  22.5 us (33%)
  Pallas kernels  16.7 us (24%)
  other arithmetic  1.7 us (2%)
  between operations  0.91 us (1%)
    ppermute x11, waiting for transfers between devices, send(): return lax.ppermute(message, axes, plan.perm(row_xor, section_xor))  18.9 us
    pallas_call x8, Pallas kernels, call(): pl.pallas_call(kernel, out_shape=out_shape, in_specs=[HBM if i in hbm els...  16.7 us
    ppermute x11, starting transfers between devices, send(): return lax.ppermute(message, axes, plan.perm(row_xor, section_xor))  16.7 us
    ppermute x3, waiting for transfers between devices, shards(): buffers.append(lax.ppermute(packed[k], axes, plan.perm(0, k)))  6.2 us
    ppermute x3, starting transfers between devices, shards(): buffers.append(lax.ppermute(packed[k], axes, plan.perm(0, k)))  5.71 us
  transfers between devices with their start and end apart: 15, of which 11 were waited for; matrix products, arithmetic and copies ran while one was open for 1% of the time, Pallas kernels for 12%

profile of v5, /device:TPU:0, one launch (start us, length us, event | category | flops | bytes accessed | tf_op | source)
XLA Modules:
  0.0 68.3 jit_solution(13955643852406066269)
XLA Ops:
  0.6 1.0 %shard_map.77 = (f32[136,128]{1,0:T(8,128)S(1)}, f32[136,128]{1,0:T(8,128)S(1)}, f32[136,128]{1,0:T(8,128)S(1)}, f32[136,128]{1,0:T(8,128)S(1)}) custom-call(s32[1,16,32]{2,1,0:T(8,128)} %predicates_hbm.1, f32[1,128,128]{2,1,0:T(8,128)} %weight_hbm.1, f32[1,128]{1,0:T(1,128)} %bias_hbm.1), custom_call_target="tpu_custom_call" | custom-call | tf_op jit(solution)/shard_map/pallas_call | solution.py:320
  1.6 3.1 %collective-permute-start = (f32[136,128]{1,0:T(8,128)S(1)}, f32[136,128]{1,0:T(8,128)S(1)}, u32[]{:S(2)}, u32[]{:S(2)}) collective-permute-start(f32[136,128]{1,0:T(8,128)S(1)} %get-tuple-element.20), channel_id=1, source_target_pairs={{0,8},{1,9},{2,10},{3,11},{4,12},{5,13},{6,14},{7,15},{8,0},{9,1},... | collective-permute-start | bytes 208904 | tf_op jit(solution)/shard_map/ppermute | solution.py:356
  4.7 2.6 %collective-permute-start.1 = (f32[136,128]{1,0:T(8,128)S(1)}, f32[136,128]{1,0:T(8,128)S(1)}, u32[]{:S(2)}, u32[]{:S(2)}) collective-permute-start(f32[136,128]{1,0:T(8,128)S(1)} %get-tuple-element.21), channel_id=1, source_target_pairs={{0,16},{1,17},{2,18},{3,19},{4,20},{5,21},{6,22},{7,23},{8,24},{9,... | collective-permute-start | bytes 208904 | tf_op jit(solution)/shard_map/ppermute | solution.py:356
  7.3 0.0 collective-permute-start.2
  7.3 0.0 collective-permute-done.b1
  7.3 4.9 %collective-permute-done.1.b2 = f32[136,128]{1,0:T(8,128)S(1)} collective-permute-done((f32[136,128]{1,0:T(8,128)S(1)}, f32[136,128]{1,0:T(8,128)S(1)}, u32[]{:S(2)}, u32[]{:S(2)}) %collective-permute-start.1) | collective-permute-done | bytes 69664 | tf_op jit(solution)/shard_map/ppermute | solution.py:356
  12.2 1.3 %collective-permute-done.2.b3 = f32[136,128]{1,0:T(8,128)S(1)} collective-permute-done((f32[136,128]{1,0:T(8,128)S(1)}, f32[136,128]{1,0:T(8,128)S(1)}, u32[]{:S(2)}, u32[]{:S(2)}) %collective-permute-start.2) | collective-permute-done | bytes 69664 | tf_op jit(solution)/shard_map/ppermute | solution.py:356
  13.5 6.3 %shard_map.78 = (f32[4168,128]{1,0:T(8,128)S(1)}, f32[5120,128]{1,0:T(8,128)S(1)}, f32[41,8,128]{2,1,0:T(8,128)S(1)}, bf16[4,256,256]{2,1,0:T(8,128)(2,1)S(1)}, f32[4,8,128]{2,1,0:T(8,128)S(1)}) custom-call(f32[4,1024,128]{2,1,0:T(8,128)} %x_hbm.1, s32[4,1024]{1,0:T(4,128)} %keys_hbm.1, s32[1,4]{1,0:T(1,128)} %bitcast.65, ...), custom_call_target="tpu_custom_call" | custom-call | tf_op jit(solution)/shard_map/pallas_call | solution.py:320
  19.8 0.1 collective-permute-start.3
  19.9 1.2 %shard_map.79 = (f32[4136,128]{1,0:T(8,128)S(1)}, f32[32,128]{1,0:T(8,128)S(1)}) custom-call(f32[5120,128]{1,0:T(8,128)S(1)} %get-tuple-element.24.packed, f32[41,8,128]{2,1,0:T(8,128)S(1)} %get-tuple-element.25.lines_ref, bf16[4,256,256]{2,1,0:T(8,128)(2,1)S(1)} %get-tuple-element.26.weight, f32[4,8,128]{2,1,0:T(8,128)S(1)} %get-tuple-element.27.bias), custom_call_target="tpu_custom_call" | custom-call | tf_op jit(solution)/shard_map/pallas_call | solution.py:320
  21.1 1.7 %shard_map.80.mine_ref = f32[2048,128]{1,0:T(8,128)S(1)} custom-call(f32[4136,128]{1,0:T(8,128)S(1)} %get-tuple-element.28.own_ref.mine_ref), custom_call_target="tpu_custom_call" | custom-call | tf_op jit(solution)/shard_map/pallas_call | solution.py:320
  22.8 1.3 %collective-permute-done.3.other_ref = f32[4168,128]{1,0:T(8,128)S(1)} collective-permute-done((f32[4168,128]{1,0:T(8,128)S(1)}, f32[4168,128]{1,0:T(8,128)S(1)}, u32[]{:S(2)}, u32[]{:S(2)}) %collective-permute-start.3) | collective-permute-done | bytes 2134048 | tf_op jit(solution)/shard_map/ppermute | solution.py:382
  24.1 1.1 %shard_map.83 = (f32[516,128]{1,0:T(8,128)S(1)}, f32[516,128]{1,0:T(8,128)S(1)}) custom-call(f32[4168,128]{1,0:T(8,128)S(1)} %collective-permute-done.3.other_ref, f32[2048,128]{1,0:T(8,128)S(1)} %shard_map.80.mine_ref, f32[32,128]{1,0:T(8,128)S(1)} %get-tuple-element.35.count_ref), custom_call_target="tpu_custom_call" | custom-call | tf_op jit(solution)/shard_map/pallas_call | solution.py:320
  25.2 1.6 %collective-permute-start.6 = (f32[516,128]{1,0:T(8,128)S(1)}, f32[516,128]{1,0:T(8,128)S(1)}, u32[]{:S(2)}, u32[]{:S(2)}) collective-permute-start(f32[516,128]{1,0:T(8,128)S(1)} %get-tuple-element.34), channel_id=1, source_target_pairs={{0,4},{1,5},{2,6},{3,7},{4,0},{5,1},{6,2},{7,3},{8,12},{9,13},{10,... | collective-permute-start | bytes 792584 | tf_op jit(solution)/shard_map/ppermute | solution.py:411
  26.8 1.5 %collective-permute-start.4 = (f32[516,128]{1,0:T(8,128)S(1)}, f32[516,128]{1,0:T(8,128)S(1)}, u32[]{:S(2)}, u32[]{:S(2)}) collective-permute-start(f32[516,128]{1,0:T(8,128)S(1)} %get-tuple-element.32), channel_id=1, source_target_pairs={{0,2},{1,3},{2,0},{3,1},{4,6},{5,7},{6,4},{7,5},{8,10},{9,11},{10,... | collective-permute-start | bytes 792584 | tf_op jit(solution)/shard_map/ppermute | solution.py:411
  28.3 1.1 %shard_map.81 = f32[1032,128]{1,0:T(8,128)S(1)} custom-call(f32[4168,128]{1,0:T(8,128)S(1)} %collective-permute-done.3.other_ref, f32[2048,128]{1,0:T(8,128)S(1)} %shard_map.80.mine_ref, f32[32,128]{1,0:T(8,128)S(1)} %get-tuple-element.35.count_ref), custom_call_target="tpu_custom_call" | custom-call | tf_op jit(solution)/shard_map/pallas_call | solution.py:320
  29.5 2.1 %shard_map.82 = (f32[516,128]{1,0:T(8,128)S(1)}, f32[516,128]{1,0:T(8,128)S(1)}) custom-call(f32[4168,128]{1,0:T(8,128)S(1)} %collective-permute-done.3.other_ref, f32[4136,128]{1,0:T(8,128)S(1)} %get-tuple-element.28.own_ref.mine_ref, f32[32,128]{1,0:T(8,128)S(1)} %get-tuple-element.35.count_ref), custom_call_target="tpu_custom_call" | custom-call | tf_op jit(solution)/shard_map/pallas_call | solution.py:320
  31.6 2.5 %collective-permute-done.6 = f32[516,128]{1,0:T(8,128)S(1)} collective-permute-done((f32[516,128]{1,0:T(8,128)S(1)}, f32[516,128]{1,0:T(8,128)S(1)}, u32[]{:S(2)}, u32[]{:S(2)}) %collective-permute-start.6) | collective-permute-done | bytes 264224 | tf_op jit(solution)/shard_map/ppermute | solution.py:411
  34.1 1.3 %collective-permute-done.4 = f32[516,128]{1,0:T(8,128)S(1)} collective-permute-done((f32[516,128]{1,0:T(8,128)S(1)}, f32[516,128]{1,0:T(8,128)S(1)}, u32[]{:S(2)}, u32[]{:S(2)}) %collective-permute-start.4) | collective-permute-done | bytes 264224 | tf_op jit(solution)/shard_map/ppermute | solution.py:411
  35.5 1.0 %collective-permute-start.5 = (f32[258,128]{1,0:T(8,128)S(1)}, f32[258,128]{1,0:T(8,128)S(1)}, u32[]{:S(2)}, u32[]{:S(2)}) collective-permute-start(f32[258,128]{1,0:T(8,128)S(1)} %get-tuple-element.50), channel_id=1, source_target_pairs={{0,4},{1,5},{2,6},{3,7},{4,0},{5,1},{6,2},{7,3},{8,12},{9,13},{10,... | collective-permute-start | bytes 396296 | tf_op jit(solution)/shard_map/ppermute | solution.py:411
  36.5 0.4 collective-permute-start.10
  36.9 1.5 %collective-permute-start.7 = (f32[258,128]{1,0:T(8,128)S(1)}, f32[258,128]{1,0:T(8,128)S(1)}, u32[]{:S(2)}, u32[]{:S(2)}) collective-permute-start(f32[258,128]{1,0:T(8,128)S(1)} %get-tuple-element.51), channel_id=1, source_target_pairs={{0,2},{1,3},{2,0},{3,1},{4,6},{5,7},{6,4},{7,5},{8,10},{9,11},{10,... | collective-permute-start | bytes 396296 | tf_op jit(solution)/shard_map/ppermute | solution.py:411
  38.4 2.1 %shard_map.84 = f32[1032,128]{1,0:T(8,128)S(1)} custom-call(f32[4168,128]{1,0:T(8,128)S(1)} %collective-permute-done.3.other_ref, f32[4136,128]{1,0:T(8,128)S(1)} %get-tuple-element.28.own_ref.mine_ref, f32[32,128]{1,0:T(8,128)S(1)} %get-tuple-element.35.count_ref), custom_call_target="tpu_custom_call" | custom-call | tf_op jit(solution)/shard_map/pallas_call | solution.py:320
  40.5 0.1 collective-permute-done.5
  40.7 1.6 %collective-permute-done.7 = f32[258,128]{1,0:T(8,128)S(1)} collective-permute-done((f32[258,128]{1,0:T(8,128)S(1)}, f32[258,128]{1,0:T(8,128)S(1)}, u32[]{:S(2)}, u32[]{:S(2)}) %collective-permute-start.7) | collective-permute-done | bytes 132128 | tf_op jit(solution)/shard_map/ppermute | solution.py:411
  42.3 3.7 %collective-permute-start.9 = (f32[258,128]{1,0:T(8,128)S(1)}, f32[258,128]{1,0:T(8,128)S(1)}, u32[]{:S(2)}, u32[]{:S(2)}) collective-permute-start(f32[258,128]{1,0:T(8,128)S(1)} %pad_maximum_fusion.3), channel_id=1, source_target_pairs={{0,24},{1,25},{2,26},{3,27},{4,28},{5,29},{6,30},{7,31},{8,16},{9,... | collective-permute-start | bytes 396296 | tf_op jit(solution)/shard_map/ppermute | solution.py:411
  46.0 4.3 %collective-permute-done.10 = f32[1032,128]{1,0:T(8,128)S(1)} collective-permute-done((f32[1032,128]{1,0:T(8,128)S(1)}, f32[1032,128]{1,0:T(8,128)S(1)}, u32[]{:S(2)}, u32[]{:S(2)}) %collective-permute-start.10) | collective-permute-done | bytes 528416 | tf_op jit(solution)/shard_map/ppermute | solution.py:411
  50.3 0.1 add.68
  50.5 1.0 %collective-permute-start.13 = (f32[258,128]{1,0:T(8,128)S(1)}, f32[258,128]{1,0:T(8,128)S(1)}, u32[]{:S(2)}, u32[]{:S(2)}) collective-permute-start(f32[258,128]{1,0:T(8,128)S(1)} %pad_maximum_fusion.5), channel_id=1, source_target_pairs={{0,4},{1,5},{2,6},{3,7},{4,0},{5,1},{6,2},{7,3},{8,12},{9,13},{10,... | collective-permute-start | bytes 396296 | tf_op jit(solution)/shard_map/ppermute | solution.py:411
  51.5 4.7 %collective-permute-start.8 = (f32[258,128]{1,0:T(8,128)S(1)}, f32[258,128]{1,0:T(8,128)S(1)}, u32[]{:S(2)}, u32[]{:S(2)}) collective-permute-start(f32[258,128]{1,0:T(8,128)S(1)} %pad_maximum_fusion.2), channel_id=1, source_target_pairs={{0,16},{1,17},{2,18},{3,19},{4,20},{5,21},{6,22},{7,23},{8,24},{9,... | collective-permute-start | bytes 396296 | tf_op jit(solution)/shard_map/ppermute | solution.py:411
  56.3 0.4 collective-permute-start.11
  56.6 0.0 collective-permute-done.13
  56.7 5.4 %collective-permute-done.11 = f32[258,128]{1,0:T(8,128)S(1)} collective-permute-done((f32[258,128]{1,0:T(8,128)S(1)}, f32[258,128]{1,0:T(8,128)S(1)}, u32[]{:S(2)}, u32[]{:S(2)}) %collective-permute-start.11) | collective-permute-done | bytes 132128 | tf_op jit(solution)/shard_map/ppermute | solution.py:411
  62.2 0.4 collective-permute-start.14
  62.6 0.5 collective-permute-start.12
  63.1 3.4 %collective-permute-done.14 = f32[129,128]{1,0:T(8,128)S(1)} collective-permute-done((f32[129,128]{1,0:T(8,128)S(1)}, f32[129,128]{1,0:T(8,128)S(1)}, u32[]{:S(2)}, u32[]{:S(2)}) %collective-permute-start.14) | collective-permute-done | bytes 66080 | tf_op jit(solution)/shard_map/ppermute | solution.py:411
  66.6 0.3 collective-permute-done.12
  66.9 0.0 collective-permute-done.9
  66.9 0.0 collective-permute-done.8
  67.0 0.6 broadcast_maximum_fusion
  67.5 0.8 %slice_divide_fusion = f32[256,128]{1,0:T(8,128)} fusion(f32[258,128]{1,0:T(8,128)S(1)} %maximum_add_fusion, f32[256]{0:T(256)S(1)} %get-tuple-element.36), kind=kLoop, calls=%fused_computation.10 | loop fusion | flops 32768 | bytes 263168 | tf_op jit(solution)/shard_map/div | solution.py:445
  (37 shorter events, 0.4 us)
Async XLA Ops:
  1.6 5.7 %collective-permute-start = (f32[136,128]{1,0:T(8,128)S(1)}, f32[136,128]{1,0:T(8,128)S(1)}, u32[]{:S(2)}, u32[]{:S(2)}) collective-permute-start(f32[136,128]{1,0:T(8,128)S(1)} %get-tuple-element.20), channel_id=1, source_target_pairs={{0,8},{1,9},{2,10},{3,11},{4,12},{5,13},{6,14},{7,15},{8,0},{9,1},... | collective-permute-start | bytes 208904 | tf_op jit(solution)/shard_map/ppermute | solution.py:356
  4.7 7.5 %collective-permute-start.1 = (f32[136,128]{1,0:T(8,128)S(1)}, f32[136,128]{1,0:T(8,128)S(1)}, u32[]{:S(2)}, u32[]{:S(2)}) collective-permute-start(f32[136,128]{1,0:T(8,128)S(1)} %get-tuple-element.21), channel_id=1, source_target_pairs={{0,16},{1,17},{2,18},{3,19},{4,20},{5,21},{6,22},{7,23},{8,24},{9,... | collective-permute-start | bytes 208904 | tf_op jit(solution)/shard_map/ppermute | solution.py:356
  7.3 6.2 %collective-permute-start.2 = (f32[136,128]{1,0:T(8,128)S(1)}, f32[136,128]{1,0:T(8,128)S(1)}, u32[]{:S(2)}, u32[]{:S(2)}) collective-permute-start(f32[136,128]{1,0:T(8,128)S(1)} %get-tuple-element.22), channel_id=1, source_target_pairs={{0,24},{1,25},{2,26},{3,27},{4,28},{5,29},{6,30},{7,31},{8,16},{9,... | collective-permute-start | bytes 208904 | tf_op jit(solution)/shard_map/ppermute | solution.py:356
  19.8 4.3 %collective-permute-start.3 = (f32[4168,128]{1,0:T(8,128)S(1)}, f32[4168,128]{1,0:T(8,128)S(1)}, u32[]{:S(2)}, u32[]{:S(2)}) collective-permute-start(f32[4168,128]{1,0:T(8,128)S(1)} %get-tuple-element.23), channel_id=1, source_target_pairs={{0,1},{1,0},{2,3},{3,2},{4,5},{5,4},{6,7},{7,6},{8,9},{9,8},{10,11... | collective-permute-start | bytes 6402056 | tf_op jit(solution)/shard_map/ppermute | solution.py:382
  25.2 8.8 %collective-permute-start.6 = (f32[516,128]{1,0:T(8,128)S(1)}, f32[516,128]{1,0:T(8,128)S(1)}, u32[]{:S(2)}, u32[]{:S(2)}) collective-permute-start(f32[516,128]{1,0:T(8,128)S(1)} %get-tuple-element.34), channel_id=1, source_target_pairs={{0,4},{1,5},{2,6},{3,7},{4,0},{5,1},{6,2},{7,3},{8,12},{9,13},{10,... | collective-permute-start | bytes 792584 | tf_op jit(solution)/shard_map/ppermute | solution.py:411
  26.8 8.6 %collective-permute-start.4 = (f32[516,128]{1,0:T(8,128)S(1)}, f32[516,128]{1,0:T(8,128)S(1)}, u32[]{:S(2)}, u32[]{:S(2)}) collective-permute-start(f32[516,128]{1,0:T(8,128)S(1)} %get-tuple-element.32), channel_id=1, source_target_pairs={{0,2},{1,3},{2,0},{3,1},{4,6},{5,7},{6,4},{7,5},{8,10},{9,11},{10,... | collective-permute-start | bytes 792584 | tf_op jit(solution)/shard_map/ppermute | solution.py:411
  35.5 5.1 %collective-permute-start.5 = (f32[258,128]{1,0:T(8,128)S(1)}, f32[258,128]{1,0:T(8,128)S(1)}, u32[]{:S(2)}, u32[]{:S(2)}) collective-permute-start(f32[258,128]{1,0:T(8,128)S(1)} %get-tuple-element.50), channel_id=1, source_target_pairs={{0,4},{1,5},{2,6},{3,7},{4,0},{5,1},{6,2},{7,3},{8,12},{9,13},{10,... | collective-permute-start | bytes 396296 | tf_op jit(solution)/shard_map/ppermute | solution.py:411
  36.5 13.8 %collective-permute-start.10 = (f32[1032,128]{1,0:T(8,128)S(1)}, f32[1032,128]{1,0:T(8,128)S(1)}, u32[]{:S(2)}, u32[]{:S(2)}) collective-permute-start(f32[1032,128]{1,0:T(8,128)S(1)} %shard_map.81), channel_id=1, source_target_pairs={{0,8},{1,9},{2,10},{3,11},{4,12},{5,13},{6,14},{7,15},{8,0},{9,1},... | collective-permute-start | bytes 1585160 | tf_op jit(solution)/shard_map/ppermute | solution.py:411
  36.9 5.3 %collective-permute-start.7 = (f32[258,128]{1,0:T(8,128)S(1)}, f32[258,128]{1,0:T(8,128)S(1)}, u32[]{:S(2)}, u32[]{:S(2)}) collective-permute-start(f32[258,128]{1,0:T(8,128)S(1)} %get-tuple-element.51), channel_id=1, source_target_pairs={{0,2},{1,3},{2,0},{3,1},{4,6},{5,7},{6,4},{7,5},{8,10},{9,11},{10,... | collective-permute-start | bytes 396296 | tf_op jit(solution)/shard_map/ppermute | solution.py:411
  42.3 24.6 %collective-permute-start.9 = (f32[258,128]{1,0:T(8,128)S(1)}, f32[258,128]{1,0:T(8,128)S(1)}, u32[]{:S(2)}, u32[]{:S(2)}) collective-permute-start(f32[258,128]{1,0:T(8,128)S(1)} %pad_maximum_fusion.3), channel_id=1, source_target_pairs={{0,24},{1,25},{2,26},{3,27},{4,28},{5,29},{6,30},{7,31},{8,16},{9,... | collective-permute-start | bytes 396296 | tf_op jit(solution)/shard_map/ppermute | solution.py:411
  50.5 6.2 %collective-permute-start.13 = (f32[258,128]{1,0:T(8,128)S(1)}, f32[258,128]{1,0:T(8,128)S(1)}, u32[]{:S(2)}, u32[]{:S(2)}) collective-permute-start(f32[258,128]{1,0:T(8,128)S(1)} %pad_maximum_fusion.5), channel_id=1, source_target_pairs={{0,4},{1,5},{2,6},{3,7},{4,0},{5,1},{6,2},{7,3},{8,12},{9,13},{10,... | collective-permute-start | bytes 396296 | tf_op jit(solution)/shard_map/ppermute | solution.py:411
  51.5 15.4 %collective-permute-start.8 = (f32[258,128]{1,0:T(8,128)S(1)}, f32[258,128]{1,0:T(8,128)S(1)}, u32[]{:S(2)}, u32[]{:S(2)}) collective-permute-start(f32[258,128]{1,0:T(8,128)S(1)} %pad_maximum_fusion.2), channel_id=1, source_target_pairs={{0,16},{1,17},{2,18},{3,19},{4,20},{5,21},{6,22},{7,23},{8,24},{9,... | collective-permute-start | bytes 396296 | tf_op jit(solution)/shard_map/ppermute | solution.py:411
  56.3 5.8 %collective-permute-start.11 = (f32[258,128]{1,0:T(8,128)S(1)}, f32[258,128]{1,0:T(8,128)S(1)}, u32[]{:S(2)}, u32[]{:S(2)}) collective-permute-start(f32[258,128]{1,0:T(8,128)S(1)} %pad_maximum_fusion.4), channel_id=1, source_target_pairs={{0,2},{1,3},{2,0},{3,1},{4,6},{5,7},{6,4},{7,5},{8,10},{9,11},{10,... | collective-permute-start | bytes 396296 | tf_op jit(solution)/shard_map/ppermute | solution.py:411
  62.2 4.4 %collective-permute-start.14 = (f32[129,128]{1,0:T(8,128)S(1)}, f32[129,128]{1,0:T(8,128)S(1)}, u32[]{:S(2)}, u32[]{:S(2)}) collective-permute-start(f32[129,128]{1,0:T(8,128)S(1)} %pad_maximum_fusion.8), channel_id=1, source_target_pairs={{0,2},{1,3},{2,0},{3,1},{4,6},{5,7},{6,4},{7,5},{8,10},{9,11},{10,... | collective-permute-start | bytes 198152 | tf_op jit(solution)/shard_map/ppermute | solution.py:411
  62.6 4.3 %collective-permute-start.12 = (f32[129,128]{1,0:T(8,128)S(1)}, f32[129,128]{1,0:T(8,128)S(1)}, u32[]{:S(2)}, u32[]{:S(2)}) collective-permute-start(f32[129,128]{1,0:T(8,128)S(1)} %pad_maximum_fusion.7), channel_id=1, source_target_pairs={{0,4},{1,5},{2,6},{3,7},{4,0},{5,1},{6,2},{7,3},{8,12},{9,13},{10,... | collective-permute-start | bytes 198152 | tf_op jit(solution)/shard_map/ppermute | solution.py:411

commit v6 on v5

--- a/solution.py
+++ b/solution.py
@@ -440,9 +440,26 @@
     for step in range(plan.planes):
         _, states = halve(states, step)
     finals.append(close_message(jnp.concatenate([s for s, _ in states]), jnp.concatenate([c for _, c in states])))
-    total = functools.reduce(jnp.add, finals)
-    number = total[plan.owned :].reshape(-1)[: plan.owned]
-    return total[: plan.owned] / jnp.maximum(number, 1.0)[:, None], number
+    across = min(LANES, plan.owned)
+    means, number = call(
+        functools.partial(finish_kernel, plan),
+        (shape(plan.owned, width), shape(plan.owned // across, across)),
+        finals,
+        limit=8,
+    )
+    return means, number.reshape(-1)
+
+
+def finish_kernel(plan, *refs):
+    *parts, means_ref, number_ref = refs
+    total = functools.reduce(jnp.add, [part[: plan.owned, :] for part in parts])
+    number = functools.reduce(jnp.add, [part[plan.owned :, :] for part in parts])
+    number_ref[...] = number[:, : number_ref.shape[1]]
+    columns = []
+    for i in range(number.shape[0]):
+        column = jnp.transpose(jnp.broadcast_to(jnp.maximum(number[i : i + 1], 1.0), (8, LANES)))
+        columns.append(jnp.broadcast_to(column[:, :1], (LANES, total.shape[1])))
+    means_ref[...] = total / jnp.concatenate(columns, axis=0)[: plan.owned]
 
 
 def solution(mesh):

time: 68.5 us -> 68.1 us (level)
  other arithmetic: 1.7 us -> 0.36 us
  Pallas kernels: 16.7 us -> 17.6 us
    pallas_call x8 -> x9, Pallas kernels: 16.7 us -> 17.6 us  [call(): pl.pallas_call(kernel, out_shape=out_shape, in_specs=[HBM if i in hbm els...]
    div x1 -> x0, other arithmetic: 0.76 us -> none  [shards(): return (total[:plan.owned] / jnp.maximum(number, 1.0)[:, None], number)]
where the time goes in v6:
time: 68.1 us; the launch traced here: 67.8 us
  waiting for transfers between devices  26.4 us (39%)
  starting transfers between devices  22.5 us (33%)
  Pallas kernels  17.6 us (26%)
  between operations  0.92 us (1%)
    ppermute x11, waiting for transfers between devices, send(): return lax.ppermute(message, axes, plan.perm(row_xor, section_xor))  18.9 us
    pallas_call x9, Pallas kernels, call(): pl.pallas_call(kernel, out_shape=out_shape, in_specs=[HBM if i in hbm els...  17.6 us
    ppermute x11, starting transfers between devices, send(): return lax.ppermute(message, axes, plan.perm(row_xor, section_xor))  16.7 us
    ppermute x3, waiting for transfers between devices, shards(): buffers.append(lax.ppermute(packed[k], axes, plan.perm(0, k)))  6.2 us
    ppermute x3, starting transfers between devices, shards(): buffers.append(lax.ppermute(packed[k], axes, plan.perm(0, k)))  5.71 us
  transfers between devices with their start and end apart: 15, of which 11 were waited for; matrix products, arithmetic and copies ran while one was open for 1% of the time, Pallas kernels for 12%

profile of v6, /device:TPU:0, one launch (start us, length us, event | category | flops | bytes accessed | tf_op | source)
XLA Modules:
  0.0 67.8 jit_solution(11338504524422527615)
XLA Ops:
  0.6 1.0 %shard_map.77 = (f32[136,128]{1,0:T(8,128)S(1)}, f32[136,128]{1,0:T(8,128)S(1)}, f32[136,128]{1,0:T(8,128)S(1)}, f32[136,128]{1,0:T(8,128)S(1)}) custom-call(s32[1,16,32]{2,1,0:T(8,128)} %predicates_hbm.1, f32[1,128,128]{2,1,0:T(8,128)} %weight_hbm.1, f32[1,128]{1,0:T(1,128)} %bias_hbm.1), custom_call_target="tpu_custom_call" | custom-call | tf_op jit(solution)/shard_map/pallas_call | solution.py:320
  1.6 3.1 %collective-permute-start = (f32[136,128]{1,0:T(8,128)S(1)}, f32[136,128]{1,0:T(8,128)S(1)}, u32[]{:S(2)}, u32[]{:S(2)}) collective-permute-start(f32[136,128]{1,0:T(8,128)S(1)} %get-tuple-element.22), channel_id=1, source_target_pairs={{0,8},{1,9},{2,10},{3,11},{4,12},{5,13},{6,14},{7,15},{8,0},{9,1},... | collective-permute-start | bytes 208904 | tf_op jit(solution)/shard_map/ppermute | solution.py:356
  4.7 2.6 %collective-permute-start.1 = (f32[136,128]{1,0:T(8,128)S(1)}, f32[136,128]{1,0:T(8,128)S(1)}, u32[]{:S(2)}, u32[]{:S(2)}) collective-permute-start(f32[136,128]{1,0:T(8,128)S(1)} %get-tuple-element.23), channel_id=1, source_target_pairs={{0,16},{1,17},{2,18},{3,19},{4,20},{5,21},{6,22},{7,23},{8,24},{9,... | collective-permute-start | bytes 208904 | tf_op jit(solution)/shard_map/ppermute | solution.py:356
  7.3 0.0 collective-permute-start.2
  7.3 0.0 collective-permute-done.b1
  7.3 4.9 %collective-permute-done.1.b2 = f32[136,128]{1,0:T(8,128)S(1)} collective-permute-done((f32[136,128]{1,0:T(8,128)S(1)}, f32[136,128]{1,0:T(8,128)S(1)}, u32[]{:S(2)}, u32[]{:S(2)}) %collective-permute-start.1) | collective-permute-done | bytes 69664 | tf_op jit(solution)/shard_map/ppermute | solution.py:356
  12.2 1.3 %collective-permute-done.2.b3 = f32[136,128]{1,0:T(8,128)S(1)} collective-permute-done((f32[136,128]{1,0:T(8,128)S(1)}, f32[136,128]{1,0:T(8,128)S(1)}, u32[]{:S(2)}, u32[]{:S(2)}) %collective-permute-start.2) | collective-permute-done | bytes 69664 | tf_op jit(solution)/shard_map/ppermute | solution.py:356
  13.5 6.3 %shard_map.78 = (f32[4168,128]{1,0:T(8,128)S(1)}, f32[5120,128]{1,0:T(8,128)S(1)}, f32[41,8,128]{2,1,0:T(8,128)S(1)}, bf16[4,256,256]{2,1,0:T(8,128)(2,1)S(1)}, f32[4,8,128]{2,1,0:T(8,128)S(1)}) custom-call(f32[4,1024,128]{2,1,0:T(8,128)} %x_hbm.1, s32[4,1024]{1,0:T(4,128)} %keys_hbm.1, s32[1,4]{1,0:T(1,128)} %bitcast.63, ...), custom_call_target="tpu_custom_call" | custom-call | tf_op jit(solution)/shard_map/pallas_call | solution.py:320
  19.8 0.1 collective-permute-start.3
  19.9 1.2 %shard_map.79 = (f32[4136,128]{1,0:T(8,128)S(1)}, f32[32,128]{1,0:T(8,128)S(1)}) custom-call(f32[5120,128]{1,0:T(8,128)S(1)} %get-tuple-element.26.packed, f32[41,8,128]{2,1,0:T(8,128)S(1)} %get-tuple-element.27.lines_ref, bf16[4,256,256]{2,1,0:T(8,128)(2,1)S(1)} %get-tuple-element.28.weight, f32[4,8,128]{2,1,0:T(8,128)S(1)} %get-tuple-element.29.bias), custom_call_target="tpu_custom_call" | custom-call | tf_op jit(solution)/shard_map/pallas_call | solution.py:320
  21.1 1.7 %shard_map.80.mine_ref = f32[2048,128]{1,0:T(8,128)S(1)} custom-call(f32[4136,128]{1,0:T(8,128)S(1)} %get-tuple-element.30.own_ref.mine_ref), custom_call_target="tpu_custom_call" | custom-call | tf_op jit(solution)/shard_map/pallas_call | solution.py:320
  22.8 1.3 %collective-permute-done.3.other_ref = f32[4168,128]{1,0:T(8,128)S(1)} collective-permute-done((f32[4168,128]{1,0:T(8,128)S(1)}, f32[4168,128]{1,0:T(8,128)S(1)}, u32[]{:S(2)}, u32[]{:S(2)}) %collective-permute-start.3) | collective-permute-done | bytes 2134048 | tf_op jit(solution)/shard_map/ppermute | solution.py:382
  24.1 1.1 %shard_map.83 = (f32[516,128]{1,0:T(8,128)S(1)}, f32[516,128]{1,0:T(8,128)S(1)}) custom-call(f32[4168,128]{1,0:T(8,128)S(1)} %collective-permute-done.3.other_ref, f32[2048,128]{1,0:T(8,128)S(1)} %shard_map.80.mine_ref, f32[32,128]{1,0:T(8,128)S(1)} %get-tuple-element.37.count_ref), custom_call_target="tpu_custom_call" | custom-call | tf_op jit(solution)/shard_map/pallas_call | solution.py:320
  25.2 1.6 %collective-permute-start.6 = (f32[516,128]{1,0:T(8,128)S(1)}, f32[516,128]{1,0:T(8,128)S(1)}, u32[]{:S(2)}, u32[]{:S(2)}) collective-permute-start(f32[516,128]{1,0:T(8,128)S(1)} %get-tuple-element.36), channel_id=1, source_target_pairs={{0,4},{1,5},{2,6},{3,7},{4,0},{5,1},{6,2},{7,3},{8,12},{9,13},{10,... | collective-permute-start | bytes 792584 | tf_op jit(solution)/shard_map/ppermute | solution.py:411
  26.8 1.5 %collective-permute-start.4 = (f32[516,128]{1,0:T(8,128)S(1)}, f32[516,128]{1,0:T(8,128)S(1)}, u32[]{:S(2)}, u32[]{:S(2)}) collective-permute-start(f32[516,128]{1,0:T(8,128)S(1)} %get-tuple-element.34), channel_id=1, source_target_pairs={{0,2},{1,3},{2,0},{3,1},{4,6},{5,7},{6,4},{7,5},{8,10},{9,11},{10,... | collective-permute-start | bytes 792584 | tf_op jit(solution)/shard_map/ppermute | solution.py:411
  28.3 1.1 %shard_map.81 = f32[1032,128]{1,0:T(8,128)S(1)} custom-call(f32[4168,128]{1,0:T(8,128)S(1)} %collective-permute-done.3.other_ref, f32[2048,128]{1,0:T(8,128)S(1)} %shard_map.80.mine_ref, f32[32,128]{1,0:T(8,128)S(1)} %get-tuple-element.37.count_ref), custom_call_target="tpu_custom_call" | custom-call | tf_op jit(solution)/shard_map/pallas_call | solution.py:320
  29.5 2.1 %shard_map.82 = (f32[516,128]{1,0:T(8,128)S(1)}, f32[516,128]{1,0:T(8,128)S(1)}) custom-call(f32[4168,128]{1,0:T(8,128)S(1)} %collective-permute-done.3.other_ref, f32[4136,128]{1,0:T(8,128)S(1)} %get-tuple-element.30.own_ref.mine_ref, f32[32,128]{1,0:T(8,128)S(1)} %get-tuple-element.37.count_ref), custom_call_target="tpu_custom_call" | custom-call | tf_op jit(solution)/shard_map/pallas_call | solution.py:320
  31.6 2.5 %collective-permute-done.6 = f32[516,128]{1,0:T(8,128)S(1)} collective-permute-done((f32[516,128]{1,0:T(8,128)S(1)}, f32[516,128]{1,0:T(8,128)S(1)}, u32[]{:S(2)}, u32[]{:S(2)}) %collective-permute-start.6) | collective-permute-done | bytes 264224 | tf_op jit(solution)/shard_map/ppermute | solution.py:411
  34.1 1.3 %collective-permute-done.4 = f32[516,128]{1,0:T(8,128)S(1)} collective-permute-done((f32[516,128]{1,0:T(8,128)S(1)}, f32[516,128]{1,0:T(8,128)S(1)}, u32[]{:S(2)}, u32[]{:S(2)}) %collective-permute-start.4) | collective-permute-done | bytes 264224 | tf_op jit(solution)/shard_map/ppermute | solution.py:411
  35.5 1.0 %collective-permute-start.5 = (f32[258,128]{1,0:T(8,128)S(1)}, f32[258,128]{1,0:T(8,128)S(1)}, u32[]{:S(2)}, u32[]{:S(2)}) collective-permute-start(f32[258,128]{1,0:T(8,128)S(1)} %get-tuple-element.52), channel_id=1, source_target_pairs={{0,4},{1,5},{2,6},{3,7},{4,0},{5,1},{6,2},{7,3},{8,12},{9,13},{10,... | collective-permute-start | bytes 396296 | tf_op jit(solution)/shard_map/ppermute | solution.py:411
  36.5 0.4 collective-permute-start.10
  36.9 1.5 %collective-permute-start.7 = (f32[258,128]{1,0:T(8,128)S(1)}, f32[258,128]{1,0:T(8,128)S(1)}, u32[]{:S(2)}, u32[]{:S(2)}) collective-permute-start(f32[258,128]{1,0:T(8,128)S(1)} %get-tuple-element.53), channel_id=1, source_target_pairs={{0,2},{1,3},{2,0},{3,1},{4,6},{5,7},{6,4},{7,5},{8,10},{9,11},{10,... | collective-permute-start | bytes 396296 | tf_op jit(solution)/shard_map/ppermute | solution.py:411
  38.4 2.1 %shard_map.84 = f32[1032,128]{1,0:T(8,128)S(1)} custom-call(f32[4168,128]{1,0:T(8,128)S(1)} %collective-permute-done.3.other_ref, f32[4136,128]{1,0:T(8,128)S(1)} %get-tuple-element.30.own_ref.mine_ref, f32[32,128]{1,0:T(8,128)S(1)} %get-tuple-element.37.count_ref), custom_call_target="tpu_custom_call" | custom-call | tf_op jit(solution)/shard_map/pallas_call | solution.py:320
  40.5 0.1 collective-permute-done.5
  40.7 1.6 %collective-permute-done.7 = f32[258,128]{1,0:T(8,128)S(1)} collective-permute-done((f32[258,128]{1,0:T(8,128)S(1)}, f32[258,128]{1,0:T(8,128)S(1)}, u32[]{:S(2)}, u32[]{:S(2)}) %collective-permute-start.7) | collective-permute-done | bytes 132128 | tf_op jit(solution)/shard_map/ppermute | solution.py:411
  42.3 3.7 %collective-permute-start.9 = (f32[258,128]{1,0:T(8,128)S(1)}, f32[258,128]{1,0:T(8,128)S(1)}, u32[]{:S(2)}, u32[]{:S(2)}) collective-permute-start(f32[258,128]{1,0:T(8,128)S(1)} %pad_maximum_fusion.3), channel_id=1, source_target_pairs={{0,24},{1,25},{2,26},{3,27},{4,28},{5,29},{6,30},{7,31},{8,16},{9,... | collective-permute-start | bytes 396296 | tf_op jit(solution)/shard_map/ppermute | solution.py:411
  46.0 4.3 %collective-permute-done.10 = f32[1032,128]{1,0:T(8,128)S(1)} collective-permute-done((f32[1032,128]{1,0:T(8,128)S(1)}, f32[1032,128]{1,0:T(8,128)S(1)}, u32[]{:S(2)}, u32[]{:S(2)}) %collective-permute-start.10) | collective-permute-done | bytes 528416 | tf_op jit(solution)/shard_map/ppermute | solution.py:411
  50.3 0.1 add.61
  50.5 1.0 %collective-permute-start.13 = (f32[258,128]{1,0:T(8,128)S(1)}, f32[258,128]{1,0:T(8,128)S(1)}, u32[]{:S(2)}, u32[]{:S(2)}) collective-permute-start(f32[258,128]{1,0:T(8,128)S(1)} %pad_maximum_fusion.5), channel_id=1, source_target_pairs={{0,4},{1,5},{2,6},{3,7},{4,0},{5,1},{6,2},{7,3},{8,12},{9,13},{10,... | collective-permute-start | bytes 396296 | tf_op jit(solution)/shard_map/ppermute | solution.py:411
  51.5 4.7 %collective-permute-start.8 = (f32[258,128]{1,0:T(8,128)S(1)}, f32[258,128]{1,0:T(8,128)S(1)}, u32[]{:S(2)}, u32[]{:S(2)}) collective-permute-start(f32[258,128]{1,0:T(8,128)S(1)} %pad_maximum_fusion.2), channel_id=1, source_target_pairs={{0,16},{1,17},{2,18},{3,19},{4,20},{5,21},{6,22},{7,23},{8,24},{9,... | collective-permute-start | bytes 396296 | tf_op jit(solution)/shard_map/ppermute | solution.py:411
  56.3 0.4 collective-permute-start.11
  56.6 0.0 collective-permute-done.13
  56.7 5.4 %collective-permute-done.11 = f32[258,128]{1,0:T(8,128)S(1)} collective-permute-done((f32[258,128]{1,0:T(8,128)S(1)}, f32[258,128]{1,0:T(8,128)S(1)}, u32[]{:S(2)}, u32[]{:S(2)}) %collective-permute-start.11) | collective-permute-done | bytes 132128 | tf_op jit(solution)/shard_map/ppermute | solution.py:411
  62.2 0.4 collective-permute-start.14
  62.6 0.5 collective-permute-start.12
  63.1 3.4 %collective-permute-done.14 = f32[129,128]{1,0:T(8,128)S(1)} collective-permute-done((f32[129,128]{1,0:T(8,128)S(1)}, f32[129,128]{1,0:T(8,128)S(1)}, u32[]{:S(2)}, u32[]{:S(2)}) %collective-permute-start.14) | collective-permute-done | bytes 66080 | tf_op jit(solution)/shard_map/ppermute | solution.py:411
  66.6 0.3 collective-permute-done.12
  66.9 0.0 collective-permute-done.9.refs_1_
  66.9 0.0 collective-permute-done.8.refs_0_
  67.0 0.9 %shard_map.85 = (f32[256,128]{1,0:T(8,128)}, f32[2,128]{1,0:T(2,128)}) custom-call(f32[258,128]{1,0:T(8,128)S(1)} %collective-permute-done.8.refs_0_, f32[258,128]{1,0:T(8,128)S(1)} %collective-permute-done.9.refs_1_, f32[258,128]{1,0:T(8,128)S(1)} %pad_maximum_fusion.6.refs_2_), custom_call_target="tpu_custom_call" | custom-call | tf_op jit(solution)/shard_map/pallas_call | solution.py:320
  (37 shorter events, 0.4 us)
Async XLA Ops:
  1.6 5.7 %collective-permute-start = (f32[136,128]{1,0:T(8,128)S(1)}, f32[136,128]{1,0:T(8,128)S(1)}, u32[]{:S(2)}, u32[]{:S(2)}) collective-permute-start(f32[136,128]{1,0:T(8,128)S(1)} %get-tuple-element.22), channel_id=1, source_target_pairs={{0,8},{1,9},{2,10},{3,11},{4,12},{5,13},{6,14},{7,15},{8,0},{9,1},... | collective-permute-start | bytes 208904 | tf_op jit(solution)/shard_map/ppermute | solution.py:356
  4.7 7.5 %collective-permute-start.1 = (f32[136,128]{1,0:T(8,128)S(1)}, f32[136,128]{1,0:T(8,128)S(1)}, u32[]{:S(2)}, u32[]{:S(2)}) collective-permute-start(f32[136,128]{1,0:T(8,128)S(1)} %get-tuple-element.23), channel_id=1, source_target_pairs={{0,16},{1,17},{2,18},{3,19},{4,20},{5,21},{6,22},{7,23},{8,24},{9,... | collective-permute-start | bytes 208904 | tf_op jit(solution)/shard_map/ppermute | solution.py:356
  7.3 6.2 %collective-permute-start.2 = (f32[136,128]{1,0:T(8,128)S(1)}, f32[136,128]{1,0:T(8,128)S(1)}, u32[]{:S(2)}, u32[]{:S(2)}) collective-permute-start(f32[136,128]{1,0:T(8,128)S(1)} %get-tuple-element.24), channel_id=1, source_target_pairs={{0,24},{1,25},{2,26},{3,27},{4,28},{5,29},{6,30},{7,31},{8,16},{9,... | collective-permute-start | bytes 208904 | tf_op jit(solution)/shard_map/ppermute | solution.py:356
  19.8 4.3 %collective-permute-start.3 = (f32[4168,128]{1,0:T(8,128)S(1)}, f32[4168,128]{1,0:T(8,128)S(1)}, u32[]{:S(2)}, u32[]{:S(2)}) collective-permute-start(f32[4168,128]{1,0:T(8,128)S(1)} %get-tuple-element.25), channel_id=1, source_target_pairs={{0,1},{1,0},{2,3},{3,2},{4,5},{5,4},{6,7},{7,6},{8,9},{9,8},{10,11... | collective-permute-start | bytes 6402056 | tf_op jit(solution)/shard_map/ppermute | solution.py:382
  25.2 8.8 %collective-permute-start.6 = (f32[516,128]{1,0:T(8,128)S(1)}, f32[516,128]{1,0:T(8,128)S(1)}, u32[]{:S(2)}, u32[]{:S(2)}) collective-permute-start(f32[516,128]{1,0:T(8,128)S(1)} %get-tuple-element.36), channel_id=1, source_target_pairs={{0,4},{1,5},{2,6},{3,7},{4,0},{5,1},{6,2},{7,3},{8,12},{9,13},{10,... | collective-permute-start | bytes 792584 | tf_op jit(solution)/shard_map/ppermute | solution.py:411
  26.8 8.6 %collective-permute-start.4 = (f32[516,128]{1,0:T(8,128)S(1)}, f32[516,128]{1,0:T(8,128)S(1)}, u32[]{:S(2)}, u32[]{:S(2)}) collective-permute-start(f32[516,128]{1,0:T(8,128)S(1)} %get-tuple-element.34), channel_id=1, source_target_pairs={{0,2},{1,3},{2,0},{3,1},{4,6},{5,7},{6,4},{7,5},{8,10},{9,11},{10,... | collective-permute-start | bytes 792584 | tf_op jit(solution)/shard_map/ppermute | solution.py:411
  35.5 5.1 %collective-permute-start.5 = (f32[258,128]{1,0:T(8,128)S(1)}, f32[258,128]{1,0:T(8,128)S(1)}, u32[]{:S(2)}, u32[]{:S(2)}) collective-permute-start(f32[258,128]{1,0:T(8,128)S(1)} %get-tuple-element.52), channel_id=1, source_target_pairs={{0,4},{1,5},{2,6},{3,7},{4,0},{5,1},{6,2},{7,3},{8,12},{9,13},{10,... | collective-permute-start | bytes 396296 | tf_op jit(solution)/shard_map/ppermute | solution.py:411
  36.5 13.8 %collective-permute-start.10 = (f32[1032,128]{1,0:T(8,128)S(1)}, f32[1032,128]{1,0:T(8,128)S(1)}, u32[]{:S(2)}, u32[]{:S(2)}) collective-permute-start(f32[1032,128]{1,0:T(8,128)S(1)} %shard_map.81), channel_id=1, source_target_pairs={{0,8},{1,9},{2,10},{3,11},{4,12},{5,13},{6,14},{7,15},{8,0},{9,1},... | collective-permute-start | bytes 1585160 | tf_op jit(solution)/shard_map/ppermute | solution.py:411
  36.9 5.3 %collective-permute-start.7 = (f32[258,128]{1,0:T(8,128)S(1)}, f32[258,128]{1,0:T(8,128)S(1)}, u32[]{:S(2)}, u32[]{:S(2)}) collective-permute-start(f32[258,128]{1,0:T(8,128)S(1)} %get-tuple-element.53), channel_id=1, source_target_pairs={{0,2},{1,3},{2,0},{3,1},{4,6},{5,7},{6,4},{7,5},{8,10},{9,11},{10,... | collective-permute-start | bytes 396296 | tf_op jit(solution)/shard_map/ppermute | solution.py:411
  42.3 24.6 %collective-permute-start.9 = (f32[258,128]{1,0:T(8,128)S(1)}, f32[258,128]{1,0:T(8,128)S(1)}, u32[]{:S(2)}, u32[]{:S(2)}) collective-permute-start(f32[258,128]{1,0:T(8,128)S(1)} %pad_maximum_fusion.3), channel_id=1, source_target_pairs={{0,24},{1,25},{2,26},{3,27},{4,28},{5,29},{6,30},{7,31},{8,16},{9,... | collective-permute-start | bytes 396296 | tf_op jit(solution)/shard_map/ppermute | solution.py:411
  50.5 6.2 %collective-permute-start.13 = (f32[258,128]{1,0:T(8,128)S(1)}, f32[258,128]{1,0:T(8,128)S(1)}, u32[]{:S(2)}, u32[]{:S(2)}) collective-permute-start(f32[258,128]{1,0:T(8,128)S(1)} %pad_maximum_fusion.5), channel_id=1, source_target_pairs={{0,4},{1,5},{2,6},{3,7},{4,0},{5,1},{6,2},{7,3},{8,12},{9,13},{10,... | collective-permute-start | bytes 396296 | tf_op jit(solution)/shard_map/ppermute | solution.py:411
  51.5 15.4 %collective-permute-start.8 = (f32[258,128]{1,0:T(8,128)S(1)}, f32[258,128]{1,0:T(8,128)S(1)}, u32[]{:S(2)}, u32[]{:S(2)}) collective-permute-start(f32[258,128]{1,0:T(8,128)S(1)} %pad_maximum_fusion.2), channel_id=1, source_target_pairs={{0,16},{1,17},{2,18},{3,19},{4,20},{5,21},{6,22},{7,23},{8,24},{9,... | collective-permute-start | bytes 396296 | tf_op jit(solution)/shard_map/ppermute | solution.py:411
  56.3 5.8 %collective-permute-start.11 = (f32[258,128]{1,0:T(8,128)S(1)}, f32[258,128]{1,0:T(8,128)S(1)}, u32[]{:S(2)}, u32[]{:S(2)}) collective-permute-start(f32[258,128]{1,0:T(8,128)S(1)} %pad_maximum_fusion.4), channel_id=1, source_target_pairs={{0,2},{1,3},{2,0},{3,1},{4,6},{5,7},{6,4},{7,5},{8,10},{9,11},{10,... | collective-permute-start | bytes 396296 | tf_op jit(solution)/shard_map/ppermute | solution.py:411
  62.2 4.4 %collective-permute-start.14 = (f32[129,128]{1,0:T(8,128)S(1)}, f32[129,128]{1,0:T(8,128)S(1)}, u32[]{:S(2)}, u32[]{:S(2)}) collective-permute-start(f32[129,128]{1,0:T(8,128)S(1)} %pad_maximum_fusion.9), channel_id=1, source_target_pairs={{0,2},{1,3},{2,0},{3,1},{4,6},{5,7},{6,4},{7,5},{8,10},{9,11},{10,... | collective-permute-start | bytes 198152 | tf_op jit(solution)/shard_map/ppermute | solution.py:411
  62.6 4.3 %collective-permute-start.12 = (f32[129,128]{1,0:T(8,128)S(1)}, f32[129,128]{1,0:T(8,128)S(1)}, u32[]{:S(2)}, u32[]{:S(2)}) collective-permute-start(f32[129,128]{1,0:T(8,128)S(1)} %pad_maximum_fusion.8), channel_id=1, source_target_pairs={{0,4},{1,5},{2,6},{3,7},{4,0},{5,1},{6,2},{7,3},{8,12},{9,13},{10,... | collective-permute-start | bytes 198152 | tf_op jit(solution)/shard_map/ppermute | solution.py:411

commit v7 on v6

--- a/solution.py
+++ b/solution.py
@@ -101,10 +101,33 @@
         buffer[width + 4 : width + 5, :] = bias_ref[...]
 
 
+def prepare_kernel(plan, x_hbm, keys_hbm, both_ref, codes_ref, x_ref, keys_ref, sems):
+    batches, block, width = x_hbm.shape
+    keys_copy, *x_copies = fetch(
+        ((keys_hbm, keys_ref), *((x_hbm.at[m], x_ref.at[m]) for m in range(batches))),
+        sems,
+    )
+    z = lax.axis_index("section")
+    place = lax.axis_index("rows") >> 1
+    tile = codes_ref.shape[1]
+    keys_copy.wait()
+    for m in range(batches):
+        code = slot_codes(plan, keys_ref[m : m + 1, :], z, place).astype(F32)
+        for q in range(block // tile):
+            at = m * (block // tile) + q
+            codes_ref[at : at + 1, :] = code[:, q * tile : (q + 1) * tile]
+    for m in range(batches):
+        x_copies[m].wait()
+        high, low = split(x_ref[m])
+        both_ref[m * block : (m + 1) * block, :width] = high
+        both_ref[m * block : (m + 1) * block, width:] = low
+
+
 def advance_kernel(
     plan,
-    x_hbm,
-    keys_hbm,
+    batches,
+    both_ref,
+    codes_ref,
     valid_hbm,
     b0,
     b1,
@@ -115,8 +138,6 @@
     own_lines,
     weight,
     bias,
-    x_ref,
-    keys_ref,
     valid_ref,
     bytes_,
     sparse,
@@ -124,15 +145,11 @@
     out_lines,
     sems,
 ):
-    batches, block, width = x_hbm.shape
-    keys_copy, valid_copy, *x_copies = fetch(
-        ((keys_hbm, keys_ref), (valid_hbm, valid_ref), *((x_hbm.at[m], x_ref.at[m]) for m in range(batches))),
-        sems,
-    )
+    block, width = both_ref.shape[0] // batches, both_ref.shape[1] // 2
+    (valid_copy,) = fetch(((valid_hbm, valid_ref),), sems)
     z = lax.axis_index("section")
     row = lax.axis_index("rows")
     core = row & 1
-    place = row >> 1
     for k, buffer in enumerate((b0, b1, b2, b3)):
         level = z ^ k
         high, low = split(buffer[:width, :])
@@ -149,9 +166,8 @@
     spread = (iota((LANES, block), 0) == (iota((LANES, block), 1) >> 5)).astype(F32).astype(BF16)
     found = jnp.dot(words, spread, preferred_element_type=F32).astype(jnp.int32)
     which = (lane >> 3) & 3
-    keys_copy.wait()
     valid_copy.wait()
-    tile = sparse.shape[2]
+    tile = sparse.shape[1]
     per_batch = block // tile
     for m in range(batches):
         flags = []
@@ -165,14 +181,12 @@
         for flag in flags[-2::-1]:
             depth = flag * (1 + depth)
         depth = jnp.where(lane < valid_ref[:, m : m + 1], depth, 0).astype(F32)
-        code = slot_codes(plan, keys_ref[m : m + 1, :], z, place).astype(F32)
         for q in range(per_batch):
             at = m * per_batch + q
-            sparse[0, at : at + 1, :] = depth[:, q * tile : (q + 1) * tile]
-            sparse[1, at : at + 1, :] = code[:, q * tile : (q + 1) * tile]
-
-    depths = sparse[0]
-    here = jnp.where(sparse[1] >= plan.half, 1.0, 0.0) == core.astype(F32)
+            sparse[at : at + 1, :] = depth[:, q * tile : (q + 1) * tile]
+
+    depths = sparse[...]
+    here = jnp.where(codes_ref[...] >= plan.half, 1.0, 0.0) == core.astype(F32)
     before = (iota((tile, tile), 0) < iota((tile, tile), 1)).astype(F32).astype(BF16)
     lists = []
     for same in (here, jnp.logical_not(here)):
@@ -188,19 +202,18 @@
             lines_ref[i] = empty
     offsets = [0, 0]
     for m in range(batches):
-        x_copies[m].wait()
         for q in range(per_batch):
             at = m * per_batch + q
             spots = iota((tile, tile), 0).astype(F32)
             moves = [jnp.where(places[at : at + 1] == spots, 1.0, 0.0).astype(BF16) for _, places in lists]
             move = jnp.concatenate(moves, axis=0)
-            both = jnp.concatenate(split(x_ref[m, q * tile : (q + 1) * tile, :]), axis=1)
+            both = both_ref[at * tile : (at + 1) * tile, :]
             moved = jnp.dot(move, both, preferred_element_type=F32)
             moved = moved[:, :width] + moved[:, width:]
-            code = sparse[1, at : at + 1, :] + 1.0
+            code = codes_ref[at : at + 1, :] + 1.0
             high = jnp.floor(code * (1.0 / LANES))
             info = jnp.where(row8 == 0, high, jnp.where(row8 == 1, code - high * LANES, 0.0))
-            info = jnp.where(row8 == 2, sparse[0, at : at + 1, :], info).astype(BF16)
+            info = jnp.where(row8 == 2, sparse[at : at + 1, :], info).astype(BF16)
             infos = lax.dot_general(info, move, (((1,), (1,)), ((), ())), preferred_element_type=F32)
             for l, (live, _) in enumerate(lists):
                 offset = offsets[l]
@@ -359,25 +372,35 @@
     tables = plan.half // LANES
     tile = min(256, block)
     listed = (shape(rows + LEVEL, width), shape(lines + LEVEL // LANES + 1, 8, LANES))
+    both, codes = call(
+        functools.partial(prepare_kernel, plan),
+        (jax.ShapeDtypeStruct((rows, 2 * width), BF16), shape(rows // tile, tile)),
+        (rows_data, row_keys),
+        scratch=[
+            pltpu.VMEM((batches, block, width), F32),
+            pltpu.VMEM((batches, block), jnp.int32),
+            pltpu.SemaphoreType.DMA((batches + 1,)),
+        ],
+        hbm=(0, 1),
+        limit=8,
+    )
     given, *mine = call(
-        functools.partial(advance_kernel, plan),
+        functools.partial(advance_kernel, plan, batches),
         (
             shape(rows + lines + tables + 8, width),
             *listed,
             jax.ShapeDtypeStruct((SECTIONS, 2 * width, 2 * width), BF16),
             shape(SECTIONS, 8, width),
         ),
-        (rows_data, row_keys, valid_counts.reshape(1, batches), *buffers),
+        (both, codes, valid_counts.reshape(1, batches), *buffers),
         scratch=[
-            pltpu.VMEM((batches, block, width), F32),
-            pltpu.VMEM((batches, block), jnp.int32),
             pltpu.VMEM((1, batches), jnp.int32),
             pltpu.VMEM((SECTIONS, 8, LANES), F32),
-            pltpu.VMEM((2, rows // tile, tile), F32),
+            pltpu.VMEM((rows // tile, tile), F32),
             *(pltpu.VMEM(one.shape, F32) for one in listed),
-            pltpu.SemaphoreType.DMA((batches + 2,)),
+            pltpu.SemaphoreType.DMA((1,)),
         ],
-        hbm=(0, 1, 2),
+        hbm=(2,),
     )
     other = lax.ppermute(given, axes, plan.perm(1, 0))
     own, count = call(

time: 68.1 us -> 67.4 us (0.990)
  waiting for transfers between devices: 26.4 us -> 24.7 us
  Pallas kernels: 17.6 us -> 18.6 us
    ppermute x3, waiting for transfers between devices: 6.2 us -> 4.5 us  [shards(): buffers.append(lax.ppermute(packed[k], axes, plan.perm(0, k)))]
    pallas_call x9 -> x10, Pallas kernels: 17.6 us -> 18.6 us  [call(): pl.pallas_call(kernel, out_shape=out_shape, in_specs=[HBM if i in hbm els...]
  transfers between devices with their start and end apart: 15 -> 15, of which waited for: 11 -> 11; matrix products, arithmetic and copies ran while one was open for 1% -> 1% of each run, Pallas kernels for 12% -> 15%
where the time goes in v7:
time: 67.4 us; the launch traced here: 67.1 us
  waiting for transfers between devices  24.7 us (37%)
  starting transfers between devices  22.4 us (33%)
  Pallas kernels  18.6 us (28%)
  between operations  0.94 us (1%)
    ppermute x11, waiting for transfers between devices, send(): return lax.ppermute(message, axes, plan.perm(row_xor, section_xor))  18.9 us
    pallas_call x10, Pallas kernels, call(): pl.pallas_call(kernel, out_shape=out_shape, in_specs=[HBM if i in hbm els...  18.6 us
    ppermute x11, starting transfers between devices, send(): return lax.ppermute(message, axes, plan.perm(row_xor, section_xor))  16.6 us
    ppermute x3, starting transfers between devices, shards(): buffers.append(lax.ppermute(packed[k], axes, plan.perm(0, k)))  5.71 us
    ppermute x3, waiting for transfers between devices, shards(): buffers.append(lax.ppermute(packed[k], axes, plan.perm(0, k)))  4.5 us
  transfers between devices with their start and end apart: 15, of which 11 were waited for; matrix products, arithmetic and copies ran while one was open for 1% of the time, Pallas kernels for 15%

profile of v7, /device:TPU:0, one launch (start us, length us, event | category | flops | bytes accessed | tf_op | source)
XLA Modules:
  0.0 67.1 jit_solution(5059197520192509381)
XLA Ops:
  0.6 1.0 %shard_map.78 = (f32[136,128]{1,0:T(8,128)S(1)}, f32[136,128]{1,0:T(8,128)S(1)}, f32[136,128]{1,0:T(8,128)S(1)}, f32[136,128]{1,0:T(8,128)S(1)}) custom-call(s32[1,16,32]{2,1,0:T(8,128)} %predicates_hbm.1, f32[1,128,128]{2,1,0:T(8,128)} %weight_hbm.1, f32[1,128]{1,0:T(1,128)} %bias_hbm.1), custom_call_target="tpu_custom_call" | custom-call | tf_op jit(solution)/shard_map/pallas_call | solution.py:333
  1.6 3.1 %collective-permute-start = (f32[136,128]{1,0:T(8,128)S(1)}, f32[136,128]{1,0:T(8,128)S(1)}, u32[]{:S(2)}, u32[]{:S(2)}) collective-permute-start(f32[136,128]{1,0:T(8,128)S(1)} %get-tuple-element.26), channel_id=1, source_target_pairs={{0,8},{1,9},{2,10},{3,11},{4,12},{5,13},{6,14},{7,15},{8,0},{9,1},... | collective-permute-start | bytes 208904 | tf_op jit(solution)/shard_map/ppermute | solution.py:369
  4.7 2.6 %collective-permute-start.1 = (f32[136,128]{1,0:T(8,128)S(1)}, f32[136,128]{1,0:T(8,128)S(1)}, u32[]{:S(2)}, u32[]{:S(2)}) collective-permute-start(f32[136,128]{1,0:T(8,128)S(1)} %get-tuple-element.27), channel_id=1, source_target_pairs={{0,16},{1,17},{2,18},{3,19},{4,20},{5,21},{6,22},{7,23},{8,24},{9,... | collective-permute-start | bytes 208904 | tf_op jit(solution)/shard_map/ppermute | solution.py:369
  7.3 0.0 collective-permute-start.2
  7.3 1.7 %shard_map.77 = (bf16[4096,256]{1,0:T(8,128)(2,1)S(1)}, f32[16,256]{1,0:T(8,128)S(1)}) custom-call(f32[4,1024,128]{2,1,0:T(8,128)} %x_hbm.1, s32[4,1024]{1,0:T(4,128)} %keys_hbm.1), custom_call_target="tpu_custom_call" | custom-call | tf_op jit(solution)/shard_map/pallas_call | solution.py:333
  9.0 0.0 collective-permute-done.b1
  9.0 3.2 %collective-permute-done.1.b2 = f32[136,128]{1,0:T(8,128)S(1)} collective-permute-done((f32[136,128]{1,0:T(8,128)S(1)}, f32[136,128]{1,0:T(8,128)S(1)}, u32[]{:S(2)}, u32[]{:S(2)}) %collective-permute-start.1) | collective-permute-done | bytes 69664 | tf_op jit(solution)/shard_map/ppermute | solution.py:369
  12.2 1.3 %collective-permute-done.2.b3 = f32[136,128]{1,0:T(8,128)S(1)} collective-permute-done((f32[136,128]{1,0:T(8,128)S(1)}, f32[136,128]{1,0:T(8,128)S(1)}, u32[]{:S(2)}, u32[]{:S(2)}) %collective-permute-start.2) | collective-permute-done | bytes 69664 | tf_op jit(solution)/shard_map/ppermute | solution.py:369
  13.5 5.6 %shard_map.79 = (f32[4168,128]{1,0:T(8,128)S(1)}, f32[5120,128]{1,0:T(8,128)S(1)}, f32[41,8,128]{2,1,0:T(8,128)S(1)}, bf16[4,256,256]{2,1,0:T(8,128)(2,1)S(1)}, f32[4,8,128]{2,1,0:T(8,128)S(1)}) custom-call(bf16[4096,256]{1,0:T(8,128)(2,1)S(1)} %get-tuple-element.23.both_ref, f32[16,256]{1,0:T(8,128)S(1)} %get-tuple-element.24.codes_ref, s32[1,4]{1,0:T(1,128)} %bitcast.63, ...), custom_call_target="tpu_custom_call" | custom-call | tf_op jit(solution)/shard_map/pallas_call | solution.py:333
  19.2 0.1 collective-permute-start.3
  19.2 1.2 %shard_map.80 = (f32[4136,128]{1,0:T(8,128)S(1)}, f32[32,128]{1,0:T(8,128)S(1)}) custom-call(f32[5120,128]{1,0:T(8,128)S(1)} %get-tuple-element.30.packed, f32[41,8,128]{2,1,0:T(8,128)S(1)} %get-tuple-element.31.lines_ref, bf16[4,256,256]{2,1,0:T(8,128)(2,1)S(1)} %get-tuple-element.32.weight, f32[4,8,128]{2,1,0:T(8,128)S(1)} %get-tuple-element.33.bias), custom_call_target="tpu_custom_call" | custom-call | tf_op jit(solution)/shard_map/pallas_call | solution.py:333
  20.4 1.7 %shard_map.81.mine_ref = f32[2048,128]{1,0:T(8,128)S(1)} custom-call(f32[4136,128]{1,0:T(8,128)S(1)} %get-tuple-element.34.own_ref.mine_ref), custom_call_target="tpu_custom_call" | custom-call | tf_op jit(solution)/shard_map/pallas_call | solution.py:333
  22.2 1.3 %collective-permute-done.3.other_ref = f32[4168,128]{1,0:T(8,128)S(1)} collective-permute-done((f32[4168,128]{1,0:T(8,128)S(1)}, f32[4168,128]{1,0:T(8,128)S(1)}, u32[]{:S(2)}, u32[]{:S(2)}) %collective-permute-start.3) | collective-permute-done | bytes 2134048 | tf_op jit(solution)/shard_map/ppermute | solution.py:405
  23.4 1.1 %shard_map.84 = (f32[516,128]{1,0:T(8,128)S(1)}, f32[516,128]{1,0:T(8,128)S(1)}) custom-call(f32[4168,128]{1,0:T(8,128)S(1)} %collective-permute-done.3.other_ref, f32[2048,128]{1,0:T(8,128)S(1)} %shard_map.81.mine_ref, f32[32,128]{1,0:T(8,128)S(1)} %get-tuple-element.41.count_ref), custom_call_target="tpu_custom_call" | custom-call | tf_op jit(solution)/shard_map/pallas_call | solution.py:333
  24.6 1.6 %collective-permute-start.6 = (f32[516,128]{1,0:T(8,128)S(1)}, f32[516,128]{1,0:T(8,128)S(1)}, u32[]{:S(2)}, u32[]{:S(2)}) collective-permute-start(f32[516,128]{1,0:T(8,128)S(1)} %get-tuple-element.40), channel_id=1, source_target_pairs={{0,4},{1,5},{2,6},{3,7},{4,0},{5,1},{6,2},{7,3},{8,12},{9,13},{10,... | collective-permute-start | bytes 792584 | tf_op jit(solution)/shard_map/ppermute | solution.py:434
  26.2 1.5 %collective-permute-start.4 = (f32[516,128]{1,0:T(8,128)S(1)}, f32[516,128]{1,0:T(8,128)S(1)}, u32[]{:S(2)}, u32[]{:S(2)}) collective-permute-start(f32[516,128]{1,0:T(8,128)S(1)} %get-tuple-element.38), channel_id=1, source_target_pairs={{0,2},{1,3},{2,0},{3,1},{4,6},{5,7},{6,4},{7,5},{8,10},{9,11},{10,... | collective-permute-start | bytes 792584 | tf_op jit(solution)/shard_map/ppermute | solution.py:434
  27.6 1.1 %shard_map.82 = f32[1032,128]{1,0:T(8,128)S(1)} custom-call(f32[4168,128]{1,0:T(8,128)S(1)} %collective-permute-done.3.other_ref, f32[2048,128]{1,0:T(8,128)S(1)} %shard_map.81.mine_ref, f32[32,128]{1,0:T(8,128)S(1)} %get-tuple-element.41.count_ref), custom_call_target="tpu_custom_call" | custom-call | tf_op jit(solution)/shard_map/pallas_call | solution.py:333
  28.8 2.1 %shard_map.83 = (f32[516,128]{1,0:T(8,128)S(1)}, f32[516,128]{1,0:T(8,128)S(1)}) custom-call(f32[4168,128]{1,0:T(8,128)S(1)} %collective-permute-done.3.other_ref, f32[4136,128]{1,0:T(8,128)S(1)} %get-tuple-element.34.own_ref.mine_ref, f32[32,128]{1,0:T(8,128)S(1)} %get-tuple-element.41.count_ref), custom_call_target="tpu_custom_call" | custom-call | tf_op jit(solution)/shard_map/pallas_call | solution.py:333
  30.9 2.5 %collective-permute-done.6 = f32[516,128]{1,0:T(8,128)S(1)} collective-permute-done((f32[516,128]{1,0:T(8,128)S(1)}, f32[516,128]{1,0:T(8,128)S(1)}, u32[]{:S(2)}, u32[]{:S(2)}) %collective-permute-start.6) | collective-permute-done | bytes 264224 | tf_op jit(solution)/shard_map/ppermute | solution.py:434
  33.5 1.3 %collective-permute-done.4 = f32[516,128]{1,0:T(8,128)S(1)} collective-permute-done((f32[516,128]{1,0:T(8,128)S(1)}, f32[516,128]{1,0:T(8,128)S(1)}, u32[]{:S(2)}, u32[]{:S(2)}) %collective-permute-start.4) | collective-permute-done | bytes 264224 | tf_op jit(solution)/shard_map/ppermute | solution.py:434
  34.9 1.0 %collective-permute-start.5 = (f32[258,128]{1,0:T(8,128)S(1)}, f32[258,128]{1,0:T(8,128)S(1)}, u32[]{:S(2)}, u32[]{:S(2)}) collective-permute-start(f32[258,128]{1,0:T(8,128)S(1)} %get-tuple-element.56), channel_id=1, source_target_pairs={{0,4},{1,5},{2,6},{3,7},{4,0},{5,1},{6,2},{7,3},{8,12},{9,13},{10,... | collective-permute-start | bytes 396296 | tf_op jit(solution)/shard_map/ppermute | solution.py:434
  35.9 0.4 collective-permute-start.10
  36.2 1.5 %collective-permute-start.7 = (f32[258,128]{1,0:T(8,128)S(1)}, f32[258,128]{1,0:T(8,128)S(1)}, u32[]{:S(2)}, u32[]{:S(2)}) collective-permute-start(f32[258,128]{1,0:T(8,128)S(1)} %get-tuple-element.57), channel_id=1, source_target_pairs={{0,2},{1,3},{2,0},{3,1},{4,6},{5,7},{6,4},{7,5},{8,10},{9,11},{10,... | collective-permute-start | bytes 396296 | tf_op jit(solution)/shard_map/ppermute | solution.py:434
  37.7 2.1 %shard_map.85 = f32[1032,128]{1,0:T(8,128)S(1)} custom-call(f32[4168,128]{1,0:T(8,128)S(1)} %collective-permute-done.3.other_ref, f32[4136,128]{1,0:T(8,128)S(1)} %get-tuple-element.34.own_ref.mine_ref, f32[32,128]{1,0:T(8,128)S(1)} %get-tuple-element.41.count_ref), custom_call_target="tpu_custom_call" | custom-call | tf_op jit(solution)/shard_map/pallas_call | solution.py:333
  39.9 0.1 collective-permute-done.5
  40.0 1.6 %collective-permute-done.7 = f32[258,128]{1,0:T(8,128)S(1)} collective-permute-done((f32[258,128]{1,0:T(8,128)S(1)}, f32[258,128]{1,0:T(8,128)S(1)}, u32[]{:S(2)}, u32[]{:S(2)}) %collective-permute-start.7) | collective-permute-done | bytes 132128 | tf_op jit(solution)/shard_map/ppermute | solution.py:434
  41.6 3.7 %collective-permute-start.9 = (f32[258,128]{1,0:T(8,128)S(1)}, f32[258,128]{1,0:T(8,128)S(1)}, u32[]{:S(2)}, u32[]{:S(2)}) collective-permute-start(f32[258,128]{1,0:T(8,128)S(1)} %pad_maximum_fusion.3), channel_id=1, source_target_pairs={{0,24},{1,25},{2,26},{3,27},{4,28},{5,29},{6,30},{7,31},{8,16},{9,... | collective-permute-start | bytes 396296 | tf_op jit(solution)/shard_map/ppermute | solution.py:434
  45.3 4.3 %collective-permute-done.10 = f32[1032,128]{1,0:T(8,128)S(1)} collective-permute-done((f32[1032,128]{1,0:T(8,128)S(1)}, f32[1032,128]{1,0:T(8,128)S(1)}, u32[]{:S(2)}, u32[]{:S(2)}) %collective-permute-start.10) | collective-permute-done | bytes 528416 | tf_op jit(solution)/shard_map/ppermute | solution.py:434
  49.6 0.1 add.61
  49.8 1.0 %collective-permute-start.13 = (f32[258,128]{1,0:T(8,128)S(1)}, f32[258,128]{1,0:T(8,128)S(1)}, u32[]{:S(2)}, u32[]{:S(2)}) collective-permute-start(f32[258,128]{1,0:T(8,128)S(1)} %pad_maximum_fusion.5), channel_id=1, source_target_pairs={{0,4},{1,5},{2,6},{3,7},{4,0},{5,1},{6,2},{7,3},{8,12},{9,13},{10,... | collective-permute-start | bytes 396296 | tf_op jit(solution)/shard_map/ppermute | solution.py:434
  50.8 4.7 %collective-permute-start.8 = (f32[258,128]{1,0:T(8,128)S(1)}, f32[258,128]{1,0:T(8,128)S(1)}, u32[]{:S(2)}, u32[]{:S(2)}) collective-permute-start(f32[258,128]{1,0:T(8,128)S(1)} %pad_maximum_fusion.2), channel_id=1, source_target_pairs={{0,16},{1,17},{2,18},{3,19},{4,20},{5,21},{6,22},{7,23},{8,24},{9,... | collective-permute-start | bytes 396296 | tf_op jit(solution)/shard_map/ppermute | solution.py:434
  55.6 0.4 collective-permute-start.11
  56.0 0.0 collective-permute-done.13
  56.0 5.4 %collective-permute-done.11 = f32[258,128]{1,0:T(8,128)S(1)} collective-permute-done((f32[258,128]{1,0:T(8,128)S(1)}, f32[258,128]{1,0:T(8,128)S(1)}, u32[]{:S(2)}, u32[]{:S(2)}) %collective-permute-start.11) | collective-permute-done | bytes 132128 | tf_op jit(solution)/shard_map/ppermute | solution.py:434
  61.5 0.4 collective-permute-start.14
  61.9 0.5 collective-permute-start.12
  62.4 3.4 %collective-permute-done.14 = f32[129,128]{1,0:T(8,128)S(1)} collective-permute-done((f32[129,128]{1,0:T(8,128)S(1)}, f32[129,128]{1,0:T(8,128)S(1)}, u32[]{:S(2)}, u32[]{:S(2)}) %collective-permute-start.14) | collective-permute-done | bytes 66080 | tf_op jit(solution)/shard_map/ppermute | solution.py:434
  65.9 0.3 collective-permute-done.12
  66.3 0.0 collective-permute-done.9.refs_1_
  66.3 0.0 collective-permute-done.8.refs_0_
  66.3 0.9 %shard_map.86 = (f32[256,128]{1,0:T(8,128)}, f32[2,128]{1,0:T(2,128)}) custom-call(f32[258,128]{1,0:T(8,128)S(1)} %collective-permute-done.8.refs_0_, f32[258,128]{1,0:T(8,128)S(1)} %collective-permute-done.9.refs_1_, f32[258,128]{1,0:T(8,128)S(1)} %pad_maximum_fusion.6.refs_2_), custom_call_target="tpu_custom_call" | custom-call | tf_op jit(solution)/shard_map/pallas_call | solution.py:333
  (37 shorter events, 0.4 us)
Async XLA Ops:
  1.6 7.4 %collective-permute-start = (f32[136,128]{1,0:T(8,128)S(1)}, f32[136,128]{1,0:T(8,128)S(1)}, u32[]{:S(2)}, u32[]{:S(2)}) collective-permute-start(f32[136,128]{1,0:T(8,128)S(1)} %get-tuple-element.26), channel_id=1, source_target_pairs={{0,8},{1,9},{2,10},{3,11},{4,12},{5,13},{6,14},{7,15},{8,0},{9,1},... | collective-permute-start | bytes 208904 | tf_op jit(solution)/shard_map/ppermute | solution.py:369
  4.7 7.5 %collective-permute-start.1 = (f32[136,128]{1,0:T(8,128)S(1)}, f32[136,128]{1,0:T(8,128)S(1)}, u32[]{:S(2)}, u32[]{:S(2)}) collective-permute-start(f32[136,128]{1,0:T(8,128)S(1)} %get-tuple-element.27), channel_id=1, source_target_pairs={{0,16},{1,17},{2,18},{3,19},{4,20},{5,21},{6,22},{7,23},{8,24},{9,... | collective-permute-start | bytes 208904 | tf_op jit(solution)/shard_map/ppermute | solution.py:369
  7.3 6.2 %collective-permute-start.2 = (f32[136,128]{1,0:T(8,128)S(1)}, f32[136,128]{1,0:T(8,128)S(1)}, u32[]{:S(2)}, u32[]{:S(2)}) collective-permute-start(f32[136,128]{1,0:T(8,128)S(1)} %get-tuple-element.28), channel_id=1, source_target_pairs={{0,24},{1,25},{2,26},{3,27},{4,28},{5,29},{6,30},{7,31},{8,16},{9,... | collective-permute-start | bytes 208904 | tf_op jit(solution)/shard_map/ppermute | solution.py:369
  19.2 4.3 %collective-permute-start.3 = (f32[4168,128]{1,0:T(8,128)S(1)}, f32[4168,128]{1,0:T(8,128)S(1)}, u32[]{:S(2)}, u32[]{:S(2)}) collective-permute-start(f32[4168,128]{1,0:T(8,128)S(1)} %get-tuple-element.29), channel_id=1, source_target_pairs={{0,1},{1,0},{2,3},{3,2},{4,5},{5,4},{6,7},{7,6},{8,9},{9,8},{10,11... | collective-permute-start | bytes 6402056 | tf_op jit(solution)/shard_map/ppermute | solution.py:405
  24.6 8.8 %collective-permute-start.6 = (f32[516,128]{1,0:T(8,128)S(1)}, f32[516,128]{1,0:T(8,128)S(1)}, u32[]{:S(2)}, u32[]{:S(2)}) collective-permute-start(f32[516,128]{1,0:T(8,128)S(1)} %get-tuple-element.40), channel_id=1, source_target_pairs={{0,4},{1,5},{2,6},{3,7},{4,0},{5,1},{6,2},{7,3},{8,12},{9,13},{10,... | collective-permute-start | bytes 792584 | tf_op jit(solution)/shard_map/ppermute | solution.py:434
  26.2 8.6 %collective-permute-start.4 = (f32[516,128]{1,0:T(8,128)S(1)}, f32[516,128]{1,0:T(8,128)S(1)}, u32[]{:S(2)}, u32[]{:S(2)}) collective-permute-start(f32[516,128]{1,0:T(8,128)S(1)} %get-tuple-element.38), channel_id=1, source_target_pairs={{0,2},{1,3},{2,0},{3,1},{4,6},{5,7},{6,4},{7,5},{8,10},{9,11},{10,... | collective-permute-start | bytes 792584 | tf_op jit(solution)/shard_map/ppermute | solution.py:434
  34.9 5.1 %collective-permute-start.5 = (f32[258,128]{1,0:T(8,128)S(1)}, f32[258,128]{1,0:T(8,128)S(1)}, u32[]{:S(2)}, u32[]{:S(2)}) collective-permute-start(f32[258,128]{1,0:T(8,128)S(1)} %get-tuple-element.56), channel_id=1, source_target_pairs={{0,4},{1,5},{2,6},{3,7},{4,0},{5,1},{6,2},{7,3},{8,12},{9,13},{10,... | collective-permute-start | bytes 396296 | tf_op jit(solution)/shard_map/ppermute | solution.py:434
  35.9 13.8 %collective-permute-start.10 = (f32[1032,128]{1,0:T(8,128)S(1)}, f32[1032,128]{1,0:T(8,128)S(1)}, u32[]{:S(2)}, u32[]{:S(2)}) collective-permute-start(f32[1032,128]{1,0:T(8,128)S(1)} %shard_map.82), channel_id=1, source_target_pairs={{0,8},{1,9},{2,10},{3,11},{4,12},{5,13},{6,14},{7,15},{8,0},{9,1},... | collective-permute-start | bytes 1585160 | tf_op jit(solution)/shard_map/ppermute | solution.py:434
  36.2 5.3 %collective-permute-start.7 = (f32[258,128]{1,0:T(8,128)S(1)}, f32[258,128]{1,0:T(8,128)S(1)}, u32[]{:S(2)}, u32[]{:S(2)}) collective-permute-start(f32[258,128]{1,0:T(8,128)S(1)} %get-tuple-element.57), channel_id=1, source_target_pairs={{0,2},{1,3},{2,0},{3,1},{4,6},{5,7},{6,4},{7,5},{8,10},{9,11},{10,... | collective-permute-start | bytes 396296 | tf_op jit(solution)/shard_map/ppermute | solution.py:434
  41.6 24.6 %collective-permute-start.9 = (f32[258,128]{1,0:T(8,128)S(1)}, f32[258,128]{1,0:T(8,128)S(1)}, u32[]{:S(2)}, u32[]{:S(2)}) collective-permute-start(f32[258,128]{1,0:T(8,128)S(1)} %pad_maximum_fusion.3), channel_id=1, source_target_pairs={{0,24},{1,25},{2,26},{3,27},{4,28},{5,29},{6,30},{7,31},{8,16},{9,... | collective-permute-start | bytes 396296 | tf_op jit(solution)/shard_map/ppermute | solution.py:434
  49.8 6.2 %collective-permute-start.13 = (f32[258,128]{1,0:T(8,128)S(1)}, f32[258,128]{1,0:T(8,128)S(1)}, u32[]{:S(2)}, u32[]{:S(2)}) collective-permute-start(f32[258,128]{1,0:T(8,128)S(1)} %pad_maximum_fusion.5), channel_id=1, source_target_pairs={{0,4},{1,5},{2,6},{3,7},{4,0},{5,1},{6,2},{7,3},{8,12},{9,13},{10,... | collective-permute-start | bytes 396296 | tf_op jit(solution)/shard_map/ppermute | solution.py:434
  50.8 15.4 %collective-permute-start.8 = (f32[258,128]{1,0:T(8,128)S(1)}, f32[258,128]{1,0:T(8,128)S(1)}, u32[]{:S(2)}, u32[]{:S(2)}) collective-permute-start(f32[258,128]{1,0:T(8,128)S(1)} %pad_maximum_fusion.2), channel_id=1, source_target_pairs={{0,16},{1,17},{2,18},{3,19},{4,20},{5,21},{6,22},{7,23},{8,24},{9,... | collective-permute-start | bytes 396296 | tf_op jit(solution)/shard_map/ppermute | solution.py:434
  55.6 5.8 %collective-permute-start.11 = (f32[258,128]{1,0:T(8,128)S(1)}, f32[258,128]{1,0:T(8,128)S(1)}, u32[]{:S(2)}, u32[]{:S(2)}) collective-permute-start(f32[258,128]{1,0:T(8,128)S(1)} %pad_maximum_fusion.4), channel_id=1, source_target_pairs={{0,2},{1,3},{2,0},{3,1},{4,6},{5,7},{6,4},{7,5},{8,10},{9,11},{10,... | collective-permute-start | bytes 396296 | tf_op jit(solution)/shard_map/ppermute | solution.py:434
  61.5 4.4 %collective-permute-start.14 = (f32[129,128]{1,0:T(8,128)S(1)}, f32[129,128]{1,0:T(8,128)S(1)}, u32[]{:S(2)}, u32[]{:S(2)}) collective-permute-start(f32[129,128]{1,0:T(8,128)S(1)} %pad_maximum_fusion.9), channel_id=1, source_target_pairs={{0,2},{1,3},{2,0},{3,1},{4,6},{5,7},{6,4},{7,5},{8,10},{9,11},{10,... | collective-permute-start | bytes 198152 | tf_op jit(solution)/shard_map/ppermute | solution.py:434
  61.9 4.3 %collective-permute-start.12 = (f32[129,128]{1,0:T(8,128)S(1)}, f32[129,128]{1,0:T(8,128)S(1)}, u32[]{:S(2)}, u32[]{:S(2)}) collective-permute-start(f32[129,128]{1,0:T(8,128)S(1)} %pad_maximum_fusion.8), channel_id=1, source_target_pairs={{0,4},{1,5},{2,6},{3,7},{4,0},{5,1},{6,2},{7,3},{8,12},{9,13},{10,... | collective-permute-start | bytes 198152 | tf_op jit(solution)/shard_map/ppermute | solution.py:434

commit v8 on v7

--- a/solution.py
+++ b/solution.py
@@ -204,8 +204,10 @@
     for m in range(batches):
         for q in range(per_batch):
             at = m * per_batch + q
-            spots = iota((tile, tile), 0).astype(F32)
-            moves = [jnp.where(places[at : at + 1] == spots, 1.0, 0.0).astype(BF16) for _, places in lists]
+            spots = iota((tile, tile), 0).astype(F32).astype(BF16)
+            moves = [
+                jnp.where(places[at : at + 1].astype(BF16) == spots, BF16(1.0), BF16(0.0)) for _, places in lists
+            ]
             move = jnp.concatenate(moves, axis=0)
             both = both_ref[at * tile : (at + 1) * tile, :]
             moved = jnp.dot(move, both, preferred_element_type=F32)

time: 67.4 us -> 67.4 us (level)
  no operation moved by 1% of the time
where the time goes in v8:
time: 67.4 us; the launch traced here: 67.2 us
  waiting for transfers between devices  24.7 us (37%)
  starting transfers between devices  22.5 us (33%)
  Pallas kernels  18.6 us (28%)
  between operations  0.94 us (1%)
    ppermute x11, waiting for transfers between devices, send(): return lax.ppermute(message, axes, plan.perm(row_xor, section_xor))  18.9 us
    pallas_call x10, Pallas kernels, call(): pl.pallas_call(kernel, out_shape=out_shape, in_specs=[HBM if i in hbm els...  18.6 us
    ppermute x11, starting transfers between devices, send(): return lax.ppermute(message, axes, plan.perm(row_xor, section_xor))  16.7 us
    ppermute x3, starting transfers between devices, shards(): buffers.append(lax.ppermute(packed[k], axes, plan.perm(0, k)))  5.71 us
    ppermute x3, waiting for transfers between devices, shards(): buffers.append(lax.ppermute(packed[k], axes, plan.perm(0, k)))  4.5 us
  transfers between devices with their start and end apart: 15, of which 11 were waited for; matrix products, arithmetic and copies ran while one was open for 1% of the time, Pallas kernels for 15%

profile of v8, /device:TPU:0, one launch (start us, length us, event | category | flops | bytes accessed | tf_op | source)
XLA Modules:
  0.0 67.2 jit_solution(4001052135695144380)
XLA Ops:
  0.6 1.0 %shard_map.78 = (f32[136,128]{1,0:T(8,128)S(1)}, f32[136,128]{1,0:T(8,128)S(1)}, f32[136,128]{1,0:T(8,128)S(1)}, f32[136,128]{1,0:T(8,128)S(1)}) custom-call(s32[1,16,32]{2,1,0:T(8,128)} %predicates_hbm.1, f32[1,128,128]{2,1,0:T(8,128)} %weight_hbm.1, f32[1,128]{1,0:T(1,128)} %bias_hbm.1), custom_call_target="tpu_custom_call" | custom-call | tf_op jit(solution)/shard_map/pallas_call | solution.py:335
  1.6 3.1 %collective-permute-start = (f32[136,128]{1,0:T(8,128)S(1)}, f32[136,128]{1,0:T(8,128)S(1)}, u32[]{:S(2)}, u32[]{:S(2)}) collective-permute-start(f32[136,128]{1,0:T(8,128)S(1)} %get-tuple-element.26), channel_id=1, source_target_pairs={{0,8},{1,9},{2,10},{3,11},{4,12},{5,13},{6,14},{7,15},{8,0},{9,1},... | collective-permute-start | bytes 208904 | tf_op jit(solution)/shard_map/ppermute | solution.py:371
  4.7 2.6 %collective-permute-start.1 = (f32[136,128]{1,0:T(8,128)S(1)}, f32[136,128]{1,0:T(8,128)S(1)}, u32[]{:S(2)}, u32[]{:S(2)}) collective-permute-start(f32[136,128]{1,0:T(8,128)S(1)} %get-tuple-element.27), channel_id=1, source_target_pairs={{0,16},{1,17},{2,18},{3,19},{4,20},{5,21},{6,22},{7,23},{8,24},{9,... | collective-permute-start | bytes 208904 | tf_op jit(solution)/shard_map/ppermute | solution.py:371
  7.3 0.0 collective-permute-start.2
  7.3 1.7 %shard_map.77 = (bf16[4096,256]{1,0:T(8,128)(2,1)S(1)}, f32[16,256]{1,0:T(8,128)S(1)}) custom-call(f32[4,1024,128]{2,1,0:T(8,128)} %x_hbm.1, s32[4,1024]{1,0:T(4,128)} %keys_hbm.1), custom_call_target="tpu_custom_call" | custom-call | tf_op jit(solution)/shard_map/pallas_call | solution.py:335
  9.0 0.0 collective-permute-done.b1
  9.0 3.2 %collective-permute-done.1.b2 = f32[136,128]{1,0:T(8,128)S(1)} collective-permute-done((f32[136,128]{1,0:T(8,128)S(1)}, f32[136,128]{1,0:T(8,128)S(1)}, u32[]{:S(2)}, u32[]{:S(2)}) %collective-permute-start.1) | collective-permute-done | bytes 69664 | tf_op jit(solution)/shard_map/ppermute | solution.py:371
  12.2 1.3 %collective-permute-done.2.b3 = f32[136,128]{1,0:T(8,128)S(1)} collective-permute-done((f32[136,128]{1,0:T(8,128)S(1)}, f32[136,128]{1,0:T(8,128)S(1)}, u32[]{:S(2)}, u32[]{:S(2)}) %collective-permute-start.2) | collective-permute-done | bytes 69664 | tf_op jit(solution)/shard_map/ppermute | solution.py:371
  13.5 5.6 %shard_map.79 = (f32[4168,128]{1,0:T(8,128)S(1)}, f32[5120,128]{1,0:T(8,128)S(1)}, f32[41,8,128]{2,1,0:T(8,128)S(1)}, bf16[4,256,256]{2,1,0:T(8,128)(2,1)S(1)}, f32[4,8,128]{2,1,0:T(8,128)S(1)}) custom-call(bf16[4096,256]{1,0:T(8,128)(2,1)S(1)} %get-tuple-element.23.both_ref, f32[16,256]{1,0:T(8,128)S(1)} %get-tuple-element.24.codes_ref, s32[1,4]{1,0:T(1,128)} %bitcast.63, ...), custom_call_target="tpu_custom_call" | custom-call | tf_op jit(solution)/shard_map/pallas_call | solution.py:335
  19.2 0.1 collective-permute-start.3
  19.2 1.2 %shard_map.80 = (f32[4136,128]{1,0:T(8,128)S(1)}, f32[32,128]{1,0:T(8,128)S(1)}) custom-call(f32[5120,128]{1,0:T(8,128)S(1)} %get-tuple-element.30.packed, f32[41,8,128]{2,1,0:T(8,128)S(1)} %get-tuple-element.31.lines_ref, bf16[4,256,256]{2,1,0:T(8,128)(2,1)S(1)} %get-tuple-element.32.weight, f32[4,8,128]{2,1,0:T(8,128)S(1)} %get-tuple-element.33.bias), custom_call_target="tpu_custom_call" | custom-call | tf_op jit(solution)/shard_map/pallas_call | solution.py:335
  20.4 1.7 %shard_map.81.mine_ref = f32[2048,128]{1,0:T(8,128)S(1)} custom-call(f32[4136,128]{1,0:T(8,128)S(1)} %get-tuple-element.34.own_ref.mine_ref), custom_call_target="tpu_custom_call" | custom-call | tf_op jit(solution)/shard_map/pallas_call | solution.py:335
  22.2 1.3 %collective-permute-done.3.other_ref = f32[4168,128]{1,0:T(8,128)S(1)} collective-permute-done((f32[4168,128]{1,0:T(8,128)S(1)}, f32[4168,128]{1,0:T(8,128)S(1)}, u32[]{:S(2)}, u32[]{:S(2)}) %collective-permute-start.3) | collective-permute-done | bytes 2134048 | tf_op jit(solution)/shard_map/ppermute | solution.py:407
  23.4 1.1 %shard_map.84 = (f32[516,128]{1,0:T(8,128)S(1)}, f32[516,128]{1,0:T(8,128)S(1)}) custom-call(f32[4168,128]{1,0:T(8,128)S(1)} %collective-permute-done.3.other_ref, f32[2048,128]{1,0:T(8,128)S(1)} %shard_map.81.mine_ref, f32[32,128]{1,0:T(8,128)S(1)} %get-tuple-element.41.count_ref), custom_call_target="tpu_custom_call" | custom-call | tf_op jit(solution)/shard_map/pallas_call | solution.py:335
  24.6 1.6 %collective-permute-start.6 = (f32[516,128]{1,0:T(8,128)S(1)}, f32[516,128]{1,0:T(8,128)S(1)}, u32[]{:S(2)}, u32[]{:S(2)}) collective-permute-start(f32[516,128]{1,0:T(8,128)S(1)} %get-tuple-element.40), channel_id=1, source_target_pairs={{0,4},{1,5},{2,6},{3,7},{4,0},{5,1},{6,2},{7,3},{8,12},{9,13},{10,... | collective-permute-start | bytes 792584 | tf_op jit(solution)/shard_map/ppermute | solution.py:436
  26.2 1.5 %collective-permute-start.4 = (f32[516,128]{1,0:T(8,128)S(1)}, f32[516,128]{1,0:T(8,128)S(1)}, u32[]{:S(2)}, u32[]{:S(2)}) collective-permute-start(f32[516,128]{1,0:T(8,128)S(1)} %get-tuple-element.38), channel_id=1, source_target_pairs={{0,2},{1,3},{2,0},{3,1},{4,6},{5,7},{6,4},{7,5},{8,10},{9,11},{10,... | collective-permute-start | bytes 792584 | tf_op jit(solution)/shard_map/ppermute | solution.py:436
  27.7 1.1 %shard_map.82 = f32[1032,128]{1,0:T(8,128)S(1)} custom-call(f32[4168,128]{1,0:T(8,128)S(1)} %collective-permute-done.3.other_ref, f32[2048,128]{1,0:T(8,128)S(1)} %shard_map.81.mine_ref, f32[32,128]{1,0:T(8,128)S(1)} %get-tuple-element.41.count_ref), custom_call_target="tpu_custom_call" | custom-call | tf_op jit(solution)/shard_map/pallas_call | solution.py:335
  28.8 2.1 %shard_map.83 = (f32[516,128]{1,0:T(8,128)S(1)}, f32[516,128]{1,0:T(8,128)S(1)}) custom-call(f32[4168,128]{1,0:T(8,128)S(1)} %collective-permute-done.3.other_ref, f32[4136,128]{1,0:T(8,128)S(1)} %get-tuple-element.34.own_ref.mine_ref, f32[32,128]{1,0:T(8,128)S(1)} %get-tuple-element.41.count_ref), custom_call_target="tpu_custom_call" | custom-call | tf_op jit(solution)/shard_map/pallas_call | solution.py:335
  30.9 2.5 %collective-permute-done.6 = f32[516,128]{1,0:T(8,128)S(1)} collective-permute-done((f32[516,128]{1,0:T(8,128)S(1)}, f32[516,128]{1,0:T(8,128)S(1)}, u32[]{:S(2)}, u32[]{:S(2)}) %collective-permute-start.6) | collective-permute-done | bytes 264224 | tf_op jit(solution)/shard_map/ppermute | solution.py:436
  33.5 1.3 %collective-permute-done.4 = f32[516,128]{1,0:T(8,128)S(1)} collective-permute-done((f32[516,128]{1,0:T(8,128)S(1)}, f32[516,128]{1,0:T(8,128)S(1)}, u32[]{:S(2)}, u32[]{:S(2)}) %collective-permute-start.4) | collective-permute-done | bytes 264224 | tf_op jit(solution)/shard_map/ppermute | solution.py:436
  34.9 1.0 %collective-permute-start.5 = (f32[258,128]{1,0:T(8,128)S(1)}, f32[258,128]{1,0:T(8,128)S(1)}, u32[]{:S(2)}, u32[]{:S(2)}) collective-permute-start(f32[258,128]{1,0:T(8,128)S(1)} %get-tuple-element.56), channel_id=1, source_target_pairs={{0,4},{1,5},{2,6},{3,7},{4,0},{5,1},{6,2},{7,3},{8,12},{9,13},{10,... | collective-permute-start | bytes 396296 | tf_op jit(solution)/shard_map/ppermute | solution.py:436
  35.9 0.3 collective-permute-start.10
  36.2 1.5 %collective-permute-start.7 = (f32[258,128]{1,0:T(8,128)S(1)}, f32[258,128]{1,0:T(8,128)S(1)}, u32[]{:S(2)}, u32[]{:S(2)}) collective-permute-start(f32[258,128]{1,0:T(8,128)S(1)} %get-tuple-element.57), channel_id=1, source_target_pairs={{0,2},{1,3},{2,0},{3,1},{4,6},{5,7},{6,4},{7,5},{8,10},{9,11},{10,... | collective-permute-start | bytes 396296 | tf_op jit(solution)/shard_map/ppermute | solution.py:436
  37.7 2.1 %shard_map.85 = f32[1032,128]{1,0:T(8,128)S(1)} custom-call(f32[4168,128]{1,0:T(8,128)S(1)} %collective-permute-done.3.other_ref, f32[4136,128]{1,0:T(8,128)S(1)} %get-tuple-element.34.own_ref.mine_ref, f32[32,128]{1,0:T(8,128)S(1)} %get-tuple-element.41.count_ref), custom_call_target="tpu_custom_call" | custom-call | tf_op jit(solution)/shard_map/pallas_call | solution.py:335
  39.9 0.1 collective-permute-done.5
  40.0 1.6 %collective-permute-done.7 = f32[258,128]{1,0:T(8,128)S(1)} collective-permute-done((f32[258,128]{1,0:T(8,128)S(1)}, f32[258,128]{1,0:T(8,128)S(1)}, u32[]{:S(2)}, u32[]{:S(2)}) %collective-permute-start.7) | collective-permute-done | bytes 132128 | tf_op jit(solution)/shard_map/ppermute | solution.py:436
  41.6 3.7 %collective-permute-start.9 = (f32[258,128]{1,0:T(8,128)S(1)}, f32[258,128]{1,0:T(8,128)S(1)}, u32[]{:S(2)}, u32[]{:S(2)}) collective-permute-start(f32[258,128]{1,0:T(8,128)S(1)} %pad_maximum_fusion.3), channel_id=1, source_target_pairs={{0,24},{1,25},{2,26},{3,27},{4,28},{5,29},{6,30},{7,31},{8,16},{9,... | collective-permute-start | bytes 396296 | tf_op jit(solution)/shard_map/ppermute | solution.py:436
  45.3 4.3 %collective-permute-done.10 = f32[1032,128]{1,0:T(8,128)S(1)} collective-permute-done((f32[1032,128]{1,0:T(8,128)S(1)}, f32[1032,128]{1,0:T(8,128)S(1)}, u32[]{:S(2)}, u32[]{:S(2)}) %collective-permute-start.10) | collective-permute-done | bytes 528416 | tf_op jit(solution)/shard_map/ppermute | solution.py:436
  49.6 0.1 add.61
  49.8 1.0 %collective-permute-start.13 = (f32[258,128]{1,0:T(8,128)S(1)}, f32[258,128]{1,0:T(8,128)S(1)}, u32[]{:S(2)}, u32[]{:S(2)}) collective-permute-start(f32[258,128]{1,0:T(8,128)S(1)} %pad_maximum_fusion.5), channel_id=1, source_target_pairs={{0,4},{1,5},{2,6},{3,7},{4,0},{5,1},{6,2},{7,3},{8,12},{9,13},{10,... | collective-permute-start | bytes 396296 | tf_op jit(solution)/shard_map/ppermute | solution.py:436
  50.9 4.7 %collective-permute-start.8 = (f32[258,128]{1,0:T(8,128)S(1)}, f32[258,128]{1,0:T(8,128)S(1)}, u32[]{:S(2)}, u32[]{:S(2)}) collective-permute-start(f32[258,128]{1,0:T(8,128)S(1)} %pad_maximum_fusion.2), channel_id=1, source_target_pairs={{0,16},{1,17},{2,18},{3,19},{4,20},{5,21},{6,22},{7,23},{8,24},{9,... | collective-permute-start | bytes 396296 | tf_op jit(solution)/shard_map/ppermute | solution.py:436
  55.6 0.4 collective-permute-start.11
  56.0 0.0 collective-permute-done.13
  56.0 5.4 %collective-permute-done.11 = f32[258,128]{1,0:T(8,128)S(1)} collective-permute-done((f32[258,128]{1,0:T(8,128)S(1)}, f32[258,128]{1,0:T(8,128)S(1)}, u32[]{:S(2)}, u32[]{:S(2)}) %collective-permute-start.11) | collective-permute-done | bytes 132128 | tf_op jit(solution)/shard_map/ppermute | solution.py:436
  61.5 0.4 collective-permute-start.14
  61.9 0.5 collective-permute-start.12
  62.5 3.4 %collective-permute-done.14 = f32[129,128]{1,0:T(8,128)S(1)} collective-permute-done((f32[129,128]{1,0:T(8,128)S(1)}, f32[129,128]{1,0:T(8,128)S(1)}, u32[]{:S(2)}, u32[]{:S(2)}) %collective-permute-start.14) | collective-permute-done | bytes 66080 | tf_op jit(solution)/shard_map/ppermute | solution.py:436
  65.9 0.3 collective-permute-done.12
  66.3 0.0 collective-permute-done.9.refs_1_
  66.3 0.0 collective-permute-done.8.refs_0_
  66.3 0.9 %shard_map.86 = (f32[256,128]{1,0:T(8,128)}, f32[2,128]{1,0:T(2,128)}) custom-call(f32[258,128]{1,0:T(8,128)S(1)} %collective-permute-done.8.refs_0_, f32[258,128]{1,0:T(8,128)S(1)} %collective-permute-done.9.refs_1_, f32[258,128]{1,0:T(8,128)S(1)} %pad_maximum_fusion.6.refs_2_), custom_call_target="tpu_custom_call" | custom-call | tf_op jit(solution)/shard_map/pallas_call | solution.py:335
  (37 shorter events, 0.4 us)
Async XLA Ops:
  1.6 7.4 %collective-permute-start = (f32[136,128]{1,0:T(8,128)S(1)}, f32[136,128]{1,0:T(8,128)S(1)}, u32[]{:S(2)}, u32[]{:S(2)}) collective-permute-start(f32[136,128]{1,0:T(8,128)S(1)} %get-tuple-element.26), channel_id=1, source_target_pairs={{0,8},{1,9},{2,10},{3,11},{4,12},{5,13},{6,14},{7,15},{8,0},{9,1},... | collective-permute-start | bytes 208904 | tf_op jit(solution)/shard_map/ppermute | solution.py:371
  4.7 7.5 %collective-permute-start.1 = (f32[136,128]{1,0:T(8,128)S(1)}, f32[136,128]{1,0:T(8,128)S(1)}, u32[]{:S(2)}, u32[]{:S(2)}) collective-permute-start(f32[136,128]{1,0:T(8,128)S(1)} %get-tuple-element.27), channel_id=1, source_target_pairs={{0,16},{1,17},{2,18},{3,19},{4,20},{5,21},{6,22},{7,23},{8,24},{9,... | collective-permute-start | bytes 208904 | tf_op jit(solution)/shard_map/ppermute | solution.py:371
  7.3 6.2 %collective-permute-start.2 = (f32[136,128]{1,0:T(8,128)S(1)}, f32[136,128]{1,0:T(8,128)S(1)}, u32[]{:S(2)}, u32[]{:S(2)}) collective-permute-start(f32[136,128]{1,0:T(8,128)S(1)} %get-tuple-element.28), channel_id=1, source_target_pairs={{0,24},{1,25},{2,26},{3,27},{4,28},{5,29},{6,30},{7,31},{8,16},{9,... | collective-permute-start | bytes 208904 | tf_op jit(solution)/shard_map/ppermute | solution.py:371
  19.2 4.3 %collective-permute-start.3 = (f32[4168,128]{1,0:T(8,128)S(1)}, f32[4168,128]{1,0:T(8,128)S(1)}, u32[]{:S(2)}, u32[]{:S(2)}) collective-permute-start(f32[4168,128]{1,0:T(8,128)S(1)} %get-tuple-element.29), channel_id=1, source_target_pairs={{0,1},{1,0},{2,3},{3,2},{4,5},{5,4},{6,7},{7,6},{8,9},{9,8},{10,11... | collective-permute-start | bytes 6402056 | tf_op jit(solution)/shard_map/ppermute | solution.py:407
  24.6 8.8 %collective-permute-start.6 = (f32[516,128]{1,0:T(8,128)S(1)}, f32[516,128]{1,0:T(8,128)S(1)}, u32[]{:S(2)}, u32[]{:S(2)}) collective-permute-start(f32[516,128]{1,0:T(8,128)S(1)} %get-tuple-element.40), channel_id=1, source_target_pairs={{0,4},{1,5},{2,6},{3,7},{4,0},{5,1},{6,2},{7,3},{8,12},{9,13},{10,... | collective-permute-start | bytes 792584 | tf_op jit(solution)/shard_map/ppermute | solution.py:436
  26.2 8.6 %collective-permute-start.4 = (f32[516,128]{1,0:T(8,128)S(1)}, f32[516,128]{1,0:T(8,128)S(1)}, u32[]{:S(2)}, u32[]{:S(2)}) collective-permute-start(f32[516,128]{1,0:T(8,128)S(1)} %get-tuple-element.38), channel_id=1, source_target_pairs={{0,2},{1,3},{2,0},{3,1},{4,6},{5,7},{6,4},{7,5},{8,10},{9,11},{10,... | collective-permute-start | bytes 792584 | tf_op jit(solution)/shard_map/ppermute | solution.py:436
  34.9 5.1 %collective-permute-start.5 = (f32[258,128]{1,0:T(8,128)S(1)}, f32[258,128]{1,0:T(8,128)S(1)}, u32[]{:S(2)}, u32[]{:S(2)}) collective-permute-start(f32[258,128]{1,0:T(8,128)S(1)} %get-tuple-element.56), channel_id=1, source_target_pairs={{0,4},{1,5},{2,6},{3,7},{4,0},{5,1},{6,2},{7,3},{8,12},{9,13},{10,... | collective-permute-start | bytes 396296 | tf_op jit(solution)/shard_map/ppermute | solution.py:436
  35.9 13.8 %collective-permute-start.10 = (f32[1032,128]{1,0:T(8,128)S(1)}, f32[1032,128]{1,0:T(8,128)S(1)}, u32[]{:S(2)}, u32[]{:S(2)}) collective-permute-start(f32[1032,128]{1,0:T(8,128)S(1)} %shard_map.82), channel_id=1, source_target_pairs={{0,8},{1,9},{2,10},{3,11},{4,12},{5,13},{6,14},{7,15},{8,0},{9,1},... | collective-permute-start | bytes 1585160 | tf_op jit(solution)/shard_map/ppermute | solution.py:436
  36.2 5.3 %collective-permute-start.7 = (f32[258,128]{1,0:T(8,128)S(1)}, f32[258,128]{1,0:T(8,128)S(1)}, u32[]{:S(2)}, u32[]{:S(2)}) collective-permute-start(f32[258,128]{1,0:T(8,128)S(1)} %get-tuple-element.57), channel_id=1, source_target_pairs={{0,2},{1,3},{2,0},{3,1},{4,6},{5,7},{6,4},{7,5},{8,10},{9,11},{10,... | collective-permute-start | bytes 396296 | tf_op jit(solution)/shard_map/ppermute | solution.py:436
  41.6 24.6 %collective-permute-start.9 = (f32[258,128]{1,0:T(8,128)S(1)}, f32[258,128]{1,0:T(8,128)S(1)}, u32[]{:S(2)}, u32[]{:S(2)}) collective-permute-start(f32[258,128]{1,0:T(8,128)S(1)} %pad_maximum_fusion.3), channel_id=1, source_target_pairs={{0,24},{1,25},{2,26},{3,27},{4,28},{5,29},{6,30},{7,31},{8,16},{9,... | collective-permute-start | bytes 396296 | tf_op jit(solution)/shard_map/ppermute | solution.py:436
  49.8 6.2 %collective-permute-start.13 = (f32[258,128]{1,0:T(8,128)S(1)}, f32[258,128]{1,0:T(8,128)S(1)}, u32[]{:S(2)}, u32[]{:S(2)}) collective-permute-start(f32[258,128]{1,0:T(8,128)S(1)} %pad_maximum_fusion.5), channel_id=1, source_target_pairs={{0,4},{1,5},{2,6},{3,7},{4,0},{5,1},{6,2},{7,3},{8,12},{9,13},{10,... | collective-permute-start | bytes 396296 | tf_op jit(solution)/shard_map/ppermute | solution.py:436
  50.9 15.4 %collective-permute-start.8 = (f32[258,128]{1,0:T(8,128)S(1)}, f32[258,128]{1,0:T(8,128)S(1)}, u32[]{:S(2)}, u32[]{:S(2)}) collective-permute-start(f32[258,128]{1,0:T(8,128)S(1)} %pad_maximum_fusion.2), channel_id=1, source_target_pairs={{0,16},{1,17},{2,18},{3,19},{4,20},{5,21},{6,22},{7,23},{8,24},{9,... | collective-permute-start | bytes 396296 | tf_op jit(solution)/shard_map/ppermute | solution.py:436
  55.6 5.8 %collective-permute-start.11 = (f32[258,128]{1,0:T(8,128)S(1)}, f32[258,128]{1,0:T(8,128)S(1)}, u32[]{:S(2)}, u32[]{:S(2)}) collective-permute-start(f32[258,128]{1,0:T(8,128)S(1)} %pad_maximum_fusion.4), channel_id=1, source_target_pairs={{0,2},{1,3},{2,0},{3,1},{4,6},{5,7},{6,4},{7,5},{8,10},{9,11},{10,... | collective-permute-start | bytes 396296 | tf_op jit(solution)/shard_map/ppermute | solution.py:436
  61.5 4.4 %collective-permute-start.14 = (f32[129,128]{1,0:T(8,128)S(1)}, f32[129,128]{1,0:T(8,128)S(1)}, u32[]{:S(2)}, u32[]{:S(2)}) collective-permute-start(f32[129,128]{1,0:T(8,128)S(1)} %pad_maximum_fusion.9), channel_id=1, source_target_pairs={{0,2},{1,3},{2,0},{3,1},{4,6},{5,7},{6,4},{7,5},{8,10},{9,11},{10,... | collective-permute-start | bytes 198152 | tf_op jit(solution)/shard_map/ppermute | solution.py:436
  61.9 4.3 %collective-permute-start.12 = (f32[129,128]{1,0:T(8,128)S(1)}, f32[129,128]{1,0:T(8,128)S(1)}, u32[]{:S(2)}, u32[]{:S(2)}) collective-permute-start(f32[129,128]{1,0:T(8,128)S(1)} %pad_maximum_fusion.8), channel_id=1, source_target_pairs={{0,4},{1,5},{2,6},{3,7},{4,0},{5,1},{6,2},{7,3},{8,12},{9,13},{10,... | collective-permute-start | bytes 198152 | tf_op jit(solution)/shard_map/ppermute | solution.py:436
